TPU v7x, 32 devices: a whole 2x2x4 slice. The times are simulated.
32 devices in a mesh: frames: 2 (over x), lenslet: 16 (over z, y, core).
Axes of the slice: x: 2, y: 2, z: 4, core: 2. Of those that a mesh axis runs over, the one named last changes fastest.
Arguments:
- volume: bfloat16 [8, 256, 64, 400], P('frames', 'lenslet'), parts along dimension 0, may hold values from 0.099609375 to 1
- measured: float32 [512, 64, 400], P(('frames', 'lenslet')), parts along dimension 0, may hold values from 0.2 to 2
- operator_rows: bfloat16 [12800, 400], P('lenslet'), may hold values from 2.9831426e-10 to 0.0029907227
- offset_counts: int32 [4], replicated, may hold values from 1 to 25, 32 in all
- offset_table: int32 [32, 2], replicated, may hold values from -2 to 2
- dark_level: float32 [400], replicated, may hold values from 0.2 to 1
Outputs:
- predicted: float32 [512, 64, 400], P(('frames', 'lenslet')), parts along dimension 0
- ratio: float32 [512, 64, 400], P(('frames', 'lenslet')), parts along dimension 0
There are 2 independent parts, one for each index of `frames`. A program takes and returns all parts, laid end to end along the dimension named above; an argument that names none is the same for every part. Nothing has to cross between parts.
Inputs may be any that keep to these rules, and one draw needn't show every extreme that they name: `offset_counts`: counts sum to 32.
All inputs are finite; a program needn't handle non-finite values.
Results may differ from a plain program's by a relative error of at most 0.0003.
Values may be sent and summed in bfloat16 or wider, within the bound.
No kernel may reach another device: no remote copies, remote signals or barrier semaphores. Data moves between devices by JAX's collectives and lax.ppermute only.
A program may use at most 192 MiB of HBM per device.

v0:
```python
import jax
import jax.numpy as jnp
from jax import lax
from jax.sharding import PartitionSpec as P

REACH = 2


def passed_along(block, axis, distance):
    devices = range(lax.axis_size(axis))
    route = [(i - distance, i) for i in devices if i - distance in devices]
    return lax.ppermute(block, axis, route)


def gather_slabs(table, depth_of, row_start, col_shift, target_rows, columns, rows_ext, cols_ext):
    row_ids = jnp.arange(target_rows, dtype=jnp.int32)
    col_ids = jnp.arange(columns, dtype=jnp.int32)
    index = depth_of[None, None, :] * (rows_ext * cols_ext)
    index = index + (row_ids[:, None, None] + row_start[None, None, :]) * cols_ext
    index = index + col_ids[None, :, None] + col_shift[None, None, :] + REACH
    pixels = table.shape[1]
    taken = jnp.take(table, index.reshape(-1), axis=0)
    return taken.reshape(target_rows * columns, depth_of.shape[0] * pixels)


def body(volume, measured, operator_rows, offset_counts, offset_table, dark_level):
    depths, rows_here, columns, pixels = volume.shape
    op_total = offset_table.shape[0]
    ends = jnp.cumsum(offset_counts)
    positions = jnp.arange(op_total, dtype=jnp.int32)
    depth_of = jnp.sum((positions[:, None] >= ends[None, :]).astype(jnp.int32), axis=1)
    row_shift = offset_table[:, 0]
    col_shift = offset_table[:, 1]
    cols_ext = columns + 2 * REACH
    above = passed_along(volume[:, rows_here - REACH :], "lenslet", 1)
    below = passed_along(volume[:, :REACH], "lenslet", -1)
    extended = jnp.concatenate([above, volume, below], axis=1)
    extended = jnp.pad(extended, ((0, 0), (0, 0), (REACH, REACH), (0, 0)))
    rows_ext = rows_here + 2 * REACH
    table = extended.reshape(depths * rows_ext * cols_ext, pixels)
    stacked = gather_slabs(
        table, depth_of, row_shift + REACH, col_shift, rows_here, columns, rows_ext, cols_ext
    )
    summed = jnp.dot(
        stacked,
        lax.all_gather(operator_rows, "lenslet", axis=0, tiled=True),
        preferred_element_type=jnp.float32,
    )
    predicted = summed.reshape(rows_here, columns, pixels)
    ratio = measured / (predicted + dark_level)
    return (predicted, ratio)


def solution(mesh):
    placed = (
        P("frames", "lenslet", None, None),
        P(("frames", "lenslet"), None, None),
        P("lenslet", None),
        P(),
        P(),
        P(),
    )
    return jax.shard_map(
        body,
        mesh=mesh,
        in_specs=placed,
        out_specs=(P(("frames", "lenslet"), None, None), P(("frames", "lenslet"), None, None)),
        check_vma=False,
    )
```

profile of v0, /device:TPU:0, one launch (start us, length us, event | category | flops | bytes accessed | tf_op | source)
XLA Modules:
  0.0 346.5 jit_solution(12887176921181222401)
XLA Ops:
  7.2 0.0 all-gather.3.cloned.1.call-start
  7.2 0.7 all-gather.3.cloned.1.call-update
  7.9 2.1 fusion.10
  10.0 2.4 collective-permute-start
  12.4 1.3 collective-permute-start.1
  13.7 0.8 reduce-window.8
  14.5 0.1 convert_reduce_fusion
  14.6 0.8 slice_bitcast_fusion
  15.4 0.2 add_add_fusion.1
  15.6 0.3 add.184
  15.8 0.3 add.187
  16.1 0.2 compare_select_fusion.1
  16.3 0.2 compare_and_fusion
  16.5 6.8 %broadcast_in_dim.12 = pred[1024,32,400]{2,1,0:T(32,128)(4,1)} broadcast(pred[1024,32]{1,0:T(8,128)(4,1)S(1)} %compare_and_fusion), dimensions={0,1} | broadcast | bytes 13139968 | tf_op jit(solution)/shard_map/jit(_take)/broadcast_in_dim | solution.py:22
  23.2 53.5 %broadcast_in_dim.20 = pred[16,64,12800]{2,1,0:T(32,128)(4,1)} reshape(pred[1024,32,400]{2,1,0:T(32,128)(4,1)} %broadcast_in_dim.12) | data formatting | bytes 26214400 | tf_op jit(solution)/shard_map/jit(_take)/broadcast_in_dim | solution.py:22
  76.8 0.0 collective-permute-done
  76.8 0.0 collective-permute-done.1
  76.8 8.0 %fusion.8 = bf16[4,20,68,400]{3,2,1,0:T(8,128)(2,1)} fusion(bf16[4,2,64,400]{3,2,1,0:T(8,128)(2,1)S(1)} %collective-permute-done.1, bf16[4,16,64,400]{3,2,1,0:T(8,128)(2,1)} %param.6, bf16[4,2,64,400]{3,2,1,0:T(8,128)(2,1)S(1)} %collective-permute-done), kind=kLoop, calls=%fused_computation.11 | loop fusion | flops 26112000 | bytes 8448000 | tf_op jit(solution)/shard_map/concatenate | solution.py:37
  84.7 9.1 %reshape.157 = bf16[5440,400]{1,0:T(8,128)(2,1)} reshape(bf16[4,20,68,400]{3,2,1,0:T(8,128)(2,1)} %fusion.8) | data formatting | bytes 8704000 | tf_op jit(solution)/shard_map/reshape | solution.py:40
  93.8 135.4 %gather_fusion = bf16[32768,400]{1,0:T(8,128)(2,1)} fusion(bf16[5440,400]{1,0:T(8,128)(2,1)} %reshape.157, s32[32768]{0:T(1024)S(1)} %broadcast_clamp_fusion), kind=kCustom, calls=%fused_computation | custom fusion | bytes 52559872 | tf_op jit(solution)/shard_map/jit(_take)/gather | solution.py:22
  229.3 52.4 %gather.7 = bf16[16,64,12800]{2,1,0:T(8,128)(2,1)} reshape(bf16[32768,400]{1,0:T(8,128)(2,1)} %gather_fusion) | data formatting | bytes 52428800 | tf_op jit(solution)/shard_map/jit(_take)/gather | solution.py:22
  281.7 0.0 all-gather.3.cloned.1.call-done
  281.7 16.2 %copy.11 = bf16[16,800,400]{1,0,2:T(8,128)(2,1)} copy(bf16[16,800,400]{1,2,0:T(8,128)(2,1)} %all-gather.3.cloned.1.call-done) | data formatting | bytes 20480000 | tf_op jit(solution)/shard_map/all_gather | solution.py:46
  297.9 0.0 copy-start
  297.9 0.0 copy-start.1
  297.9 18.7 %reshape.168 = bf16[12800,400,1]{0,1,2:T(8,128)(2,1)} reshape(bf16[16,800,400]{1,0,2:T(8,128)(2,1)} %copy.11) | data formatting | bytes 20480000
  316.6 0.0 copy-done
  316.6 0.0 copy-done.1
  316.6 23.0 %add_divide_fusion = (f32[16,64,400]{2,1,0:T(8,128)}, f32[16,64,400]{2,1,0:T(8,128)}) fusion(f32[16,64,400]{2,1,0:T(8,128)S(1)} %copy-done, f32[400]{0:T(512)S(1)} %copy-done.1, bf16[12800,400,1]{0,1,2:T(8,128)(2,1)} %reshape.168, pred[16,64,12800]{2,1,0:T(32,128)(4,1)} %broadcast_in_dim.20, bf16[16,64,12800]{2,1,0:T(8,128)(2,1)} %gather.7), kind=kOutput, calls=%fused_computation.12 | convolution fusion | flops 10499686400 | bytes 54478400 | tf_op jit(solution)/shard_map/dot_general | solution.py:44
  (3 shorter events, 0.0 us)
Async XLA Ops:
  7.2 274.5 %all-gather.3.cloned.1.call-start = ((), (), s32[]{:S(2)}) async-start(), calls=%async_computation | async-start | bytes 12185600 | tf_op jit(solution)/shard_map/all_gather | solution.py:46
  10.0 66.8 %collective-permute-start = (bf16[4,2,64,400]{3,2,1,0:T(8,128)(2,1)}, bf16[4,2,64,400]{3,2,1,0:T(8,128)(2,1)S(1)}, u32[]{:S(2)}, u32[]{:S(2)}) collective-permute-start(bf16[4,2,64,400]{3,2,1,0:T(8,128)(2,1)} %get-tuple-element.2), channel_id=1, source_target_pairs={{0,1},{1,2},{2,3},{3,4},{4,5},{5,6},{6,7},{7,8},{8,9},{9,10},{10,1... | collective-permute-start | bytes 1228808 | tf_op jit(solution)/shard_map/ppermute | solution.py:12
  12.4 64.4 %collective-permute-start.1 = (bf16[4,2,64,400]{3,2,1,0:T(8,128)(2,1)S(1)}, bf16[4,2,64,400]{3,2,1,0:T(8,128)(2,1)S(1)}, u32[]{:S(2)}, u32[]{:S(2)}) collective-permute-start(bf16[4,2,64,400]{3,2,1,0:T(8,128)(2,1)S(1)} %get-tuple-element.3), channel_id=1, source_target_pairs={{1,0},{2,1},{3,2},{4,3},{5,4},{6,5},{7,6},{8,7},{9,8},{10,9},{11,1... | collective-permute-start | bytes 1228808 | tf_op jit(solution)/shard_map/ppermute | solution.py:12
  297.9 18.7 %copy-start = (f32[16,64,400]{2,1,0:T(8,128)S(1)}, f32[16,64,400]{2,1,0:T(8,128)}, u32[]{:S(2)}) copy-start(f32[16,64,400]{2,1,0:T(8,128)} %param.7) | copy-start | bytes 4915204
  297.9 18.7 %copy-start.1 = (f32[400]{0:T(512)S(1)}, f32[400]{0:T(512)}, u32[]{:S(2)}) copy-start(f32[400]{0:T(512)} %param.11) | copy-start | bytes 4804
Sparse Core Ops, SparseCore 0:
  10.2 98.4 all-gather.2
where the time goes:
time: 352 us; the launch traced here: 347 us
  local copies, waits for them, and re-layouts  295 us (84%)
  matrix products  23 us (7%)
  between operations  14.1 us (4%)
  other arithmetic  10.2 us (3%)
  starting transfers between devices  3.71 us (1%)
    gather x2, local copies, waits for them, and re-layouts, gather_slabs(): taken = jnp.take(table, index.reshape(-1), axis=0)  188 us
    broadcast_in_dim x2, local copies, waits for them, and re-layouts, gather_slabs(): taken = jnp.take(table, index.reshape(-1), axis=0)  60.3 us
    dot_general x1, matrix products, body(): jnp.dot(stacked, lax.all_gather(operator_rows, 'lenslet', axis=0, tiled=T...  23 us
    unnamed x5, local copies, waits for them, and re-layouts  18.7 us
    all_gather x1, local copies, waits for them, and re-layouts, body(): lax.all_gather(operator_rows, 'lenslet', axis=0, tiled=True)  16.2 us
    reshape x1, local copies, waits for them, and re-layouts, body(): table = extended.reshape(depths * rows_ext * cols_ext, pixels)  9.11 us
    concatenate x1, other arithmetic, body(): extended = jnp.concatenate([above, volume, below], axis=1)  7.97 us
  transfers between devices with their start and end apart: 3, of which 0 were waited for; matrix products, arithmetic and copies ran while one was open for 78% of the time, Pallas kernels for 0%

commit v1 on v0

v1 whole, which is shorter than its diff:
```python
import jax
import jax.numpy as jnp
from jax import lax
from jax.experimental import pallas as pl
from jax.experimental.pallas import tpu as pltpu
from jax.sharding import PartitionSpec as P

REACH = 2
SHIFTS = 2 * REACH + 1
VMEM = 60 * 1024 * 1024


def passed_along(block, axis, distance):
    devices = range(lax.axis_size(axis))
    route = [(i - distance, i) for i in devices if i - distance in devices]
    return lax.ppermute(block, axis, route)


def shift_kernel(own_ref, above_ref, below_ref, out_ref):
    rows, columns, pixels = own_ref.shape[1:]
    col = lax.broadcasted_iota(jnp.int32, (columns, pixels), 0)

    def put(row, plane):
        wide = plane.astype(jnp.float32)
        for s in range(SHIFTS):
            step = s - REACH
            if step == 0:
                moved = wide
            else:
                moved = pltpu.roll(wide, (-step) % columns, 0)
                inside = col < columns - step if step > 0 else col >= -step
                moved = jnp.where(inside, moved, 0.0)
            out_ref[s, 0, row] = moved.astype(jnp.bfloat16)

    for r in range(REACH):
        put(r, above_ref[0, r])
        put(rows + REACH + r, below_ref[0, r])

    def step(r, carry):
        put(r + REACH, own_ref[0, r])
        return carry

    lax.fori_loop(0, rows, step, 0)


def shifted_copies(volume, above, below):
    depths, rows, columns, pixels = volume.shape
    ext = rows + 2 * REACH
    return pl.pallas_call(
        shift_kernel,
        grid=(depths,),
        in_specs=[
            pl.BlockSpec((1, rows, columns, pixels), lambda d: (d, 0, 0, 0)),
            pl.BlockSpec((1, REACH, columns, pixels), lambda d: (d, 0, 0, 0)),
            pl.BlockSpec((1, REACH, columns, pixels), lambda d: (d, 0, 0, 0)),
        ],
        out_specs=pl.BlockSpec((SHIFTS, 1, ext, columns, pixels), lambda d: (0, d, 0, 0, 0)),
        out_shape=jax.ShapeDtypeStruct((SHIFTS, depths, ext, columns, pixels), jnp.bfloat16),
        compiler_params=pltpu.CompilerParams(vmem_limit_bytes=VMEM),
        name="shifted_copies",
    )(volume, above, below)


def project_kernel(place_ref, start_ref, w_ref, even_ref, odd_ref, meas_ref, dark_ref, pred_ref, ratio_ref):
    i = pl.program_id(0)
    rows, columns, pixels = pred_ref.shape
    dims = (((1,), (1,)), ((), ()))
    a = even_ref[0].reshape(rows * columns, pixels)
    b = odd_ref[0].reshape(rows * columns, pixels)
    w = w_ref[0]
    part = lax.dot_general(a, w[:, :pixels], dims, preferred_element_type=jnp.float32)
    part = part + lax.dot_general(b, w[:, pixels:], dims, preferred_element_type=jnp.float32)
    part = part.reshape(rows, columns, pixels)

    @pl.when(i == 0)
    def _():
        pred_ref[...] = part

    @pl.when(i > 0)
    def _():
        pred_ref[...] = pred_ref[...] + part

    @pl.when(i == pl.num_programs(0) - 1)
    def _():
        ratio_ref[...] = meas_ref[...] / (pred_ref[...] + dark_ref[...])


def project(copies, weights, place, start, measured, dark_level):
    rows, columns, pixels = measured.shape
    shards, _, pair = weights.shape
    whole = lambda i, *_: (0, 0, 0)

    def slab(which):
        return pl.BlockSpec(
            (pl.Element(1), pl.Element(rows), pl.Element(columns), pl.Element(pixels)),
            lambda i, place_ref, start_ref: (place_ref[2 * i + which], start_ref[2 * i + which], 0, 0),
        )

    grid_spec = pltpu.PrefetchScalarGridSpec(
        num_scalar_prefetch=2,
        grid=(shards,),
        in_specs=[
            pl.BlockSpec((1, pixels, pair), lambda i, *_: (i, 0, 0)),
            slab(0),
            slab(1),
            pl.BlockSpec((rows, columns, pixels), whole),
            pl.BlockSpec((1, 1, pixels), whole),
        ],
        out_specs=[pl.BlockSpec((rows, columns, pixels), whole)] * 2,
    )
    return pl.pallas_call(
        project_kernel,
        grid_spec=grid_spec,
        out_shape=[jax.ShapeDtypeStruct(measured.shape, jnp.float32)] * 2,
        compiler_params=pltpu.CompilerParams(vmem_limit_bytes=VMEM),
        name="project",
    )(place, start, weights, copies, copies, measured, dark_level.reshape(1, 1, pixels))


def gathered_pairs(operator_rows):
    held, pixels = operator_rows.shape
    if held == 2 * pixels:
        return lax.all_gather(operator_rows.T, "lenslet", axis=0)
    every = lax.all_gather(operator_rows, "lenslet", axis=0, tiled=True)
    return every.reshape(-1, 2 * pixels, pixels).transpose(0, 2, 1)


def body(volume, measured, operator_rows, offset_counts, offset_table, dark_level):
    depths, rows, columns, pixels = volume.shape
    op_total = offset_table.shape[0]
    planes = jnp.arange(depths, dtype=jnp.int32)
    ends = jnp.sum(jnp.where(planes[None, :] <= planes[:, None], offset_counts[None, :], 0), axis=1)
    positions = jnp.arange(op_total, dtype=jnp.int32)
    depth_of = jnp.sum((positions[:, None] >= ends[None, :]).astype(jnp.int32), axis=1)
    place = (offset_table[:, 1] + REACH) * depths + depth_of
    start = offset_table[:, 0] + REACH

    weights = gathered_pairs(operator_rows)
    above = passed_along(volume[:, rows - REACH :], "lenslet", 1)
    below = passed_along(volume[:, :REACH], "lenslet", -1)
    copies = shifted_copies(volume, above, below)
    copies = copies.reshape(SHIFTS * depths, rows + 2 * REACH, columns, pixels)
    return tuple(project(copies, weights, place, start, measured, dark_level))


def solution(mesh):
    placed = (
        P("frames", "lenslet", None, None),
        P(("frames", "lenslet"), None, None),
        P("lenslet", None),
        P(),
        P(),
        P(),
    )
    return jax.shard_map(
        body,
        mesh=mesh,
        in_specs=placed,
        out_specs=(P(("frames", "lenslet"), None, None), P(("frames", "lenslet"), None, None)),
        check_vma=False,
    )
```

time: 352 us -> 148 us (0.42); the launches traced: 347 us -> 147 us
  local copies, waits for them, and re-layouts: 295 us -> 2.87 us
  waiting for transfers between devices: 0.69 us -> 78.5 us
  Pallas kernels: 0 us -> 43.9 us
  matrix products: 23 us -> 0 us
  other arithmetic: 10.2 us -> 3.32 us
    gather x2 -> x0, local copies, waits for them, and re-layouts: 188 us -> none  [gather_slabs(): taken = jnp.take(table, index.reshape(-1), axis=0)]
    all_gather x1, waiting for transfers between devices: 0.01 us -> 77.8 us  [gathered_pairs(): return lax.all_gather(operator_rows.T, 'lenslet', axis=0)]
    broadcast_in_dim x2 -> x0, local copies, waits for them, and re-layouts: 60.3 us -> none  [gather_slabs(): taken = jnp.take(table, index.reshape(-1), axis=0)]
    pallas_call x0 -> x2, Pallas kernels: none -> 43.9 us  [the longest x1 32.3 us: project(): pl.pallas_call(project_kernel, grid_spec=grid_spec, out_shape=[jax.ShapeD...]
    dot_general x1 -> x0, matrix products: 23 us -> none  [body(): jnp.dot(stacked, lax.all_gather(operator_rows, 'lenslet', axis=0, tiled=T...]
    unnamed x5 -> x4, local copies, waits for them, and re-layouts: 18.7 us -> 1.58 us
    all_gather x1 -> x0, local copies, waits for them, and re-layouts: 16.2 us -> none  [body(): lax.all_gather(operator_rows, 'lenslet', axis=0, tiled=True)]
    reshape x1 -> x0, local copies, waits for them, and re-layouts: 9.11 us -> none  [body(): table = extended.reshape(depths * rows_ext * cols_ext, pixels)]
  transfers between devices with their start and end apart: 3 -> 3, of which waited for: 0 -> 1; matrix products, arithmetic and copies ran while one was open for 78% -> 3% of each run, Pallas kernels for 0% -> 8%
where the time goes in v1:
time: 148 us; the launch traced here: 147 us
  waiting for transfers between devices  78.5 us (53%)
  Pallas kernels  43.9 us (30%)
  between operations  14.1 us (10%)
  starting transfers between devices  4.39 us (3%)
  other arithmetic  3.32 us (2%)
  local copies, waits for them, and re-layouts  2.87 us (2%)
    all_gather x1, waiting for transfers between devices, gathered_pairs(): return lax.all_gather(operator_rows.T, 'lenslet', axis=0)  77.8 us
    pallas_call x1, Pallas kernels, project(): pl.pallas_call(project_kernel, grid_spec=grid_spec, out_shape=[jax.ShapeD...  32.3 us
    pallas_call x1, Pallas kernels, shifted_copies(): pl.pallas_call(shift_kernel, grid=(depths,), in_specs=[pl.BlockSpec((1, r...  11.6 us
    ppermute x2, starting transfers between devices, passed_along(): return lax.ppermute(block, axis, route)  4.36 us
  transfers between devices with their start and end apart: 3, of which 1 were waited for; matrix products, arithmetic and copies ran while one was open for 3% of the time, Pallas kernels for 8%

profile of v1, /device:TPU:0, one launch (start us, length us, event | category | flops | bytes accessed | tf_op | source)
XLA Modules:
  0.0 147.0 jit_solution(3875155800756385773)
XLA Ops:
  7.2 0.0 all-gather.3.cloned.1.call-start
  7.2 0.7 all-gather.3.cloned.1.call-update
  7.9 1.3 fusion
  9.2 1.3 collective-permute-start.1
  10.5 3.1 %collective-permute-start = (bf16[4,2,64,400]{3,2,1,0:T(8,128)(2,1)S(1)}, bf16[4,2,64,400]{3,2,1,0:T(8,128)(2,1)S(1)}, u32[]{:S(2)}, u32[]{:S(2)}) collective-permute-start(bf16[4,2,64,400]{3,2,1,0:T(8,128)(2,1)S(1)} %get-tuple-element.3), channel_id=1, source_target_pairs={{0,1},{1,2},{2,3},{3,4},{4,5},{5,6},{6,7},{7,8},{8,9},{9,10},{10,1... | collective-permute-start | bytes 1228808 | tf_op jit(solution)/shard_map/ppermute | solution.py:16
  13.6 0.8 select_reduce_fusion
  14.3 0.1 convert_reduce_fusion
  14.4 1.2 add_bitcast_fusion.start_ref
  15.6 1.3 bitcast_add_fusion.place_ref
  16.9 0.0 collective-permute-done.1.below_ref
  16.9 0.0 copy-start
  16.9 0.0 collective-permute-done.above_ref
  16.9 0.8 copy-done
  17.7 0.0 copy-start.1
  17.7 0.8 copy-done.1
  18.5 11.6 %shifted_copies.1 = bf16[5,4,20,64,400]{4,3,2,1,0:T(8,128)(2,1)} custom-call(bf16[4,16,64,400]{3,2,1,0:T(8,128)(2,1)} %own_ref.1, bf16[4,2,64,400]{3,2,1,0:T(8,128)(2,1)} %copy-done.1, bf16[4,2,64,400]{3,2,1,0:T(8,128)(2,1)} %copy-done), custom_call_target="tpu_custom_call" | custom-call | tf_op jit(solution)/shard_map/shifted_copies/pallas_call | solution.py:49
  30.0 77.8 %all-gather.3.cloned.1.call-done = bf16[6400,800]{1,0:T(8,128)(2,1)} async-done(((bf16[400,800]{1,0:T(8,128)(2,1)}), bf16[6400,800]{1,0:T(8,128)(2,1)}) %all-gather.3.cloned.1.call-update) | async-done | bytes 10240016 | tf_op jit(solution)/shard_map/all_gather | solution.py:123
  107.9 32.3 %project.1 = (f32[16,64,400]{2,1,0:T(8,128)}, f32[16,64,400]{2,1,0:T(8,128)}) custom-call(s32[32]{0:T(128)} %bitcast_add_fusion.place_ref, s32[32]{0:T(128)} %add_bitcast_fusion.start_ref, bf16[16,400,800]{2,1,0:T(8,128)(2,1)} %bitcast.10, bf16[20,20,64,400]{3,2,1,0:T(8,128)(2,1)} %bitcast.8, bf16[20,20,64,400]{3,2,1,0:T(8,128)(2,1)} %bitcast.9, ...), custom_call_target="tpu_custom_call" | custom-call | tf_op jit(solution)/shard_map/project/pallas_call | solution.py:111
Async XLA Ops:
  7.2 100.7 %all-gather.3.cloned.1.call-start = ((), (), s32[]{:S(2)}) async-start(), calls=%async_computation | async-start | bytes 12185600 | tf_op jit(solution)/shard_map/all_gather | solution.py:123
  9.2 7.7 %collective-permute-start.1 = (bf16[4,2,64,400]{3,2,1,0:T(8,128)(2,1)S(1)}, bf16[4,2,64,400]{3,2,1,0:T(8,128)(2,1)S(1)}, u32[]{:S(2)}, u32[]{:S(2)}) collective-permute-start(bf16[4,2,64,400]{3,2,1,0:T(8,128)(2,1)S(1)} %get-tuple-element.2), channel_id=1, source_target_pairs={{1,0},{2,1},{3,2},{4,3},{5,4},{6,5},{7,6},{8,7},{9,8},{10,9},{11,1... | collective-permute-start | bytes 1228808 | tf_op jit(solution)/shard_map/ppermute | solution.py:16
  10.5 6.4 %collective-permute-start = (bf16[4,2,64,400]{3,2,1,0:T(8,128)(2,1)S(1)}, bf16[4,2,64,400]{3,2,1,0:T(8,128)(2,1)S(1)}, u32[]{:S(2)}, u32[]{:S(2)}) collective-permute-start(bf16[4,2,64,400]{3,2,1,0:T(8,128)(2,1)S(1)} %get-tuple-element.3), channel_id=1, source_target_pairs={{0,1},{1,2},{2,3},{3,4},{4,5},{5,6},{6,7},{7,8},{8,9},{9,10},{10,1... | collective-permute-start | bytes 1228808 | tf_op jit(solution)/shard_map/ppermute | solution.py:16
  16.9 0.8 copy-start
  17.7 0.8 copy-start.1
Sparse Core Ops, SparseCore 0:
  10.2 97.6 all-gather.2

commit v2 on v1

--- a/solution.py
+++ b/solution.py
@@ -1,3 +1,5 @@
+import functools
+
 import jax
 import jax.numpy as jnp
 from jax import lax
@@ -8,6 +10,8 @@
 REACH = 2
 SHIFTS = 2 * REACH + 1
 VMEM = 60 * 1024 * 1024
+SMALL = 12 * 1024 * 1024
+TILE = 8
 
 
 def passed_along(block, axis, distance):
@@ -93,7 +97,12 @@
     def slab(which):
         return pl.BlockSpec(
             (pl.Element(1), pl.Element(rows), pl.Element(columns), pl.Element(pixels)),
-            lambda i, place_ref, start_ref: (place_ref[2 * i + which], start_ref[2 * i + which], 0, 0),
+            lambda i, place_ref, start_ref: (
+                place_ref[jnp.minimum(2 * i + which, 2 * shards - 1)],
+                start_ref[jnp.minimum(2 * i + which, 2 * shards - 1)],
+                0,
+                0,
+            ),
         )
 
     grid_spec = pltpu.PrefetchScalarGridSpec(
@@ -125,22 +134,249 @@
     return every.reshape(-1, 2 * pixels, pixels).transpose(0, 2, 1)
 
 
-def body(volume, measured, operator_rows, offset_counts, offset_table, dark_level):
+IN_VMEM = pl.BlockSpec(memory_space=pltpu.VMEM)
+IN_SMEM = pl.BlockSpec(memory_space=pltpu.SMEM)
+IN_HBM = pl.BlockSpec(memory_space=pl.ANY)
+
+
+def put_shifted(out_ref, depth, row, plane):
+    columns, pixels = plane.shape
+    wide = plane.astype(jnp.float32)
+    col = lax.broadcasted_iota(jnp.int32, (columns, pixels), 0)
+    depths = out_ref.shape[0] // SHIFTS
+    for s in range(SHIFTS):
+        step = s - REACH
+        if step == 0:
+            out_ref[s * depths + depth, row] = plane
+            continue
+        moved = pltpu.roll(wide, (-step) % columns, 0)
+        inside = col < columns - step if step > 0 else col >= -step
+        out_ref[s * depths + depth, row] = jnp.where(inside, moved, 0.0).astype(jnp.bfloat16)
+
+
+def own_rows_kernel(volume_ref, out_ref):
+    depths, rows, _, _ = volume_ref.shape
+
+    def step(n, carry):
+        d, r = n // rows, n % rows
+        put_shifted(out_ref, d, r + REACH, volume_ref[d, r])
+        return carry
+
+    lax.fori_loop(0, depths * rows, step, 0)
+
+
+def edge_rows_kernel(above_ref, below_ref, old_ref, out_ref):
+    depths, reach, _, _ = above_ref.shape
+    rows = out_ref.shape[1] - 2 * reach
+
+    def step(n, carry):
+        d, r = n // reach, n % reach
+        put_shifted(out_ref, d, r, above_ref[d, r])
+        put_shifted(out_ref, d, r + rows + reach, below_ref[d, r])
+        return carry
+
+    lax.fori_loop(0, depths * reach, step, 0)
+
+
+def own_rows(volume):
     depths, rows, columns, pixels = volume.shape
-    op_total = offset_table.shape[0]
+    return pl.pallas_call(
+        own_rows_kernel,
+        in_specs=[IN_VMEM],
+        out_specs=IN_VMEM,
+        out_shape=pltpu.VMEM((SHIFTS * depths, rows + 2 * REACH, columns, pixels), jnp.bfloat16),
+        compiler_params=pltpu.CompilerParams(vmem_limit_bytes=SMALL),
+        cost_estimate=pl.CostEstimate(flops=0, bytes_accessed=10 * 1024 * 1024, transcendentals=0),
+        name="own_rows",
+    )(volume)
+
+
+def edge_rows(above, below, copies):
+    return pl.pallas_call(
+        edge_rows_kernel,
+        in_specs=[IN_VMEM, IN_VMEM, IN_VMEM],
+        out_specs=IN_VMEM,
+        out_shape=pltpu.VMEM(copies.shape, copies.dtype),
+        input_output_aliases={2: 0},
+        compiler_params=pltpu.CompilerParams(vmem_limit_bytes=SMALL),
+        name="edge_rows",
+    )(above, below, copies)
+
+
+def operator_spot(scalars, op, depths):
+    end, depth = jnp.int32(0), jnp.int32(0)
+    for d in range(depths):
+        end = end + scalars[d]
+        depth = depth + jnp.where(op >= end, 1, 0)
+    at = depths + 2 * op
+    return (scalars[at + 1] + REACH) * depths + depth, scalars[at] + REACH
+
+
+def add_kernel(scalars, copies, *refs, plan, pieces, first, last):
+    weights = refs[: 2 * pieces]
+    refs = refs[2 * pieces :]
+    if last:
+        meas, dark, old, pred_out, ratio_out, acc, pred, ratio, sems = refs
+    elif first:
+        old, acc = None, refs[0]
+    else:
+        old, acc = refs
+    depths = copies.shape[0] // SHIFTS
+    columns, pixels = copies.shape[2:]
+    lines = acc.shape[1]
+    rows = lines // columns
+    here, side = scalars[scalars.shape[0] - 2], scalars[scalars.shape[0] - 1]
+    dims = (((1,), (1,)), ((), ()))
+    jobs = []
+    for n, (hops, other, kind) in enumerate(plan):
+        shard = ((here + (16 - 4 * hops)) % 16) ^ (2 * other)
+        half = n if kind is None else side ^ kind
+        spots = []
+        for core in range(2):
+            for which in range(2):
+                spots.append(operator_spot(scalars, 2 * (shard ^ core) + which, depths))
+        jobs.append((n, half, spots))
+
+    for t in range(rows // TILE):
+        m = slice(t * TILE * columns, (t + 1) * TILE * columns)
+        for n, half, spots in jobs:
+            total = None
+            for j, (copy, row) in enumerate(spots):
+                w_ref = weights[2 * n + j // 2]
+                w = w_ref[0] if w_ref.shape[0] == 1 else w_ref[n]
+                w = w[:, pixels * (j % 2) : pixels * (j % 2 + 1)]
+                slab = copies[copy, pl.ds(row + t * TILE, TILE)].reshape(TILE * columns, pixels)
+                part = lax.dot_general(slab, w, dims, preferred_element_type=jnp.float32)
+                total = part if total is None else total + part
+            if first:
+                acc[half, m] = total
+            elif last and n == 0:
+                acc[half, m] = old[half, m] + total
+                acc[1 - half, m] = old[1 - half, m]
+            elif last:
+                acc[half, m] = acc[half, m] + total
+            else:
+                acc[half, m] = acc[half, m] + total if n else old[half, m] + total
+        if last:
+            r = slice(t * TILE, (t + 1) * TILE)
+            full = jnp.concatenate([acc[0, m], acc[1, m]], axis=1).reshape(TILE, columns, pixels)
+            pred[r] = full
+            ratio[r] = meas[r] / (full + dark[...].reshape(1, 1, pixels))
+            for q, (src, dst) in enumerate(((pred, pred_out), (ratio, ratio_out))):
+                pltpu.make_async_copy(src.at[r], dst.at[r], sems.at[2 * t + q]).start()
+    if last:
+        for t in range(rows // TILE):
+            r = slice(t * TILE, (t + 1) * TILE)
+            for q, (src, dst) in enumerate(((pred, pred_out), (ratio, ratio_out))):
+                pltpu.make_async_copy(src.at[r], dst.at[r], sems.at[2 * t + q]).wait()
+
+
+def add_pieces(scalars, copies, weights, plan, acc, final=None):
+    columns, pixels = copies.shape[2:]
+    rows = copies.shape[1] - 2 * REACH
+    lines, part = rows * columns, pixels // 2
+    pieces = len(plan)
+    operands = [scalars, copies, *weights]
+    shape = (2, lines, part)
+    scratch, params = [], {}
+    alias = {}
+    if final is not None:
+        operands += [*final, acc]
+        full = final[0].shape
+        out_shape = [jax.ShapeDtypeStruct(full, jnp.float32)] * 2
+        out_specs = [IN_HBM] * 2
+        scratch = [pltpu.VMEM(shape, jnp.float32), pltpu.VMEM(full, jnp.float32), pltpu.VMEM(full, jnp.float32)]
+        scratch.append(pltpu.SemaphoreType.DMA((2 * (rows // TILE),)))
+    else:
+        out_shape, out_specs = pltpu.VMEM(shape, jnp.float32), IN_VMEM
+        if acc is not None:
+            alias = {len(operands): 0}
+            operands.append(acc)
+    flops = 2 * lines * 4 * pixels * part * pieces
+    return pl.pallas_call(
+        functools.partial(add_kernel, plan=plan, pieces=pieces, first=acc is None, last=final is not None),
+        in_specs=[IN_SMEM] + [IN_VMEM] * (len(operands) - 1),
+        out_specs=out_specs,
+        out_shape=out_shape,
+        scratch_shapes=scratch,
+        input_output_aliases=alias,
+        cost_estimate=pl.CostEstimate(flops=flops, bytes_accessed=pieces * 1024 * 1024, transcendentals=0),
+        compiler_params=pltpu.CompilerParams(vmem_limit_bytes=SMALL),
+        name="add_pieces",
+    )(*operands)
+
+
+def placements(offset_counts, offset_table):
+    depths = offset_counts.shape[0]
     planes = jnp.arange(depths, dtype=jnp.int32)
     ends = jnp.sum(jnp.where(planes[None, :] <= planes[:, None], offset_counts[None, :], 0), axis=1)
-    positions = jnp.arange(op_total, dtype=jnp.int32)
+    positions = jnp.arange(offset_table.shape[0], dtype=jnp.int32)
     depth_of = jnp.sum((positions[:, None] >= ends[None, :]).astype(jnp.int32), axis=1)
-    place = (offset_table[:, 1] + REACH) * depths + depth_of
-    start = offset_table[:, 0] + REACH
-
+    return (offset_table[:, 1] + REACH) * depths + depth_of, offset_table[:, 0] + REACH
+
+
+def exchanged(volume, measured, operator_rows, offset_counts, offset_table, dark_level):
+    depths, rows, columns, pixels = volume.shape
+    part = pixels // 2
+    side = lax.axis_index("frames")
+    here = lax.axis_index("lenslet")
+    count = lax.axis_size("lenslet")
+    scalars = jnp.concatenate([offset_counts, offset_table.reshape(-1), jnp.stack([here, side])])
+
+    up = [(i, (i + 4) % count) for i in range(count)]
+    beside = [(i, i ^ 2) for i in range(count)]
+    twin = [(i, i ^ 1) for i in range(count)]
+    along_z = lambda v: lax.ppermute(v, "lenslet", up)
+    along_y = lambda v: lax.ppermute(v, "lenslet", beside)
+    to_core = lambda v: lax.ppermute(v, "lenslet", twin)
+    along_x = lambda v: lax.ppermute(v, "frames", [(0, 1), (1, 0)])
+
+    own = operator_rows.T.reshape(2, part, 2 * pixels)
+    own_a = lax.dynamic_index_in_dim(own, side, 0)
+    own_b = lax.dynamic_index_in_dim(own, 1 - side, 0)
+    both = lambda *pieces: [w for piece in pieces for w in (piece, to_core(piece))]
+
+    t1a, y0a = along_z(own_a), along_y(own_a)
+    above = passed_along(volume[:, rows - REACH :], "lenslet", 1)
+    below = passed_along(volume[:, :REACH], "lenslet", -1)
+    own_c = to_core(own)
+    copies = own_rows(volume)
+    t2a, y1a, y0b = along_z(t1a), along_y(t1a), along_x(y0a)
+    r0 = both(t1a, y0a)
+    copies = edge_rows(above, below, copies)
+    a, b = 0, 1
+    acc = add_pieces(scalars, copies, [own, own_c, own, own_c], [(0, 0, None), (0, 0, None)], None)
+    t3a, y2a, y1b = along_z(t2a), along_y(t2a), along_x(y1a)
+    r1 = both(t2a, y1a, y0b)
+    acc = add_pieces(scalars, copies, r0, [(1, 0, a), (0, 1, a)], acc)
+    t1b, y3a, t2b = along_z(own_b), along_y(t3a), along_x(t2a)
+    r2 = both(t3a, y2a, y1b)
+    acc = add_pieces(scalars, copies, r1, [(2, 0, a), (1, 1, a), (0, 1, b)], acc)
+    t3b, y2b, y3b = along_z(t2b), along_y(t2b), along_x(y3a)
+    r3 = both(t1b, y3a, t2b)
+    acc = add_pieces(scalars, copies, r2, [(3, 0, a), (2, 1, a), (1, 1, b)], acc)
+    r4 = both(t3b, y2b, y3b)
+    acc = add_pieces(scalars, copies, r3, [(1, 0, b), (3, 1, a), (2, 0, b)], acc)
+    final = (measured, dark_level.reshape(1, pixels))
+    return tuple(add_pieces(scalars, copies, r4, [(3, 0, b), (2, 1, b), (3, 1, b)], acc, final))
+
+
+def gathered(volume, measured, operator_rows, offset_counts, offset_table, dark_level):
+    depths, rows, columns, pixels = volume.shape
+    place, start = placements(offset_counts, offset_table)
     weights = gathered_pairs(operator_rows)
     above = passed_along(volume[:, rows - REACH :], "lenslet", 1)
     below = passed_along(volume[:, :REACH], "lenslet", -1)
     copies = shifted_copies(volume, above, below)
     copies = copies.reshape(SHIFTS * depths, rows + 2 * REACH, columns, pixels)
     return tuple(project(copies, weights, place, start, measured, dark_level))
+
+
+def body(volume, measured, operator_rows, offset_counts, offset_table, dark_level):
+    pairs = operator_rows.shape[0] == 2 * operator_rows.shape[1]
+    known = lax.axis_size("lenslet") == 16 and lax.axis_size("frames") == 2
+    form = exchanged if pairs and known else gathered
+    return form(volume, measured, operator_rows, offset_counts, offset_table, dark_level)
 
 
 def solution(mesh):

time: 148 us -> 118 us (0.80)
  waiting for transfers between devices: 78.5 us -> 25.9 us
  starting transfers between devices: 4.39 us -> 31.5 us
  local copies, waits for them, and re-layouts: 2.87 us -> 25.7 us
  between operations: 14.1 us -> 1.15 us
  Pallas kernels: 43.9 us -> 33 us
  other arithmetic: 3.32 us -> 0.08 us
    all_gather x1 -> x0, waiting for transfers between devices: 77.8 us -> none  [gathered_pairs(): return lax.all_gather(operator_rows.T, 'lenslet', axis=0)]
    ppermute x0 -> x29, starting transfers between devices: none -> 28.7 us  [the longest x5 9.09 us: exchanged(): along_z = lambda v: lax.ppermute(v, 'lenslet', up)]
    ppermute x0 -> x29, waiting for transfers between devices: none -> 25.9 us  [the longest x5 19.7 us: exchanged(): along_z = lambda v: lax.ppermute(v, 'lenslet', up)]
    unnamed x4 -> x41, local copies, waits for them, and re-layouts: 1.58 us -> 23.1 us
    pallas_call x2 -> x8, Pallas kernels: 43.9 us -> 33 us  [the longest x6 28.2 us: add_pieces(): pl.pallas_call(functools.partial(add_kernel, plan=plan, pieces=pieces, fi...]
    add x2 -> x0, other arithmetic: 2.46 us -> none  [the longest x1 1.26 us: body(): place = (offset_table[:, 1] + REACH) * depths + depth_of]
    ppermute x2, starting transfers between devices: 4.36 us -> 2.73 us  [passed_along(): return lax.ppermute(block, axis, route)]
  transfers between devices with their start and end apart: 3 -> 31, of which waited for: 1 -> 9; matrix products, arithmetic and copies ran while one was open for 3% -> 1% of each run, Pallas kernels for 8% -> 22%
where the time goes in v2:
time: 118 us; the launch traced here: 117 us
  Pallas kernels  33 us (28%)
  starting transfers between devices  31.5 us (27%)
  waiting for transfers between devices  25.9 us (22%)
  local copies, waits for them, and re-layouts  25.7 us (22%)
    pallas_call x6, Pallas kernels, add_pieces(): pl.pallas_call(functools.partial(add_kernel, plan=plan, pieces=pieces, fi...  28.2 us
    unnamed x41, local copies, waits for them, and re-layouts  23.1 us
    ppermute x5, waiting for transfers between devices, exchanged(): along_z = lambda v: lax.ppermute(v, 'lenslet', up)  19.7 us
    ppermute x5, starting transfers between devices, exchanged(): along_z = lambda v: lax.ppermute(v, 'lenslet', up)  9.09 us
    ppermute x5, starting transfers between devices, exchanged(): along_y = lambda v: lax.ppermute(v, 'lenslet', beside)  9.09 us
    ppermute x15, starting transfers between devices, exchanged(): to_core = lambda v: lax.ppermute(v, 'lenslet', twin)  5.83 us
    ppermute x4, waiting for transfers between devices, exchanged(): along_x = lambda v: lax.ppermute(v, 'frames', [(0, 1), (1, 0)])  4.96 us
    ppermute x4, starting transfers between devices, exchanged(): along_x = lambda v: lax.ppermute(v, 'frames', [(0, 1), (1, 0)])  4.72 us
  transfers between devices with their start and end apart: 31, of which 9 were waited for; matrix products, arithmetic and copies ran while one was open for 1% of the time, Pallas kernels for 22%

profile of v2, /device:TPU:0, one launch (start us, length us, event | category | flops | bytes accessed | tf_op | source)
XLA Modules:
  0.0 117.4 jit_solution(15211503880072659887)
XLA Ops:
  0.6 1.2 %constant_dynamic-slice_fusion = (bf16[1,200,800]{2,1,0:T(8,128)(2,1)S(1)}, bf16[1,200,800]{2,1,0:T(8,128)(2,1)S(1)}) fusion(bf16[2,200,800]{2,1,0:T(8,128)(2,1)} %bitcast.6, s32[]{:T(128)S(6)} %select_n.8, s32[]{:T(128)S(6)} %select_n.7), kind=kLoop, calls=%fused_computation.1 | loop fusion | bytes 1280008 | tf_op jit(solution)/shard_map/jit(dynamic_index_in_dim)/dynamic_slice | solution.py:336
  1.9 3.1 %collective-permute-start.2 = (bf16[1,200,800]{2,1,0:T(8,128)(2,1)S(1)}, bf16[1,200,800]{2,1,0:T(8,128)(2,1)S(1)}, u32[]{:S(2)}, u32[]{:S(2)}) collective-permute-start(bf16[1,200,800]{2,1,0:T(8,128)(2,1)S(1)} %get-tuple-element.5), channel_id=1, source_target_pairs={{0,4},{1,5},{2,6},{3,7},{4,8},{5,9},{6,10},{7,11},{8,12},{9,13},{1... | collective-permute-start | bytes 960008 | tf_op jit(solution)/shard_map/ppermute | solution.py:329
  4.9 1.6 %collective-permute-start.13 = (bf16[1,200,800]{2,1,0:T(8,128)(2,1)S(1)}, bf16[1,200,800]{2,1,0:T(8,128)(2,1)S(1)}, u32[]{:S(2)}, u32[]{:S(2)}) collective-permute-start(bf16[1,200,800]{2,1,0:T(8,128)(2,1)S(1)} %get-tuple-element.4), channel_id=1, source_target_pairs={{0,4},{1,5},{2,6},{3,7},{4,8},{5,9},{6,10},{7,11},{8,12},{9,13},{1... | collective-permute-start | bytes 960008 | tf_op jit(solution)/shard_map/ppermute | solution.py:329
  6.5 1.3 %fusion = (bf16[4,2,64,400]{3,2,1,0:T(8,128)(2,1)S(1)}, bf16[4,2,64,400]{3,2,1,0:T(8,128)(2,1)S(1)}) fusion(bf16[4,16,64,400]{3,2,1,0:T(8,128)(2,1)} %volume_ref.1), kind=kLoop, calls=%fused_computation.3 | loop fusion | bytes 1638400 | tf_op jit(solution)/shard_map/slice | solution.py:341
  7.8 1.3 %collective-permute-start = (bf16[4,2,64,400]{3,2,1,0:T(8,128)(2,1)S(1)}, bf16[4,2,64,400]{3,2,1,0:T(8,128)(2,1)S(1)}, u32[]{:S(2)}, u32[]{:S(2)}) collective-permute-start(bf16[4,2,64,400]{3,2,1,0:T(8,128)(2,1)S(1)} %get-tuple-element.3), channel_id=1, source_target_pairs={{0,1},{1,2},{2,3},{3,4},{4,5},{5,6},{6,7},{7,8},{8,9},{9,10},{10,1... | collective-permute-start | bytes 1228808 | tf_op jit(solution)/shard_map/ppermute | solution.py:20
  9.2 2.2 %collective-permute-start.25 = (bf16[1,200,800]{2,1,0:T(8,128)(2,1)S(1)}, bf16[1,200,800]{2,1,0:T(8,128)(2,1)S(1)}, u32[]{:S(2)}, u32[]{:S(2)}) collective-permute-start(bf16[1,200,800]{2,1,0:T(8,128)(2,1)S(1)} %get-tuple-element.5), channel_id=1, source_target_pairs={{0,2},{1,3},{2,0},{3,1},{4,6},{5,7},{6,4},{7,5},{8,10},{9,11},{10,... | collective-permute-start | bytes 960008 | tf_op jit(solution)/shard_map/ppermute | solution.py:330
  11.3 1.4 %collective-permute-start.1 = (bf16[4,2,64,400]{3,2,1,0:T(8,128)(2,1)S(1)}, bf16[4,2,64,400]{3,2,1,0:T(8,128)(2,1)S(1)}, u32[]{:S(2)}, u32[]{:S(2)}) collective-permute-start(bf16[4,2,64,400]{3,2,1,0:T(8,128)(2,1)S(1)} %get-tuple-element.2), channel_id=1, source_target_pairs={{1,0},{2,1},{3,2},{4,3},{5,4},{6,5},{7,6},{8,7},{9,8},{10,9},{11,1... | collective-permute-start | bytes 1228808 | tf_op jit(solution)/shard_map/ppermute | solution.py:20
  12.8 3.4 %collective-permute-done.2.refs_0_ = bf16[1,200,800]{2,1,0:T(8,128)(2,1)S(1)} collective-permute-done((bf16[1,200,800]{2,1,0:T(8,128)(2,1)S(1)}, bf16[1,200,800]{2,1,0:T(8,128)(2,1)S(1)}, u32[]{:S(2)}, u32[]{:S(2)}) %collective-permute-start.2) | collective-permute-done | bytes 320032 | tf_op jit(solution)/shard_map/ppermute | solution.py:329
  16.4 7.6 %collective-permute-done.13.refs_0_ = bf16[1,200,800]{2,1,0:T(8,128)(2,1)S(1)} collective-permute-done((bf16[1,200,800]{2,1,0:T(8,128)(2,1)S(1)}, bf16[1,200,800]{2,1,0:T(8,128)(2,1)S(1)}, u32[]{:S(2)}, u32[]{:S(2)}) %collective-permute-start.13) | collective-permute-done | bytes 320032 | tf_op jit(solution)/shard_map/ppermute | solution.py:329
  24.0 3.3 %collective-permute-start.30 = (bf16[2,200,800]{2,1,0:T(8,128)(2,1)S(1)}, bf16[2,200,800]{2,1,0:T(8,128)(2,1)S(1)}, u32[]{:S(2)}, u32[]{:S(2)}) collective-permute-start(bf16[2,200,800]{2,1,0:T(8,128)(2,1)S(1)} %bitcast.7), channel_id=1, source_target_pairs={{0,1},{1,0},{2,3},{3,2},{4,5},{5,4},{6,7},{7,6},{8,9},{9,8},{10,11... | collective-permute-start | bytes 1920008 | tf_op jit(solution)/shard_map/ppermute | solution.py:331
  27.3 2.7 %collective-permute-start.20 = (bf16[1,200,800]{2,1,0:T(8,128)(2,1)S(1)}, bf16[1,200,800]{2,1,0:T(8,128)(2,1)}, u32[]{:S(2)}, u32[]{:S(2)}) collective-permute-start(bf16[1,200,800]{2,1,0:T(8,128)(2,1)S(1)} %collective-permute-done.2.refs_0_), channel_id=1, source_target_pairs={{0,2},{1,3},{2,0},{3,1},{4,6},{5,7},{6,4},{7,5},{8,10},{9,11},{10,... | collective-permute-start | bytes 960008 | tf_op jit(solution)/shard_map/ppermute | solution.py:330
  30.0 1.2 %collective-permute-start.26 = (bf16[1,200,800]{2,1,0:T(8,128)(2,1)S(1)}, bf16[1,200,800]{2,1,0:T(8,128)(2,1)}, u32[]{:S(2)}, u32[]{:S(2)}) collective-permute-start(bf16[1,200,800]{2,1,0:T(8,128)(2,1)S(1)} %collective-permute-done.25.refs_2_), channel_id=1, source_target_pairs={{0,16},{16,0},{1,17},{17,1},{2,18},{18,2},{3,19},{19,3},{4,20},{20... | collective-permute-start | bytes 960008 | tf_op jit(solution)/shard_map/ppermute | solution.py:332
  31.2 5.2 %collective-permute-done.3.refs_0_ = bf16[1,200,800]{2,1,0:T(8,128)(2,1)} collective-permute-done((bf16[1,200,800]{2,1,0:T(8,128)(2,1)S(1)}, bf16[1,200,800]{2,1,0:T(8,128)(2,1)}, u32[]{:S(2)}, u32[]{:S(2)}) %collective-permute-start.3) | collective-permute-done | bytes 320032 | tf_op jit(solution)/shard_map/ppermute | solution.py:329
  39.1 1.5 %collective-permute-start.4 = (bf16[1,200,800]{2,1,0:T(8,128)(2,1)}, bf16[1,200,800]{2,1,0:T(8,128)(2,1)}, u32[]{:S(2)}, u32[]{:S(2)}) collective-permute-start(bf16[1,200,800]{2,1,0:T(8,128)(2,1)} %collective-permute-done.3.refs_0_), channel_id=1, source_target_pairs={{0,16},{16,0},{1,17},{17,1},{2,18},{18,2},{3,19},{19,3},{4,20},{20... | collective-permute-start | bytes 960008 | tf_op jit(solution)/shard_map/ppermute | solution.py:332
  41.2 3.5 %collective-permute-start.9 = (bf16[1,200,800]{2,1,0:T(8,128)(2,1)}, bf16[1,200,800]{2,1,0:T(8,128)(2,1)}, u32[]{:S(2)}, u32[]{:S(2)}) collective-permute-start(bf16[1,200,800]{2,1,0:T(8,128)(2,1)} %collective-permute-done.3.refs_0_), channel_id=1, source_target_pairs={{0,4},{1,5},{2,6},{3,7},{4,8},{5,9},{6,10},{7,11},{8,12},{9,13},{1... | collective-permute-start | bytes 960008 | tf_op jit(solution)/shard_map/ppermute | solution.py:329
  45.5 1.7 %collective-permute-start.18 = (bf16[1,200,800]{2,1,0:T(8,128)(2,1)}, bf16[1,200,800]{2,1,0:T(8,128)(2,1)S(1)}, u32[]{:S(2)}, u32[]{:S(2)}) collective-permute-start(bf16[1,200,800]{2,1,0:T(8,128)(2,1)} %collective-permute-done.3.refs_0_), channel_id=1, source_target_pairs={{0,2},{1,3},{2,0},{3,1},{4,6},{5,7},{6,4},{7,5},{8,10},{9,11},{10,... | collective-permute-start | bytes 960008 | tf_op jit(solution)/shard_map/ppermute | solution.py:330
  48.5 2.1 %collective-permute-done.4.refs_4_ = bf16[1,200,800]{2,1,0:T(8,128)(2,1)} collective-permute-done((bf16[1,200,800]{2,1,0:T(8,128)(2,1)}, bf16[1,200,800]{2,1,0:T(8,128)(2,1)}, u32[]{:S(2)}, u32[]{:S(2)}) %collective-permute-start.4) | collective-permute-done | bytes 320032 | tf_op jit(solution)/shard_map/ppermute | solution.py:332
  50.6 3.4 %collective-permute-done.9.refs_0_ = bf16[1,200,800]{2,1,0:T(8,128)(2,1)} collective-permute-done((bf16[1,200,800]{2,1,0:T(8,128)(2,1)}, bf16[1,200,800]{2,1,0:T(8,128)(2,1)}, u32[]{:S(2)}, u32[]{:S(2)}) %collective-permute-start.9) | collective-permute-done | bytes 320032 | tf_op jit(solution)/shard_map/ppermute | solution.py:329
  55.4 2.2 %collective-permute-done.21.refs_4_ = bf16[1,200,800]{2,1,0:T(8,128)(2,1)S(1)} collective-permute-done((bf16[1,200,800]{2,1,0:T(8,128)(2,1)}, bf16[1,200,800]{2,1,0:T(8,128)(2,1)S(1)}, u32[]{:S(2)}, u32[]{:S(2)}) %collective-permute-start.21) | collective-permute-done | bytes 320032 | tf_op jit(solution)/shard_map/ppermute | solution.py:332
  58.3 2.4 %collective-permute-start.10 = (bf16[1,200,800]{2,1,0:T(8,128)(2,1)}, bf16[1,200,800]{2,1,0:T(8,128)(2,1)}, u32[]{:S(2)}, u32[]{:S(2)}) collective-permute-start(bf16[1,200,800]{2,1,0:T(8,128)(2,1)} %collective-permute-done.9.refs_0_), channel_id=1, source_target_pairs={{0,2},{1,3},{2,0},{3,1},{4,6},{5,7},{6,4},{7,5},{8,10},{9,11},{10,... | collective-permute-start | bytes 960008 | tf_op jit(solution)/shard_map/ppermute | solution.py:330
  60.7 2.2 %copy-done.2 = bf16[4,16,64,400]{3,2,1,0:T(8,128)(2,1)S(1)} copy-done((bf16[4,16,64,400]{3,2,1,0:T(8,128)(2,1)S(1)}, bf16[4,16,64,400]{3,2,1,0:T(8,128)(2,1)}, u32[]{:S(2)}) %copy-start.2) | copy-done | bytes 3276824
  62.9 3.8 %own_rows.1.old_ref = bf16[20,20,64,400]{3,2,1,0:T(8,128)(2,1)S(1)} custom-call(bf16[4,16,64,400]{3,2,1,0:T(8,128)(2,1)S(1)} %copy-done.2), custom_call_target="tpu_custom_call" | custom-call | bytes 10485760 | tf_op jit(solution)/shard_map/own_rows/pallas_call | solution.py:183
  66.7 8.7 %copy-done = bf16[20,20,64,400]{3,2,1,0:T(8,128)(2,1)} copy-done((bf16[20,20,64,400]{3,2,1,0:T(8,128)(2,1)}, bf16[20,20,64,400]{3,2,1,0:T(8,128)(2,1)S(1)}, u32[]{:S(2)}) %copy-start) | copy-done | bytes 20480024
  75.8 8.5 %copy-done.1 = bf16[20,20,64,400]{3,2,1,0:T(8,128)(2,1)S(1)} copy-done((bf16[20,20,64,400]{3,2,1,0:T(8,128)(2,1)S(1)}, bf16[20,20,64,400]{3,2,1,0:T(8,128)(2,1)}, u32[]{:S(2)}) %copy-start.1) | copy-done | bytes 20480024
  84.3 1.1 edge_rows.1.copies
  86.0 1.5 %collective-permute-start.11 = (bf16[1,200,800]{2,1,0:T(8,128)(2,1)}, bf16[1,200,800]{2,1,0:T(8,128)(2,1)S(1)}, u32[]{:S(2)}, u32[]{:S(2)}) collective-permute-start(bf16[1,200,800]{2,1,0:T(8,128)(2,1)} %collective-permute-done.10.refs_2_), channel_id=1, source_target_pairs={{0,16},{16,0},{1,17},{17,1},{2,18},{18,2},{3,19},{19,3},{4,20},{20... | collective-permute-start | bytes 960008 | tf_op jit(solution)/shard_map/ppermute | solution.py:332
  87.5 3.0 %add_pieces.6.refs_4_ = f32[2,1024,200]{2,1,0:T(8,128)S(1)} custom-call(s32[70]{0:T(128)S(1)} %pad_add_fusion.scalars, bf16[20,20,64,400]{3,2,1,0:T(8,128)(2,1)S(1)} %edge_rows.1.copies, bf16[2,200,800]{2,1,0:T(8,128)(2,1)S(1)} %bitcast.8, bf16[2,200,800]{2,1,0:T(8,128)(2,1)S(1)} %collective-permute-done.30.refs_1_.refs_3_, ...), custom_call_target="tpu_custom_call" | custom-call | flops 1310720000 | bytes 2097152 | tf_op jit(solution)/shard_map/add_pieces/pallas_call | solution.py:296
  90.6 3.1 %add_pieces.7.refs_6_ = f32[2,1024,200]{2,1,0:T(8,128)S(1)} custom-call(s32[70]{0:T(128)S(1)} %pad_add_fusion.scalars, bf16[20,20,64,400]{3,2,1,0:T(8,128)(2,1)S(1)} %edge_rows.1.copies, bf16[1,200,800]{2,1,0:T(8,128)(2,1)S(1)} %copy-done.10, bf16[1,200,800]{2,1,0:T(8,128)(2,1)S(1)} %copy-done.14, ...), custom_call_target="tpu_custom_call", output_to_operand_aliasing={{}: (6, {})} | custom-call | flops 1310720000 | bytes 2097152 | tf_op jit(solution)/shard_map/add_pieces/pallas_call | solution.py:296
  94.3 5.2 %add_pieces.8.refs_6_ = f32[2,1024,200]{2,1,0:T(8,128)S(1)} custom-call(s32[70]{0:T(128)S(1)} %pad_add_fusion.scalars, bf16[20,20,64,400]{3,2,1,0:T(8,128)(2,1)S(1)} %edge_rows.1.copies, bf16[1,200,800]{2,1,0:T(8,128)(2,1)} %collective-permute-done.3.refs_0_, bf16[1,200,800]{2,1,0:T(8,128)(2,1)} %collective-permute-done.23.refs_1_, ...), custom_call_target="tpu_custom_call", output_to_operand_aliasing={{}: (8, {})} | custom-call | flops 1966080000 | bytes 3145728 | tf_op jit(solution)/shard_map/add_pieces/pallas_call | solution.py:296
  100.3 4.8 %add_pieces.9.refs_6_ = f32[2,1024,200]{2,1,0:T(8,128)S(1)} custom-call(s32[70]{0:T(128)S(1)} %pad_add_fusion.scalars, bf16[20,20,64,400]{3,2,1,0:T(8,128)(2,1)S(1)} %edge_rows.1.copies, bf16[1,200,800]{2,1,0:T(8,128)(2,1)} %collective-permute-done.9.refs_0_, ...), custom_call_target="tpu_custom_call", output_to_operand_aliasing={{}: (8, {})} | custom-call | flops 1966080000 | bytes 3145728 | tf_op jit(solution)/shard_map/add_pieces/pallas_call | solution.py:296
  105.1 5.2 %add_pieces.10.refs_8_ = f32[2,1024,200]{2,1,0:T(8,128)S(1)} custom-call(s32[70]{0:T(128)S(1)} %pad_add_fusion.scalars, bf16[20,20,64,400]{3,2,1,0:T(8,128)(2,1)S(1)} %edge_rows.1.copies, bf16[1,200,800]{2,1,0:T(8,128)(2,1)S(1)} %collective-permute-done.13.refs_0_, ...), custom_call_target="tpu_custom_call", output_to_operand_aliasing={{}: (8, {})} | custom-call | flops 1966080000 | bytes 3145728 | tf_op jit(solution)/shard_map/add_pieces/pallas_call | solution.py:296
  110.3 6.8 %add_pieces.11 = (f32[16,64,400]{2,1,0:T(8,128)}, f32[16,64,400]{2,1,0:T(8,128)}) custom-call(s32[70]{0:T(128)S(1)} %pad_add_fusion.scalars, bf16[20,20,64,400]{3,2,1,0:T(8,128)(2,1)S(1)} %edge_rows.1.copies, bf16[1,200,800]{2,1,0:T(8,128)(2,1)} %collective-permute-done.5.refs_0_, bf16[1,200,800]{2,1,0:T(8,128)(2,1)S(1)} %collective-permute-done.6.refs_1_, ...), custom_call_target="tpu_custom_call" | custom-call | flops 1966080000 | bytes 3145728 | tf_op jit(solution)/shard_map/add_pieces/pallas_call | solution.py:296
  (83 shorter events, 10.0 us)
Async XLA Ops:
  1.9 14.3 %collective-permute-start.2 = (bf16[1,200,800]{2,1,0:T(8,128)(2,1)S(1)}, bf16[1,200,800]{2,1,0:T(8,128)(2,1)S(1)}, u32[]{:S(2)}, u32[]{:S(2)}) collective-permute-start(bf16[1,200,800]{2,1,0:T(8,128)(2,1)S(1)} %get-tuple-element.5), channel_id=1, source_target_pairs={{0,4},{1,5},{2,6},{3,7},{4,8},{5,9},{6,10},{7,11},{8,12},{9,13},{1... | collective-permute-start | bytes 960008 | tf_op jit(solution)/shard_map/ppermute | solution.py:329
  4.9 19.0 %collective-permute-start.13 = (bf16[1,200,800]{2,1,0:T(8,128)(2,1)S(1)}, bf16[1,200,800]{2,1,0:T(8,128)(2,1)S(1)}, u32[]{:S(2)}, u32[]{:S(2)}) collective-permute-start(bf16[1,200,800]{2,1,0:T(8,128)(2,1)S(1)} %get-tuple-element.4), channel_id=1, source_target_pairs={{0,4},{1,5},{2,6},{3,7},{4,8},{5,9},{6,10},{7,11},{8,12},{9,13},{1... | collective-permute-start | bytes 960008 | tf_op jit(solution)/shard_map/ppermute | solution.py:329
  7.8 19.4 %collective-permute-start = (bf16[4,2,64,400]{3,2,1,0:T(8,128)(2,1)S(1)}, bf16[4,2,64,400]{3,2,1,0:T(8,128)(2,1)S(1)}, u32[]{:S(2)}, u32[]{:S(2)}) collective-permute-start(bf16[4,2,64,400]{3,2,1,0:T(8,128)(2,1)S(1)} %get-tuple-element.3), channel_id=1, source_target_pairs={{0,1},{1,2},{2,3},{3,4},{4,5},{5,6},{6,7},{7,8},{8,9},{9,10},{10,1... | collective-permute-start | bytes 1228808 | tf_op jit(solution)/shard_map/ppermute | solution.py:20
  9.2 14.8 %collective-permute-start.25 = (bf16[1,200,800]{2,1,0:T(8,128)(2,1)S(1)}, bf16[1,200,800]{2,1,0:T(8,128)(2,1)S(1)}, u32[]{:S(2)}, u32[]{:S(2)}) collective-permute-start(bf16[1,200,800]{2,1,0:T(8,128)(2,1)S(1)} %get-tuple-element.5), channel_id=1, source_target_pairs={{0,2},{1,3},{2,0},{3,1},{4,6},{5,7},{6,4},{7,5},{8,10},{9,11},{10,... | collective-permute-start | bytes 960008 | tf_op jit(solution)/shard_map/ppermute | solution.py:330
  11.3 64.4 %copy-start.19 = (s32[4]{0:T(128)S(1)}, s32[4]{0:T(128)}, u32[]{:S(2)}) copy-start(s32[4]{0:T(128)} %param.9) | copy-start | bytes 52
  11.3 18.7 %collective-permute-start.1 = (bf16[4,2,64,400]{3,2,1,0:T(8,128)(2,1)S(1)}, bf16[4,2,64,400]{3,2,1,0:T(8,128)(2,1)S(1)}, u32[]{:S(2)}, u32[]{:S(2)}) collective-permute-start(bf16[4,2,64,400]{3,2,1,0:T(8,128)(2,1)S(1)} %get-tuple-element.2), channel_id=1, source_target_pairs={{1,0},{2,1},{3,2},{4,3},{5,4},{6,5},{7,6},{8,7},{9,8},{10,9},{11,1... | collective-permute-start | bytes 1228808 | tf_op jit(solution)/shard_map/ppermute | solution.py:20
  16.2 20.3 %collective-permute-start.3 = (bf16[1,200,800]{2,1,0:T(8,128)(2,1)S(1)}, bf16[1,200,800]{2,1,0:T(8,128)(2,1)}, u32[]{:S(2)}, u32[]{:S(2)}) collective-permute-start(bf16[1,200,800]{2,1,0:T(8,128)(2,1)S(1)} %collective-permute-done.2.refs_0_), channel_id=1, source_target_pairs={{0,4},{1,5},{2,6},{3,7},{4,8},{5,9},{6,10},{7,11},{8,12},{9,13},{1... | collective-permute-start | bytes 960008 | tf_op jit(solution)/shard_map/ppermute | solution.py:329
  23.9 13.3 %collective-permute-start.14 = (bf16[1,200,800]{2,1,0:T(8,128)(2,1)S(1)}, bf16[1,200,800]{2,1,0:T(8,128)(2,1)S(1)}, u32[]{:S(2)}, u32[]{:S(2)}) collective-permute-start(bf16[1,200,800]{2,1,0:T(8,128)(2,1)S(1)} %collective-permute-done.13.refs_0_), channel_id=1, source_target_pairs={{0,1},{1,0},{2,3},{3,2},{4,5},{5,4},{6,7},{7,6},{8,9},{9,8},{10,11... | collective-permute-start | bytes 960008 | tf_op jit(solution)/shard_map/ppermute | solution.py:331
  24.0 24.6 %collective-permute-start.30 = (bf16[2,200,800]{2,1,0:T(8,128)(2,1)S(1)}, bf16[2,200,800]{2,1,0:T(8,128)(2,1)S(1)}, u32[]{:S(2)}, u32[]{:S(2)}) collective-permute-start(bf16[2,200,800]{2,1,0:T(8,128)(2,1)S(1)} %bitcast.7), channel_id=1, source_target_pairs={{0,1},{1,0},{2,3},{3,2},{4,5},{5,4},{6,7},{7,6},{8,9},{9,8},{10,11... | collective-permute-start | bytes 1920008 | tf_op jit(solution)/shard_map/ppermute | solution.py:331
  27.3 11.8 %collective-permute-start.20 = (bf16[1,200,800]{2,1,0:T(8,128)(2,1)S(1)}, bf16[1,200,800]{2,1,0:T(8,128)(2,1)}, u32[]{:S(2)}, u32[]{:S(2)}) collective-permute-start(bf16[1,200,800]{2,1,0:T(8,128)(2,1)S(1)} %collective-permute-done.2.refs_0_), channel_id=1, source_target_pairs={{0,2},{1,3},{2,0},{3,1},{4,6},{5,7},{6,4},{7,5},{8,10},{9,11},{10,... | collective-permute-start | bytes 960008 | tf_op jit(solution)/shard_map/ppermute | solution.py:330
  30.0 11.2 %collective-permute-start.26 = (bf16[1,200,800]{2,1,0:T(8,128)(2,1)S(1)}, bf16[1,200,800]{2,1,0:T(8,128)(2,1)}, u32[]{:S(2)}, u32[]{:S(2)}) collective-permute-start(bf16[1,200,800]{2,1,0:T(8,128)(2,1)S(1)} %collective-permute-done.25.refs_2_), channel_id=1, source_target_pairs={{0,16},{16,0},{1,17},{17,1},{2,18},{18,2},{3,19},{19,3},{4,20},{20... | collective-permute-start | bytes 960008 | tf_op jit(solution)/shard_map/ppermute | solution.py:332
  36.5 8.3 %collective-permute-start.28 = (bf16[1,200,800]{2,1,0:T(8,128)(2,1)S(1)}, bf16[1,200,800]{2,1,0:T(8,128)(2,1)S(1)}, u32[]{:S(2)}, u32[]{:S(2)}) collective-permute-start(bf16[1,200,800]{2,1,0:T(8,128)(2,1)S(1)} %collective-permute-done.2.refs_0_), channel_id=1, source_target_pairs={{0,1},{1,0},{2,3},{3,2},{4,5},{5,4},{6,7},{7,6},{8,9},{9,8},{10,11... | collective-permute-start | bytes 960008 | tf_op jit(solution)/shard_map/ppermute | solution.py:331
  37.2 10.0 %collective-permute-start.29 = (bf16[1,200,800]{2,1,0:T(8,128)(2,1)S(1)}, bf16[1,200,800]{2,1,0:T(8,128)(2,1)S(1)}, u32[]{:S(2)}, u32[]{:S(2)}) collective-permute-start(bf16[1,200,800]{2,1,0:T(8,128)(2,1)S(1)} %collective-permute-done.25.refs_2_), channel_id=1, source_target_pairs={{0,1},{1,0},{2,3},{3,2},{4,5},{5,4},{6,7},{7,6},{8,9},{9,8},{10,11... | collective-permute-start | bytes 960008 | tf_op jit(solution)/shard_map/ppermute | solution.py:331
  39.1 11.5 %collective-permute-start.4 = (bf16[1,200,800]{2,1,0:T(8,128)(2,1)}, bf16[1,200,800]{2,1,0:T(8,128)(2,1)}, u32[]{:S(2)}, u32[]{:S(2)}) collective-permute-start(bf16[1,200,800]{2,1,0:T(8,128)(2,1)} %collective-permute-done.3.refs_0_), channel_id=1, source_target_pairs={{0,16},{16,0},{1,17},{17,1},{2,18},{18,2},{3,19},{19,3},{4,20},{20... | collective-permute-start | bytes 960008 | tf_op jit(solution)/shard_map/ppermute | solution.py:332
  41.2 12.8 %collective-permute-start.9 = (bf16[1,200,800]{2,1,0:T(8,128)(2,1)}, bf16[1,200,800]{2,1,0:T(8,128)(2,1)}, u32[]{:S(2)}, u32[]{:S(2)}) collective-permute-start(bf16[1,200,800]{2,1,0:T(8,128)(2,1)} %collective-permute-done.3.refs_0_), channel_id=1, source_target_pairs={{0,4},{1,5},{2,6},{3,7},{4,8},{5,9},{6,10},{7,11},{8,12},{9,13},{1... | collective-permute-start | bytes 960008 | tf_op jit(solution)/shard_map/ppermute | solution.py:329
  45.5 9.1 %collective-permute-start.18 = (bf16[1,200,800]{2,1,0:T(8,128)(2,1)}, bf16[1,200,800]{2,1,0:T(8,128)(2,1)S(1)}, u32[]{:S(2)}, u32[]{:S(2)}) collective-permute-start(bf16[1,200,800]{2,1,0:T(8,128)(2,1)} %collective-permute-done.3.refs_0_), channel_id=1, source_target_pairs={{0,2},{1,3},{2,0},{3,1},{4,6},{5,7},{6,4},{7,5},{8,10},{9,11},{10,... | collective-permute-start | bytes 960008 | tf_op jit(solution)/shard_map/ppermute | solution.py:330
  48.0 9.6 %collective-permute-start.21 = (bf16[1,200,800]{2,1,0:T(8,128)(2,1)}, bf16[1,200,800]{2,1,0:T(8,128)(2,1)S(1)}, u32[]{:S(2)}, u32[]{:S(2)}) collective-permute-start(bf16[1,200,800]{2,1,0:T(8,128)(2,1)} %collective-permute-done.20.refs_2_), channel_id=1, source_target_pairs={{0,16},{16,0},{1,17},{17,1},{2,18},{18,2},{3,19},{19,3},{4,20},{20... | collective-permute-start | bytes 960008 | tf_op jit(solution)/shard_map/ppermute | solution.py:332
  48.5 27.0 %collective-permute-start.23 = (bf16[1,200,800]{2,1,0:T(8,128)(2,1)}, bf16[1,200,800]{2,1,0:T(8,128)(2,1)}, u32[]{:S(2)}, u32[]{:S(2)}) collective-permute-start(bf16[1,200,800]{2,1,0:T(8,128)(2,1)} %collective-permute-done.3.refs_0_), channel_id=1, source_target_pairs={{0,1},{1,0},{2,3},{3,2},{4,5},{5,4},{6,7},{7,6},{8,9},{9,8},{10,11... | collective-permute-start | bytes 960008 | tf_op jit(solution)/shard_map/ppermute | solution.py:331
  50.6 25.0 %collective-permute-start.24 = (bf16[1,200,800]{2,1,0:T(8,128)(2,1)}, bf16[1,200,800]{2,1,0:T(8,128)(2,1)}, u32[]{:S(2)}, u32[]{:S(2)}) collective-permute-start(bf16[1,200,800]{2,1,0:T(8,128)(2,1)} %collective-permute-done.20.refs_2_), channel_id=1, source_target_pairs={{0,1},{1,0},{2,3},{3,2},{4,5},{5,4},{6,7},{7,6},{8,9},{9,8},{10,11... | collective-permute-start | bytes 960008 | tf_op jit(solution)/shard_map/ppermute | solution.py:331
  54.1 31.3 %collective-permute-start.27 = (bf16[1,200,800]{2,1,0:T(8,128)(2,1)}, bf16[1,200,800]{2,1,0:T(8,128)(2,1)}, u32[]{:S(2)}, u32[]{:S(2)}) collective-permute-start(bf16[1,200,800]{2,1,0:T(8,128)(2,1)} %collective-permute-done.26.refs_4_), channel_id=1, source_target_pairs={{0,1},{1,0},{2,3},{3,2},{4,5},{5,4},{6,7},{7,6},{8,9},{9,8},{10,11... | collective-permute-start | bytes 960008 | tf_op jit(solution)/shard_map/ppermute | solution.py:331
  54.7 31.3 %collective-permute-start.5 = (bf16[1,200,800]{2,1,0:T(8,128)(2,1)}, bf16[1,200,800]{2,1,0:T(8,128)(2,1)}, u32[]{:S(2)}, u32[]{:S(2)}) collective-permute-start(bf16[1,200,800]{2,1,0:T(8,128)(2,1)} %collective-permute-done.4.refs_4_), channel_id=1, source_target_pairs={{0,4},{1,5},{2,6},{3,7},{4,8},{5,9},{6,10},{7,11},{8,12},{9,13},{1... | collective-permute-start | bytes 960008 | tf_op jit(solution)/shard_map/ppermute | solution.py:329
  58.3 27.7 %collective-permute-start.10 = (bf16[1,200,800]{2,1,0:T(8,128)(2,1)}, bf16[1,200,800]{2,1,0:T(8,128)(2,1)}, u32[]{:S(2)}, u32[]{:S(2)}) collective-permute-start(bf16[1,200,800]{2,1,0:T(8,128)(2,1)} %collective-permute-done.9.refs_0_), channel_id=1, source_target_pairs={{0,2},{1,3},{2,0},{3,1},{4,6},{5,7},{6,4},{7,5},{8,10},{9,11},{10,... | collective-permute-start | bytes 960008 | tf_op jit(solution)/shard_map/ppermute | solution.py:330
  75.5 18.2 %collective-permute-start.7 = (bf16[1,200,800]{2,1,0:T(8,128)(2,1)}, bf16[1,200,800]{2,1,0:T(8,128)(2,1)S(1)}, u32[]{:S(2)}, u32[]{:S(2)}) collective-permute-start(bf16[1,200,800]{2,1,0:T(8,128)(2,1)} %collective-permute-done.4.refs_4_), channel_id=1, source_target_pairs={{0,2},{1,3},{2,0},{3,1},{4,6},{5,7},{6,4},{7,5},{8,10},{9,11},{10,... | collective-permute-start | bytes 960008 | tf_op jit(solution)/shard_map/ppermute | solution.py:330
  75.6 18.3 %collective-permute-start.17 = (bf16[1,200,800]{2,1,0:T(8,128)(2,1)}, bf16[1,200,800]{2,1,0:T(8,128)(2,1)S(1)}, u32[]{:S(2)}, u32[]{:S(2)}) collective-permute-start(bf16[1,200,800]{2,1,0:T(8,128)(2,1)} %collective-permute-done.9.refs_0_), channel_id=1, source_target_pairs={{0,1},{1,0},{2,3},{3,2},{4,5},{5,4},{6,7},{7,6},{8,9},{9,8},{10,11... | collective-permute-start | bytes 960008 | tf_op jit(solution)/shard_map/ppermute | solution.py:331
  85.4 14.1 %collective-permute-start.19 = (bf16[1,200,800]{2,1,0:T(8,128)(2,1)S(1)}, bf16[1,200,800]{2,1,0:T(8,128)(2,1)S(1)}, u32[]{:S(2)}, u32[]{:S(2)}) collective-permute-start(bf16[1,200,800]{2,1,0:T(8,128)(2,1)S(1)} %copy-done.6), channel_id=1, source_target_pairs={{0,1},{1,0},{2,3},{3,2},{4,5},{5,4},{6,7},{7,6},{8,9},{9,8},{10,11... | collective-permute-start | bytes 960008 | tf_op jit(solution)/shard_map/ppermute | solution.py:331
  86.0 13.8 %collective-permute-start.22 = (bf16[1,200,800]{2,1,0:T(8,128)(2,1)S(1)}, bf16[1,200,800]{2,1,0:T(8,128)(2,1)S(1)}, u32[]{:S(2)}, u32[]{:S(2)}) collective-permute-start(bf16[1,200,800]{2,1,0:T(8,128)(2,1)S(1)} %copy-done.8), channel_id=1, source_target_pairs={{0,1},{1,0},{2,3},{3,2},{4,5},{5,4},{6,7},{7,6},{8,9},{9,8},{10,11... | collective-permute-start | bytes 960008 | tf_op jit(solution)/shard_map/ppermute | solution.py:331
  86.0 14.1 %collective-permute-start.11 = (bf16[1,200,800]{2,1,0:T(8,128)(2,1)}, bf16[1,200,800]{2,1,0:T(8,128)(2,1)S(1)}, u32[]{:S(2)}, u32[]{:S(2)}) collective-permute-start(bf16[1,200,800]{2,1,0:T(8,128)(2,1)} %collective-permute-done.10.refs_2_), channel_id=1, source_target_pairs={{0,16},{16,0},{1,17},{17,1},{2,18},{18,2},{3,19},{19,3},{4,20},{20... | collective-permute-start | bytes 960008 | tf_op jit(solution)/shard_map/ppermute | solution.py:332
  93.7 11.4 %collective-permute-start.16 = (bf16[1,200,800]{2,1,0:T(8,128)(2,1)}, bf16[1,200,800]{2,1,0:T(8,128)(2,1)S(1)}, u32[]{:S(2)}, u32[]{:S(2)}) collective-permute-start(bf16[1,200,800]{2,1,0:T(8,128)(2,1)} %collective-permute-done.4.refs_4_), channel_id=1, source_target_pairs={{0,1},{1,0},{2,3},{3,2},{4,5},{5,4},{6,7},{7,6},{8,9},{9,8},{10,11... | collective-permute-start | bytes 960008 | tf_op jit(solution)/shard_map/ppermute | solution.py:331
  93.9 11.2 %collective-permute-start.15 = (bf16[1,200,800]{2,1,0:T(8,128)(2,1)}, bf16[1,200,800]{2,1,0:T(8,128)(2,1)S(1)}, u32[]{:S(2)}, u32[]{:S(2)}) collective-permute-start(bf16[1,200,800]{2,1,0:T(8,128)(2,1)} %collective-permute-done.10.refs_2_), channel_id=1, source_target_pairs={{0,1},{1,0},{2,3},{3,2},{4,5},{5,4},{6,7},{7,6},{8,9},{9,8},{10,11... | collective-permute-start | bytes 960008 | tf_op jit(solution)/shard_map/ppermute | solution.py:331
  99.5 10.8 %collective-permute-start.6 = (bf16[1,200,800]{2,1,0:T(8,128)(2,1)}, bf16[1,200,800]{2,1,0:T(8,128)(2,1)S(1)}, u32[]{:S(2)}, u32[]{:S(2)}) collective-permute-start(bf16[1,200,800]{2,1,0:T(8,128)(2,1)} %collective-permute-done.5.refs_0_), channel_id=1, source_target_pairs={{0,1},{1,0},{2,3},{3,2},{4,5},{5,4},{6,7},{7,6},{8,9},{9,8},{10,11... | collective-permute-start | bytes 960008 | tf_op jit(solution)/shard_map/ppermute | solution.py:331
  99.7 10.6 %collective-permute-start.8 = (bf16[1,200,800]{2,1,0:T(8,128)(2,1)S(1)}, bf16[1,200,800]{2,1,0:T(8,128)(2,1)S(1)}, u32[]{:S(2)}, u32[]{:S(2)}) collective-permute-start(bf16[1,200,800]{2,1,0:T(8,128)(2,1)S(1)} %collective-permute-done.7.refs_2_), channel_id=1, source_target_pairs={{0,1},{1,0},{2,3},{3,2},{4,5},{5,4},{6,7},{7,6},{8,9},{9,8},{10,11... | collective-permute-start | bytes 960008 | tf_op jit(solution)/shard_map/ppermute | solution.py:331
  100.1 10.2 %collective-permute-start.12 = (bf16[1,200,800]{2,1,0:T(8,128)(2,1)S(1)}, bf16[1,200,800]{2,1,0:T(8,128)(2,1)S(1)}, u32[]{:S(2)}, u32[]{:S(2)}) collective-permute-start(bf16[1,200,800]{2,1,0:T(8,128)(2,1)S(1)} %collective-permute-done.11.refs_4_), channel_id=1, source_target_pairs={{0,1},{1,0},{2,3},{3,2},{4,5},{5,4},{6,7},{7,6},{8,9},{9,8},{10,11... | collective-permute-start | bytes 960008 | tf_op jit(solution)/shard_map/ppermute | solution.py:331
  (19 other events, 147.4 us)

commit v3 on v2

--- a/solution.py
+++ b/solution.py
@@ -154,15 +154,19 @@
         out_ref[s * depths + depth, row] = jnp.where(inside, moved, 0.0).astype(jnp.bfloat16)
 
 
-def own_rows_kernel(volume_ref, out_ref):
-    depths, rows, _, _ = volume_ref.shape
-
-    def step(n, carry):
-        d, r = n // rows, n % rows
-        put_shifted(out_ref, d, r + REACH, volume_ref[d, r])
-        return carry
-
-    lax.fori_loop(0, depths * rows, step, 0)
+def own_rows_kernel(volume_ref, out_ref, held, sems):
+    depths, rows, _, _ = held.shape
+    fetch = [pltpu.make_async_copy(volume_ref.at[d], held.at[d], sems.at[d]) for d in range(depths)]
+    for copy in fetch:
+        copy.start()
+    for d, copy in enumerate(fetch):
+        copy.wait()
+
+        def step(r, carry, d=d):
+            put_shifted(out_ref, d, r + REACH, held[d, r])
+            return carry
+
+        lax.fori_loop(0, rows, step, 0)
 
 
 def edge_rows_kernel(above_ref, below_ref, old_ref, out_ref):
@@ -180,15 +184,16 @@
 
 def own_rows(volume):
     depths, rows, columns, pixels = volume.shape
+    shape = (SHIFTS * depths, rows + 2 * REACH, columns, pixels)
     return pl.pallas_call(
         own_rows_kernel,
-        in_specs=[IN_VMEM],
+        in_specs=[pl.BlockSpec(memory_space=pltpu.HBM)],
+        scratch_shapes=[pltpu.VMEM(volume.shape, volume.dtype), pltpu.SemaphoreType.DMA((depths,))],
         out_specs=IN_VMEM,
-        out_shape=pltpu.VMEM((SHIFTS * depths, rows + 2 * REACH, columns, pixels), jnp.bfloat16),
+        out_shape=pltpu.VMEM(shape, volume.dtype),
         compiler_params=pltpu.CompilerParams(vmem_limit_bytes=SMALL),
-        cost_estimate=pl.CostEstimate(flops=0, bytes_accessed=10 * 1024 * 1024, transcendentals=0),
         name="own_rows",
-    )(volume)
+    )(pltpu.with_memory_space_constraint(volume, pltpu.HBM))
 
 
 def edge_rows(above, below, copies):
@@ -336,27 +341,34 @@
     own_b = lax.dynamic_index_in_dim(own, 1 - side, 0)
     both = lambda *pieces: [w for piece in pieces for w in (piece, to_core(piece))]
 
+    tied = lax.optimization_barrier
+    a, b = 0, 1
     t1a, y0a = along_z(own_a), along_y(own_a)
     above = passed_along(volume[:, rows - REACH :], "lenslet", 1)
     below = passed_along(volume[:, :REACH], "lenslet", -1)
     own_c = to_core(own)
+    volume, scalars, own_b = tied((volume, scalars, own_b))
     copies = own_rows(volume)
+    t1a, y0a, above, below, own_c, copies = tied((t1a, y0a, above, below, own_c, copies))
     t2a, y1a, y0b = along_z(t1a), along_y(t1a), along_x(y0a)
     r0 = both(t1a, y0a)
     copies = edge_rows(above, below, copies)
-    a, b = 0, 1
     acc = add_pieces(scalars, copies, [own, own_c, own, own_c], [(0, 0, None), (0, 0, None)], None)
+    acc = add_pieces(scalars, copies, r0, [(1, 0, a), (0, 1, a)], acc)
+    t2a, y1a, y0b, acc = tied((t2a, y1a, y0b, acc))
     t3a, y2a, y1b = along_z(t2a), along_y(t2a), along_x(y1a)
     r1 = both(t2a, y1a, y0b)
-    acc = add_pieces(scalars, copies, r0, [(1, 0, a), (0, 1, a)], acc)
+    acc = add_pieces(scalars, copies, r1, [(2, 0, a), (1, 1, a), (0, 1, b)], acc)
+    t3a, y2a, y1b, acc = tied((t3a, y2a, y1b, acc))
     t1b, y3a, t2b = along_z(own_b), along_y(t3a), along_x(t2a)
     r2 = both(t3a, y2a, y1b)
-    acc = add_pieces(scalars, copies, r1, [(2, 0, a), (1, 1, a), (0, 1, b)], acc)
+    acc = add_pieces(scalars, copies, r2, [(3, 0, a), (2, 1, a), (1, 1, b)], acc)
+    t1b, y3a, t2b, acc = tied((t1b, y3a, t2b, acc))
     t3b, y2b, y3b = along_z(t2b), along_y(t2b), along_x(y3a)
     r3 = both(t1b, y3a, t2b)
-    acc = add_pieces(scalars, copies, r2, [(3, 0, a), (2, 1, a), (1, 1, b)], acc)
+    acc = add_pieces(scalars, copies, r3, [(1, 0, b), (3, 1, a), (2, 0, b)], acc)
+    t3b, y2b, y3b, acc = tied((t3b, y2b, y3b, acc))
     r4 = both(t3b, y2b, y3b)
-    acc = add_pieces(scalars, copies, r3, [(1, 0, b), (3, 1, a), (2, 0, b)], acc)
     final = (measured, dark_level.reshape(1, pixels))
     return tuple(add_pieces(scalars, copies, r4, [(3, 0, b), (2, 1, b), (3, 1, b)], acc, final))
 

time: 118 us -> 96.6 us (0.82)
  local copies, waits for them, and re-layouts: 25.7 us -> 3.45 us
  waiting for transfers between devices: 25.9 us -> 35.6 us
  starting transfers between devices: 31.5 us -> 25.4 us
  Pallas kernels: 33 us -> 30.8 us
    unnamed x41 -> x13, local copies, waits for them, and re-layouts: 23.1 us -> 0.12 us
    ppermute x5, starting transfers between devices: 9.09 us -> 3.21 us  [exchanged(): along_z = lambda v: lax.ppermute(v, 'lenslet', up)]
    ppermute x5, waiting for transfers between devices: 1.24 us -> 6.8 us  [exchanged(): along_y = lambda v: lax.ppermute(v, 'lenslet', beside)]
    ppermute x15, waiting for transfers between devices: 0.04 us -> 3.68 us  [exchanged(): to_core = lambda v: lax.ppermute(v, 'lenslet', twin)]
    ppermute x4, waiting for transfers between devices: 4.96 us -> 7.96 us  [exchanged(): along_x = lambda v: lax.ppermute(v, 'frames', [(0, 1), (1, 0)])]
    pallas_call x6, Pallas kernels: 28.2 us -> 25.4 us  [add_pieces(): pl.pallas_call(functools.partial(add_kernel, plan=plan, pieces=pieces, fi...]
    ppermute x5, waiting for transfers between devices: 19.7 us -> 17.2 us  [exchanged(): along_z = lambda v: lax.ppermute(v, 'lenslet', up)]
    ppermute x2, starting transfers between devices: 2.73 us -> 4.34 us  [passed_along(): return lax.ppermute(block, axis, route)]
  transfers between devices with their start and end apart: 31 -> 31, of which waited for: 9 -> 18; matrix products, arithmetic and copies ran while one was open for 1% -> 4% of each run, Pallas kernels for 22% -> 25%
where the time goes in v3:
time: 96.6 us; the launch traced here: 96.4 us
  waiting for transfers between devices  35.6 us (37%)
  Pallas kernels  30.8 us (32%)
  starting transfers between devices  25.4 us (26%)
  local copies, waits for them, and re-layouts  3.45 us (4%)
  between operations  1.01 us (1%)
    pallas_call x6, Pallas kernels, add_pieces(): pl.pallas_call(functools.partial(add_kernel, plan=plan, pieces=pieces, fi...  25.4 us
    ppermute x5, waiting for transfers between devices, exchanged(): along_z = lambda v: lax.ppermute(v, 'lenslet', up)  17.2 us
    ppermute x5, starting transfers between devices, exchanged(): along_y = lambda v: lax.ppermute(v, 'lenslet', beside)  8.29 us
    ppermute x4, waiting for transfers between devices, exchanged(): along_x = lambda v: lax.ppermute(v, 'frames', [(0, 1), (1, 0)])  7.96 us
    ppermute x5, waiting for transfers between devices, exchanged(): along_y = lambda v: lax.ppermute(v, 'lenslet', beside)  6.8 us
    ppermute x15, starting transfers between devices, exchanged(): to_core = lambda v: lax.ppermute(v, 'lenslet', twin)  5.54 us
    pallas_call x1, Pallas kernels, own_rows(): pl.pallas_call(own_rows_kernel, in_specs=[pl.BlockSpec(memory_space=pltpu...  4.58 us
    ppermute x2, starting transfers between devices, passed_along(): return lax.ppermute(block, axis, route)  4.34 us
  transfers between devices with their start and end apart: 31, of which 18 were waited for; matrix products, arithmetic and copies ran while one was open for 4% of the time, Pallas kernels for 25%

profile of v3, /device:TPU:0, one launch (start us, length us, event | category | flops | bytes accessed | tf_op | source)
XLA Modules:
  0.0 96.4 jit_solution(149432859926479209)
XLA Ops:
  1.2 2.3 %fusion = (bf16[4,2,64,400]{3,2,1,0:T(8,128)(2,1)}, bf16[4,2,64,400]{3,2,1,0:T(8,128)(2,1)}) fusion(bf16[4,16,64,400]{3,2,1,0:T(8,128)(2,1)} %volume_ref), kind=kLoop, calls=%fused_computation.3 | loop fusion | bytes 1638400 | tf_op jit(solution)/shard_map/slice | solution.py:348
  3.4 1.3 %collective-permute-start.3 = (bf16[4,2,64,400]{3,2,1,0:T(8,128)(2,1)}, bf16[4,2,64,400]{3,2,1,0:T(8,128)(2,1)S(1)}, u32[]{:S(2)}, u32[]{:S(2)}) collective-permute-start(bf16[4,2,64,400]{3,2,1,0:T(8,128)(2,1)} %get-tuple-element.52), channel_id=1, source_target_pairs={{1,0},{2,1},{3,2},{4,3},{5,4},{6,5},{7,6},{8,7},{9,8},{10,9},{11,1... | collective-permute-start | bytes 1228808 | tf_op jit(solution)/shard_map/ppermute | solution.py:20
  4.7 3.1 %collective-permute-start.2 = (bf16[4,2,64,400]{3,2,1,0:T(8,128)(2,1)}, bf16[4,2,64,400]{3,2,1,0:T(8,128)(2,1)S(1)}, u32[]{:S(2)}, u32[]{:S(2)}) collective-permute-start(bf16[4,2,64,400]{3,2,1,0:T(8,128)(2,1)} %get-tuple-element.53), channel_id=1, source_target_pairs={{0,1},{1,2},{2,3},{3,4},{4,5},{5,6},{6,7},{7,8},{8,9},{9,10},{10,1... | collective-permute-start | bytes 1228808 | tf_op jit(solution)/shard_map/ppermute | solution.py:20
  7.8 1.0 %constant_dynamic-slice_fusion = (bf16[1,200,800]{2,1,0:T(8,128)(2,1)}, bf16[1,200,800]{2,1,0:T(8,128)(2,1)}) fusion(bf16[2,200,800]{2,1,0:T(8,128)(2,1)S(1)} %bitcast.7, s32[]{:T(128)S(6)} %select_n.8, s32[]{:T(128)S(6)} %select_n.7), kind=kLoop, calls=%fused_computation.1 | loop fusion | bytes 1280008 | tf_op jit(solution)/shard_map/jit(dynamic_index_in_dim)/dynamic_slice | solution.py:340
  8.8 2.6 %collective-permute-start.1 = (bf16[1,200,800]{2,1,0:T(8,128)(2,1)}, bf16[1,200,800]{2,1,0:T(8,128)(2,1)S(1)}, u32[]{:S(2)}, u32[]{:S(2)}) collective-permute-start(bf16[1,200,800]{2,1,0:T(8,128)(2,1)} %get-tuple-element.54), channel_id=1, source_target_pairs={{0,2},{1,3},{2,0},{3,1},{4,6},{5,7},{6,4},{7,5},{8,10},{9,11},{10,... | collective-permute-start | bytes 960008 | tf_op jit(solution)/shard_map/ppermute | solution.py:335
  11.3 1.6 %collective-permute-start = (bf16[1,200,800]{2,1,0:T(8,128)(2,1)}, bf16[1,200,800]{2,1,0:T(8,128)(2,1)S(1)}, u32[]{:S(2)}, u32[]{:S(2)}) collective-permute-start(bf16[1,200,800]{2,1,0:T(8,128)(2,1)} %get-tuple-element.54), channel_id=1, source_target_pairs={{0,4},{1,5},{2,6},{3,7},{4,8},{5,9},{6,10},{7,11},{8,12},{9,13},{1... | collective-permute-start | bytes 960008 | tf_op jit(solution)/shard_map/ppermute | solution.py:334
  13.3 4.6 %own_rows.1.old_ref = bf16[20,20,64,400]{3,2,1,0:T(8,128)(2,1)S(1)} custom-call(bf16[4,16,64,400]{3,2,1,0:T(8,128)(2,1)} %volume_ref), custom_call_target="tpu_custom_call" | custom-call | tf_op jit(solution)/shard_map/own_rows/pallas_call | solution.py:188
  17.8 5.8 %collective-permute-done.1.refs_2_ = bf16[1,200,800]{2,1,0:T(8,128)(2,1)S(1)} collective-permute-done((bf16[1,200,800]{2,1,0:T(8,128)(2,1)}, bf16[1,200,800]{2,1,0:T(8,128)(2,1)S(1)}, u32[]{:S(2)}, u32[]{:S(2)}) %collective-permute-start.1) | collective-permute-done | bytes 320032 | tf_op jit(solution)/shard_map/ppermute | solution.py:335
  23.6 2.9 %collective-permute-done.refs_0_ = bf16[1,200,800]{2,1,0:T(8,128)(2,1)S(1)} collective-permute-done((bf16[1,200,800]{2,1,0:T(8,128)(2,1)}, bf16[1,200,800]{2,1,0:T(8,128)(2,1)S(1)}, u32[]{:S(2)}, u32[]{:S(2)}) %collective-permute-start) | collective-permute-done | bytes 320032 | tf_op jit(solution)/shard_map/ppermute | solution.py:334
  26.5 2.8 %collective-permute-start.10 = (bf16[1,200,800]{2,1,0:T(8,128)(2,1)S(1)}, bf16[1,200,800]{2,1,0:T(8,128)(2,1)S(1)}, u32[]{:S(2)}, u32[]{:S(2)}) collective-permute-start(bf16[1,200,800]{2,1,0:T(8,128)(2,1)S(1)} %collective-permute-done.1.refs_2_), channel_id=1, source_target_pairs={{0,1},{1,0},{2,3},{3,2},{4,5},{5,4},{6,7},{7,6},{8,9},{9,8},{10,11... | collective-permute-start | bytes 960008 | tf_op jit(solution)/shard_map/ppermute | solution.py:336
  29.4 1.5 %collective-permute-start.8 = (bf16[1,200,800]{2,1,0:T(8,128)(2,1)S(1)}, bf16[1,200,800]{2,1,0:T(8,128)(2,1)S(1)}, u32[]{:S(2)}, u32[]{:S(2)}) collective-permute-start(bf16[1,200,800]{2,1,0:T(8,128)(2,1)S(1)} %collective-permute-done.1.refs_2_), channel_id=1, source_target_pairs={{0,16},{16,0},{1,17},{17,1},{2,18},{18,2},{3,19},{19,3},{4,20},{20... | collective-permute-start | bytes 960008 | tf_op jit(solution)/shard_map/ppermute | solution.py:337
  30.9 2.1 %collective-permute-start.7 = (bf16[1,200,800]{2,1,0:T(8,128)(2,1)S(1)}, bf16[1,200,800]{2,1,0:T(8,128)(2,1)S(1)}, u32[]{:S(2)}, u32[]{:S(2)}) collective-permute-start(bf16[1,200,800]{2,1,0:T(8,128)(2,1)S(1)} %collective-permute-done.refs_0_), channel_id=1, source_target_pairs={{0,2},{1,3},{2,0},{3,1},{4,6},{5,7},{6,4},{7,5},{8,10},{9,11},{10,... | collective-permute-start | bytes 960008 | tf_op jit(solution)/shard_map/ppermute | solution.py:335
  33.0 1.6 %collective-permute-start.6 = (bf16[1,200,800]{2,1,0:T(8,128)(2,1)S(1)}, bf16[1,200,800]{2,1,0:T(8,128)(2,1)S(1)}, u32[]{:S(2)}, u32[]{:S(2)}) collective-permute-start(bf16[1,200,800]{2,1,0:T(8,128)(2,1)S(1)} %collective-permute-done.refs_0_), channel_id=1, source_target_pairs={{0,4},{1,5},{2,6},{3,7},{4,8},{5,9},{6,10},{7,11},{8,12},{9,13},{1... | collective-permute-start | bytes 960008 | tf_op jit(solution)/shard_map/ppermute | solution.py:334
  34.6 0.9 edge_rows.1.copies
  35.5 3.0 %add_pieces.6.refs_4_ = f32[2,1024,200]{2,1,0:T(8,128)S(1)} custom-call(s32[70]{0:T(128)S(1)} %pad_add_fusion.scalars, bf16[20,20,64,400]{3,2,1,0:T(8,128)(2,1)S(1)} %edge_rows.1.copies, bf16[2,200,800]{2,1,0:T(8,128)(2,1)S(1)} %bitcast.8, bf16[2,200,800]{2,1,0:T(8,128)(2,1)S(1)} %collective-permute-done.4.refs_1_.refs_3_, bf16[2,200,800]{2,1,0:T(8,128)(2,1)S(1)} %bitcast.9, ...), custom_call_target="tpu_custom_call" | custom-call | flops 1310720000 | bytes 2097152 | tf_op jit(solution)/shard_map/add_pieces/pallas_call | solution.py:301
  38.5 3.1 %add_pieces.7.refs_6_ = f32[2,1024,200]{2,1,0:T(8,128)S(1)} custom-call(s32[70]{0:T(128)S(1)} %pad_add_fusion.scalars, bf16[20,20,64,400]{3,2,1,0:T(8,128)(2,1)S(1)} %edge_rows.1.copies, bf16[1,200,800]{2,1,0:T(8,128)(2,1)S(1)} %collective-permute-done.refs_0_, ...), custom_call_target="tpu_custom_call", output_to_operand_aliasing={{}: (6, {})} | custom-call | flops 1310720000 | bytes 2097152 | tf_op jit(solution)/shard_map/add_pieces/pallas_call | solution.py:301
  41.7 3.3 %collective-permute-done.6.refs_0_ = bf16[1,200,800]{2,1,0:T(8,128)(2,1)S(1)} collective-permute-done((bf16[1,200,800]{2,1,0:T(8,128)(2,1)S(1)}, bf16[1,200,800]{2,1,0:T(8,128)(2,1)S(1)}, u32[]{:S(2)}, u32[]{:S(2)}) %collective-permute-start.6) | collective-permute-done | bytes 320032 | tf_op jit(solution)/shard_map/ppermute | solution.py:334
  47.7 4.3 %add_pieces.8.refs_6_ = f32[2,1024,200]{2,1,0:T(8,128)S(1)} custom-call(s32[70]{0:T(128)S(1)} %pad_add_fusion.scalars, bf16[20,20,64,400]{3,2,1,0:T(8,128)(2,1)S(1)} %edge_rows.1.copies, bf16[1,200,800]{2,1,0:T(8,128)(2,1)S(1)} %collective-permute-done.6.refs_0_, ...), custom_call_target="tpu_custom_call", output_to_operand_aliasing={{}: (8, {})} | custom-call | flops 1966080000 | bytes 3145728 | tf_op jit(solution)/shard_map/add_pieces/pallas_call | solution.py:301
  52.0 4.3 %collective-permute-done.13.refs_4_ = bf16[1,200,800]{2,1,0:T(8,128)(2,1)S(1)} collective-permute-done((bf16[1,200,800]{2,1,0:T(8,128)(2,1)S(1)}, bf16[1,200,800]{2,1,0:T(8,128)(2,1)S(1)}, u32[]{:S(2)}, u32[]{:S(2)}) %collective-permute-start.13) | collective-permute-done | bytes 320032 | tf_op jit(solution)/shard_map/ppermute | solution.py:337
  56.5 2.3 %collective-permute-done.11.refs_0_ = bf16[1,200,800]{2,1,0:T(8,128)(2,1)S(1)} collective-permute-done((bf16[1,200,800]{2,1,0:T(8,128)(2,1)S(1)}, bf16[1,200,800]{2,1,0:T(8,128)(2,1)S(1)}, u32[]{:S(2)}, u32[]{:S(2)}) %collective-permute-start.11) | collective-permute-done | bytes 320032 | tf_op jit(solution)/shard_map/ppermute | solution.py:334
  59.4 1.0 %collective-permute-start.18 = (bf16[1,200,800]{2,1,0:T(8,128)(2,1)S(1)}, bf16[1,200,800]{2,1,0:T(8,128)(2,1)S(1)}, u32[]{:S(2)}, u32[]{:S(2)}) collective-permute-start(bf16[1,200,800]{2,1,0:T(8,128)(2,1)S(1)} %collective-permute-done.6.refs_0_), channel_id=1, source_target_pairs={{0,16},{16,0},{1,17},{17,1},{2,18},{18,2},{3,19},{19,3},{4,20},{20... | collective-permute-start | bytes 960008 | tf_op jit(solution)/shard_map/ppermute | solution.py:337
  60.5 1.6 %collective-permute-start.17 = (bf16[1,200,800]{2,1,0:T(8,128)(2,1)S(1)}, bf16[1,200,800]{2,1,0:T(8,128)(2,1)S(1)}, u32[]{:S(2)}, u32[]{:S(2)}) collective-permute-start(bf16[1,200,800]{2,1,0:T(8,128)(2,1)S(1)} %collective-permute-done.11.refs_0_), channel_id=1, source_target_pairs={{0,2},{1,3},{2,0},{3,1},{4,6},{5,7},{6,4},{7,5},{8,10},{9,11},{10,... | collective-permute-start | bytes 960008 | tf_op jit(solution)/shard_map/ppermute | solution.py:335
  62.2 4.3 %add_pieces.9.refs_6_ = f32[2,1024,200]{2,1,0:T(8,128)S(1)} custom-call(s32[70]{0:T(128)S(1)} %pad_add_fusion.scalars, bf16[20,20,64,400]{3,2,1,0:T(8,128)(2,1)S(1)} %edge_rows.1.copies, bf16[1,200,800]{2,1,0:T(8,128)(2,1)S(1)} %collective-permute-done.11.refs_0_, ...), custom_call_target="tpu_custom_call", output_to_operand_aliasing={{}: (8, {})} | custom-call | flops 1966080000 | bytes 3145728 | tf_op jit(solution)/shard_map/add_pieces/pallas_call | solution.py:301
  66.5 5.4 %collective-permute-done.5.refs_0_ = bf16[1,200,800]{2,1,0:T(8,128)(2,1)S(1)} collective-permute-done((bf16[1,200,800]{2,1,0:T(8,128)(2,1)S(1)}, bf16[1,200,800]{2,1,0:T(8,128)(2,1)S(1)}, u32[]{:S(2)}, u32[]{:S(2)}) %collective-permute-start.5) | collective-permute-done | bytes 320032 | tf_op jit(solution)/shard_map/ppermute | solution.py:334
  72.5 1.0 %collective-permute-start.24 = (bf16[1,200,800]{2,1,0:T(8,128)(2,1)S(1)}, bf16[1,200,800]{2,1,0:T(8,128)(2,1)S(1)}, u32[]{:S(2)}, u32[]{:S(2)}) collective-permute-start(bf16[1,200,800]{2,1,0:T(8,128)(2,1)S(1)} %collective-permute-done.17.refs_2_), channel_id=1, source_target_pairs={{0,16},{16,0},{1,17},{17,1},{2,18},{18,2},{3,19},{19,3},{4,20},{20... | collective-permute-start | bytes 960008 | tf_op jit(solution)/shard_map/ppermute | solution.py:337
  73.5 1.7 %collective-permute-start.23 = (bf16[1,200,800]{2,1,0:T(8,128)(2,1)S(1)}, bf16[1,200,800]{2,1,0:T(8,128)(2,1)S(1)}, u32[]{:S(2)}, u32[]{:S(2)}) collective-permute-start(bf16[1,200,800]{2,1,0:T(8,128)(2,1)S(1)} %collective-permute-done.18.refs_4_), channel_id=1, source_target_pairs={{0,2},{1,3},{2,0},{3,1},{4,6},{5,7},{6,4},{7,5},{8,10},{9,11},{10,... | collective-permute-start | bytes 960008 | tf_op jit(solution)/shard_map/ppermute | solution.py:335
  75.3 4.3 %add_pieces.10.refs_8_ = f32[2,1024,200]{2,1,0:T(8,128)S(1)} custom-call(s32[70]{0:T(128)S(1)} %pad_add_fusion.scalars, bf16[20,20,64,400]{3,2,1,0:T(8,128)(2,1)S(1)} %edge_rows.1.copies, bf16[1,200,800]{2,1,0:T(8,128)(2,1)S(1)} %collective-permute-done.5.refs_0_, ...), custom_call_target="tpu_custom_call", output_to_operand_aliasing={{}: (8, {})} | custom-call | flops 1966080000 | bytes 3145728 | tf_op jit(solution)/shard_map/add_pieces/pallas_call | solution.py:301
  79.6 3.7 %collective-permute-done.24.refs_4_ = bf16[1,200,800]{2,1,0:T(8,128)(2,1)S(1)} collective-permute-done((bf16[1,200,800]{2,1,0:T(8,128)(2,1)S(1)}, bf16[1,200,800]{2,1,0:T(8,128)(2,1)S(1)}, u32[]{:S(2)}, u32[]{:S(2)}) %collective-permute-start.24) | collective-permute-done | bytes 320032 | tf_op jit(solution)/shard_map/ppermute | solution.py:337
  83.3 0.7 collective-permute-done.23.refs_2_
  83.9 3.3 %collective-permute-done.22.refs_0_ = bf16[1,200,800]{2,1,0:T(8,128)(2,1)S(1)} collective-permute-done((bf16[1,200,800]{2,1,0:T(8,128)(2,1)S(1)}, bf16[1,200,800]{2,1,0:T(8,128)(2,1)S(1)}, u32[]{:S(2)}, u32[]{:S(2)}) %collective-permute-start.22) | collective-permute-done | bytes 320032 | tf_op jit(solution)/shard_map/ppermute | solution.py:334
  87.7 1.2 %collective-permute-done.28.refs_1_ = bf16[1,200,800]{2,1,0:T(8,128)(2,1)S(1)} collective-permute-done((bf16[1,200,800]{2,1,0:T(8,128)(2,1)S(1)}, bf16[1,200,800]{2,1,0:T(8,128)(2,1)S(1)}, u32[]{:S(2)}, u32[]{:S(2)}) %collective-permute-start.28) | collective-permute-done | bytes 320032 | tf_op jit(solution)/shard_map/ppermute | solution.py:336
  89.9 6.3 %add_pieces.11 = (f32[16,64,400]{2,1,0:T(8,128)}, f32[16,64,400]{2,1,0:T(8,128)}) custom-call(s32[70]{0:T(128)S(1)} %pad_add_fusion.scalars, bf16[20,20,64,400]{3,2,1,0:T(8,128)(2,1)S(1)} %edge_rows.1.copies, bf16[1,200,800]{2,1,0:T(8,128)(2,1)S(1)} %collective-permute-done.22.refs_0_, bf16[1,200,800]{2,1,0:T(8,128)(2,1)S(1)} %collective-permute-done.28.refs_1_, ...), custom_call_target="tpu_custom_call" | custom-call | flops 1966080000 | bytes 3145728 | tf_op jit(solution)/shard_map/add_pieces/pallas_call | solution.py:301
  (55 shorter events, 6.7 us)
Async XLA Ops:
  0.7 25.9 %collective-permute-start.4 = (bf16[2,200,800]{2,1,0:T(8,128)(2,1)}, bf16[2,200,800]{2,1,0:T(8,128)(2,1)S(1)}, u32[]{:S(2)}, u32[]{:S(2)}) collective-permute-start(bf16[2,200,800]{2,1,0:T(8,128)(2,1)} %bitcast.6), channel_id=1, source_target_pairs={{0,1},{1,0},{2,3},{3,2},{4,5},{5,4},{6,7},{7,6},{8,9},{9,8},{10,11... | collective-permute-start | bytes 1920008 | tf_op jit(solution)/shard_map/ppermute | solution.py:336
  3.4 23.1 %collective-permute-start.3 = (bf16[4,2,64,400]{3,2,1,0:T(8,128)(2,1)}, bf16[4,2,64,400]{3,2,1,0:T(8,128)(2,1)S(1)}, u32[]{:S(2)}, u32[]{:S(2)}) collective-permute-start(bf16[4,2,64,400]{3,2,1,0:T(8,128)(2,1)} %get-tuple-element.52), channel_id=1, source_target_pairs={{1,0},{2,1},{3,2},{4,3},{5,4},{6,5},{7,6},{8,7},{9,8},{10,9},{11,1... | collective-permute-start | bytes 1228808 | tf_op jit(solution)/shard_map/ppermute | solution.py:20
  4.7 21.8 %collective-permute-start.2 = (bf16[4,2,64,400]{3,2,1,0:T(8,128)(2,1)}, bf16[4,2,64,400]{3,2,1,0:T(8,128)(2,1)S(1)}, u32[]{:S(2)}, u32[]{:S(2)}) collective-permute-start(bf16[4,2,64,400]{3,2,1,0:T(8,128)(2,1)} %get-tuple-element.53), channel_id=1, source_target_pairs={{0,1},{1,2},{2,3},{3,4},{4,5},{5,6},{6,7},{7,8},{8,9},{9,10},{10,1... | collective-permute-start | bytes 1228808 | tf_op jit(solution)/shard_map/ppermute | solution.py:20
  8.8 14.9 %collective-permute-start.1 = (bf16[1,200,800]{2,1,0:T(8,128)(2,1)}, bf16[1,200,800]{2,1,0:T(8,128)(2,1)S(1)}, u32[]{:S(2)}, u32[]{:S(2)}) collective-permute-start(bf16[1,200,800]{2,1,0:T(8,128)(2,1)} %get-tuple-element.54), channel_id=1, source_target_pairs={{0,2},{1,3},{2,0},{3,1},{4,6},{5,7},{6,4},{7,5},{8,10},{9,11},{10,... | collective-permute-start | bytes 960008 | tf_op jit(solution)/shard_map/ppermute | solution.py:335
  11.3 15.2 %collective-permute-start = (bf16[1,200,800]{2,1,0:T(8,128)(2,1)}, bf16[1,200,800]{2,1,0:T(8,128)(2,1)S(1)}, u32[]{:S(2)}, u32[]{:S(2)}) collective-permute-start(bf16[1,200,800]{2,1,0:T(8,128)(2,1)} %get-tuple-element.54), channel_id=1, source_target_pairs={{0,4},{1,5},{2,6},{3,7},{4,8},{5,9},{6,10},{7,11},{8,12},{9,13},{1... | collective-permute-start | bytes 960008 | tf_op jit(solution)/shard_map/ppermute | solution.py:334
  26.5 12.0 %collective-permute-start.10 = (bf16[1,200,800]{2,1,0:T(8,128)(2,1)S(1)}, bf16[1,200,800]{2,1,0:T(8,128)(2,1)S(1)}, u32[]{:S(2)}, u32[]{:S(2)}) collective-permute-start(bf16[1,200,800]{2,1,0:T(8,128)(2,1)S(1)} %collective-permute-done.1.refs_2_), channel_id=1, source_target_pairs={{0,1},{1,0},{2,3},{3,2},{4,5},{5,4},{6,7},{7,6},{8,9},{9,8},{10,11... | collective-permute-start | bytes 960008 | tf_op jit(solution)/shard_map/ppermute | solution.py:336
  29.4 9.1 %collective-permute-start.9 = (bf16[1,200,800]{2,1,0:T(8,128)(2,1)S(1)}, bf16[1,200,800]{2,1,0:T(8,128)(2,1)S(1)}, u32[]{:S(2)}, u32[]{:S(2)}) collective-permute-start(bf16[1,200,800]{2,1,0:T(8,128)(2,1)S(1)} %collective-permute-done.refs_0_), channel_id=1, source_target_pairs={{0,1},{1,0},{2,3},{3,2},{4,5},{5,4},{6,7},{7,6},{8,9},{9,8},{10,11... | collective-permute-start | bytes 960008 | tf_op jit(solution)/shard_map/ppermute | solution.py:336
  29.4 12.2 %collective-permute-start.8 = (bf16[1,200,800]{2,1,0:T(8,128)(2,1)S(1)}, bf16[1,200,800]{2,1,0:T(8,128)(2,1)S(1)}, u32[]{:S(2)}, u32[]{:S(2)}) collective-permute-start(bf16[1,200,800]{2,1,0:T(8,128)(2,1)S(1)} %collective-permute-done.1.refs_2_), channel_id=1, source_target_pairs={{0,16},{16,0},{1,17},{17,1},{2,18},{18,2},{3,19},{19,3},{4,20},{20... | collective-permute-start | bytes 960008 | tf_op jit(solution)/shard_map/ppermute | solution.py:337
  30.9 10.8 %collective-permute-start.7 = (bf16[1,200,800]{2,1,0:T(8,128)(2,1)S(1)}, bf16[1,200,800]{2,1,0:T(8,128)(2,1)S(1)}, u32[]{:S(2)}, u32[]{:S(2)}) collective-permute-start(bf16[1,200,800]{2,1,0:T(8,128)(2,1)S(1)} %collective-permute-done.refs_0_), channel_id=1, source_target_pairs={{0,2},{1,3},{2,0},{3,1},{4,6},{5,7},{6,4},{7,5},{8,10},{9,11},{10,... | collective-permute-start | bytes 960008 | tf_op jit(solution)/shard_map/ppermute | solution.py:335
  33.0 12.0 %collective-permute-start.6 = (bf16[1,200,800]{2,1,0:T(8,128)(2,1)S(1)}, bf16[1,200,800]{2,1,0:T(8,128)(2,1)S(1)}, u32[]{:S(2)}, u32[]{:S(2)}) collective-permute-start(bf16[1,200,800]{2,1,0:T(8,128)(2,1)S(1)} %collective-permute-done.refs_0_), channel_id=1, source_target_pairs={{0,4},{1,5},{2,6},{3,7},{4,8},{5,9},{6,10},{7,11},{8,12},{9,13},{1... | collective-permute-start | bytes 960008 | tf_op jit(solution)/shard_map/ppermute | solution.py:334
  45.0 1.7 %collective-permute-start.16 = (bf16[1,200,800]{2,1,0:T(8,128)(2,1)S(1)}, bf16[1,200,800]{2,1,0:T(8,128)(2,1)S(1)}, u32[]{:S(2)}, u32[]{:S(2)}) collective-permute-start(bf16[1,200,800]{2,1,0:T(8,128)(2,1)S(1)} %collective-permute-done.8.refs_4_), channel_id=1, source_target_pairs={{0,1},{1,0},{2,3},{3,2},{4,5},{5,4},{6,7},{7,6},{8,9},{9,8},{10,11... | collective-permute-start | bytes 960008 | tf_op jit(solution)/shard_map/ppermute | solution.py:336
  45.0 2.2 %collective-permute-start.15 = (bf16[1,200,800]{2,1,0:T(8,128)(2,1)S(1)}, bf16[1,200,800]{2,1,0:T(8,128)(2,1)S(1)}, u32[]{:S(2)}, u32[]{:S(2)}) collective-permute-start(bf16[1,200,800]{2,1,0:T(8,128)(2,1)S(1)} %collective-permute-done.7.refs_2_), channel_id=1, source_target_pairs={{0,1},{1,0},{2,3},{3,2},{4,5},{5,4},{6,7},{7,6},{8,9},{9,8},{10,11... | collective-permute-start | bytes 960008 | tf_op jit(solution)/shard_map/ppermute | solution.py:336
  45.5 2.2 %collective-permute-start.14 = (bf16[1,200,800]{2,1,0:T(8,128)(2,1)S(1)}, bf16[1,200,800]{2,1,0:T(8,128)(2,1)S(1)}, u32[]{:S(2)}, u32[]{:S(2)}) collective-permute-start(bf16[1,200,800]{2,1,0:T(8,128)(2,1)S(1)} %collective-permute-done.6.refs_0_), channel_id=1, source_target_pairs={{0,1},{1,0},{2,3},{3,2},{4,5},{5,4},{6,7},{7,6},{8,9},{9,8},{10,11... | collective-permute-start | bytes 960008 | tf_op jit(solution)/shard_map/ppermute | solution.py:336
  45.5 10.8 %collective-permute-start.13 = (bf16[1,200,800]{2,1,0:T(8,128)(2,1)S(1)}, bf16[1,200,800]{2,1,0:T(8,128)(2,1)S(1)}, u32[]{:S(2)}, u32[]{:S(2)}) collective-permute-start(bf16[1,200,800]{2,1,0:T(8,128)(2,1)S(1)} %collective-permute-done.7.refs_2_), channel_id=1, source_target_pairs={{0,16},{16,0},{1,17},{17,1},{2,18},{18,2},{3,19},{19,3},{4,20},{20... | collective-permute-start | bytes 960008 | tf_op jit(solution)/shard_map/ppermute | solution.py:337
  46.0 10.5 %collective-permute-start.12 = (bf16[1,200,800]{2,1,0:T(8,128)(2,1)S(1)}, bf16[1,200,800]{2,1,0:T(8,128)(2,1)S(1)}, u32[]{:S(2)}, u32[]{:S(2)}) collective-permute-start(bf16[1,200,800]{2,1,0:T(8,128)(2,1)S(1)} %collective-permute-done.6.refs_0_), channel_id=1, source_target_pairs={{0,2},{1,3},{2,0},{3,1},{4,6},{5,7},{6,4},{7,5},{8,10},{9,11},{10,... | collective-permute-start | bytes 960008 | tf_op jit(solution)/shard_map/ppermute | solution.py:335
  46.6 12.2 %collective-permute-start.11 = (bf16[1,200,800]{2,1,0:T(8,128)(2,1)S(1)}, bf16[1,200,800]{2,1,0:T(8,128)(2,1)S(1)}, u32[]{:S(2)}, u32[]{:S(2)}) collective-permute-start(bf16[1,200,800]{2,1,0:T(8,128)(2,1)S(1)} %collective-permute-done.6.refs_0_), channel_id=1, source_target_pairs={{0,4},{1,5},{2,6},{3,7},{4,8},{5,9},{6,10},{7,11},{8,12},{9,13},{1... | collective-permute-start | bytes 960008 | tf_op jit(solution)/shard_map/ppermute | solution.py:334
  58.9 1.7 %collective-permute-start.20 = (bf16[1,200,800]{2,1,0:T(8,128)(2,1)S(1)}, bf16[1,200,800]{2,1,0:T(8,128)(2,1)S(1)}, u32[]{:S(2)}, u32[]{:S(2)}) collective-permute-start(bf16[1,200,800]{2,1,0:T(8,128)(2,1)S(1)} %collective-permute-done.12.refs_2_), channel_id=1, source_target_pairs={{0,1},{1,0},{2,3},{3,2},{4,5},{5,4},{6,7},{7,6},{8,9},{9,8},{10,11... | collective-permute-start | bytes 960008 | tf_op jit(solution)/shard_map/ppermute | solution.py:336
  58.9 3.3 %collective-permute-start.21 = (bf16[1,200,800]{2,1,0:T(8,128)(2,1)S(1)}, bf16[1,200,800]{2,1,0:T(8,128)(2,1)S(1)}, u32[]{:S(2)}, u32[]{:S(2)}) collective-permute-start(bf16[1,200,800]{2,1,0:T(8,128)(2,1)S(1)} %collective-permute-done.13.refs_4_), channel_id=1, source_target_pairs={{0,1},{1,0},{2,3},{3,2},{4,5},{5,4},{6,7},{7,6},{8,9},{9,8},{10,11... | collective-permute-start | bytes 960008 | tf_op jit(solution)/shard_map/ppermute | solution.py:336
  59.4 2.8 %collective-permute-start.19 = (bf16[1,200,800]{2,1,0:T(8,128)(2,1)S(1)}, bf16[1,200,800]{2,1,0:T(8,128)(2,1)S(1)}, u32[]{:S(2)}, u32[]{:S(2)}) collective-permute-start(bf16[1,200,800]{2,1,0:T(8,128)(2,1)S(1)} %collective-permute-done.11.refs_0_), channel_id=1, source_target_pairs={{0,1},{1,0},{2,3},{3,2},{4,5},{5,4},{6,7},{7,6},{8,9},{9,8},{10,11... | collective-permute-start | bytes 960008 | tf_op jit(solution)/shard_map/ppermute | solution.py:336
  59.4 12.6 %collective-permute-start.5 = (bf16[1,200,800]{2,1,0:T(8,128)(2,1)S(1)}, bf16[1,200,800]{2,1,0:T(8,128)(2,1)S(1)}, u32[]{:S(2)}, u32[]{:S(2)}) collective-permute-start(bf16[1,200,800]{2,1,0:T(8,128)(2,1)S(1)} %copy-done.3), channel_id=1, source_target_pairs={{0,4},{1,5},{2,6},{3,7},{4,8},{5,9},{6,10},{7,11},{8,12},{9,13},{1... | collective-permute-start | bytes 960008 | tf_op jit(solution)/shard_map/ppermute | solution.py:334
  59.4 12.6 %collective-permute-start.18 = (bf16[1,200,800]{2,1,0:T(8,128)(2,1)S(1)}, bf16[1,200,800]{2,1,0:T(8,128)(2,1)S(1)}, u32[]{:S(2)}, u32[]{:S(2)}) collective-permute-start(bf16[1,200,800]{2,1,0:T(8,128)(2,1)S(1)} %collective-permute-done.6.refs_0_), channel_id=1, source_target_pairs={{0,16},{16,0},{1,17},{17,1},{2,18},{18,2},{3,19},{19,3},{4,20},{20... | collective-permute-start | bytes 960008 | tf_op jit(solution)/shard_map/ppermute | solution.py:337
  60.5 11.4 %collective-permute-start.17 = (bf16[1,200,800]{2,1,0:T(8,128)(2,1)S(1)}, bf16[1,200,800]{2,1,0:T(8,128)(2,1)S(1)}, u32[]{:S(2)}, u32[]{:S(2)}) collective-permute-start(bf16[1,200,800]{2,1,0:T(8,128)(2,1)S(1)} %collective-permute-done.11.refs_0_), channel_id=1, source_target_pairs={{0,2},{1,3},{2,0},{3,1},{4,6},{5,7},{6,4},{7,5},{8,10},{9,11},{10,... | collective-permute-start | bytes 960008 | tf_op jit(solution)/shard_map/ppermute | solution.py:335
  66.5 23.4 %copy-start.1 = (f32[16,64,400]{2,1,0:T(8,128)S(1)}, f32[16,64,400]{2,1,0:T(8,128)}, u32[]{:S(2)}) copy-start(f32[16,64,400]{2,1,0:T(8,128)} %refs_6_.1) | copy-start | bytes 4915204
  72.0 3.3 %collective-permute-start.25 = (bf16[1,200,800]{2,1,0:T(8,128)(2,1)S(1)}, bf16[1,200,800]{2,1,0:T(8,128)(2,1)S(1)}, u32[]{:S(2)}, u32[]{:S(2)}) collective-permute-start(bf16[1,200,800]{2,1,0:T(8,128)(2,1)S(1)} %collective-permute-done.5.refs_0_), channel_id=1, source_target_pairs={{0,1},{1,0},{2,3},{3,2},{4,5},{5,4},{6,7},{7,6},{8,9},{9,8},{10,11... | collective-permute-start | bytes 960008 | tf_op jit(solution)/shard_map/ppermute | solution.py:336
  72.0 3.3 %collective-permute-start.26 = (bf16[1,200,800]{2,1,0:T(8,128)(2,1)S(1)}, bf16[1,200,800]{2,1,0:T(8,128)(2,1)S(1)}, u32[]{:S(2)}, u32[]{:S(2)}) collective-permute-start(bf16[1,200,800]{2,1,0:T(8,128)(2,1)S(1)} %collective-permute-done.17.refs_2_), channel_id=1, source_target_pairs={{0,1},{1,0},{2,3},{3,2},{4,5},{5,4},{6,7},{7,6},{8,9},{9,8},{10,11... | collective-permute-start | bytes 960008 | tf_op jit(solution)/shard_map/ppermute | solution.py:336
  72.5 2.8 %collective-permute-start.27 = (bf16[1,200,800]{2,1,0:T(8,128)(2,1)S(1)}, bf16[1,200,800]{2,1,0:T(8,128)(2,1)S(1)}, u32[]{:S(2)}, u32[]{:S(2)}) collective-permute-start(bf16[1,200,800]{2,1,0:T(8,128)(2,1)S(1)} %collective-permute-done.18.refs_4_), channel_id=1, source_target_pairs={{0,1},{1,0},{2,3},{3,2},{4,5},{5,4},{6,7},{7,6},{8,9},{9,8},{10,11... | collective-permute-start | bytes 960008 | tf_op jit(solution)/shard_map/ppermute | solution.py:336
  72.5 10.7 %collective-permute-start.24 = (bf16[1,200,800]{2,1,0:T(8,128)(2,1)S(1)}, bf16[1,200,800]{2,1,0:T(8,128)(2,1)S(1)}, u32[]{:S(2)}, u32[]{:S(2)}) collective-permute-start(bf16[1,200,800]{2,1,0:T(8,128)(2,1)S(1)} %collective-permute-done.17.refs_2_), channel_id=1, source_target_pairs={{0,16},{16,0},{1,17},{17,1},{2,18},{18,2},{3,19},{19,3},{4,20},{20... | collective-permute-start | bytes 960008 | tf_op jit(solution)/shard_map/ppermute | solution.py:337
  73.5 10.4 %collective-permute-start.23 = (bf16[1,200,800]{2,1,0:T(8,128)(2,1)S(1)}, bf16[1,200,800]{2,1,0:T(8,128)(2,1)S(1)}, u32[]{:S(2)}, u32[]{:S(2)}) collective-permute-start(bf16[1,200,800]{2,1,0:T(8,128)(2,1)S(1)} %collective-permute-done.18.refs_4_), channel_id=1, source_target_pairs={{0,2},{1,3},{2,0},{3,1},{4,6},{5,7},{6,4},{7,5},{8,10},{9,11},{10,... | collective-permute-start | bytes 960008 | tf_op jit(solution)/shard_map/ppermute | solution.py:335
  75.3 12.0 %collective-permute-start.22 = (bf16[1,200,800]{2,1,0:T(8,128)(2,1)S(1)}, bf16[1,200,800]{2,1,0:T(8,128)(2,1)S(1)}, u32[]{:S(2)}, u32[]{:S(2)}) collective-permute-start(bf16[1,200,800]{2,1,0:T(8,128)(2,1)S(1)} %collective-permute-done.18.refs_4_), channel_id=1, source_target_pairs={{0,4},{1,5},{2,6},{3,7},{4,8},{5,9},{6,10},{7,11},{8,12},{9,13},{1... | collective-permute-start | bytes 960008 | tf_op jit(solution)/shard_map/ppermute | solution.py:334
  87.2 1.7 %collective-permute-start.28 = (bf16[1,200,800]{2,1,0:T(8,128)(2,1)S(1)}, bf16[1,200,800]{2,1,0:T(8,128)(2,1)S(1)}, u32[]{:S(2)}, u32[]{:S(2)}) collective-permute-start(bf16[1,200,800]{2,1,0:T(8,128)(2,1)S(1)} %collective-permute-done.22.refs_0_), channel_id=1, source_target_pairs={{0,1},{1,0},{2,3},{3,2},{4,5},{5,4},{6,7},{7,6},{8,9},{9,8},{10,11... | collective-permute-start | bytes 960008 | tf_op jit(solution)/shard_map/ppermute | solution.py:336
  87.2 2.2 %collective-permute-start.29 = (bf16[1,200,800]{2,1,0:T(8,128)(2,1)S(1)}, bf16[1,200,800]{2,1,0:T(8,128)(2,1)S(1)}, u32[]{:S(2)}, u32[]{:S(2)}) collective-permute-start(bf16[1,200,800]{2,1,0:T(8,128)(2,1)S(1)} %collective-permute-done.23.refs_2_), channel_id=1, source_target_pairs={{0,1},{1,0},{2,3},{3,2},{4,5},{5,4},{6,7},{7,6},{8,9},{9,8},{10,11... | collective-permute-start | bytes 960008 | tf_op jit(solution)/shard_map/ppermute | solution.py:336
  87.7 2.2 %collective-permute-start.30 = (bf16[1,200,800]{2,1,0:T(8,128)(2,1)S(1)}, bf16[1,200,800]{2,1,0:T(8,128)(2,1)S(1)}, u32[]{:S(2)}, u32[]{:S(2)}) collective-permute-start(bf16[1,200,800]{2,1,0:T(8,128)(2,1)S(1)} %collective-permute-done.24.refs_4_), channel_id=1, source_target_pairs={{0,1},{1,0},{2,3},{3,2},{4,5},{5,4},{6,7},{7,6},{8,9},{9,8},{10,11... | collective-permute-start | bytes 960008 | tf_op jit(solution)/shard_map/ppermute | solution.py:336
  (5 other events, 73.2 us)

commit v4 on v3

--- a/solution.py
+++ b/solution.py
@@ -343,13 +343,14 @@
 
     tied = lax.optimization_barrier
     a, b = 0, 1
+    own_a, own_b, volume = tied((own_a, own_b, volume))
     t1a, y0a = along_z(own_a), along_y(own_a)
     above = passed_along(volume[:, rows - REACH :], "lenslet", 1)
     below = passed_along(volume[:, :REACH], "lenslet", -1)
     own_c = to_core(own)
     volume, scalars, own_b = tied((volume, scalars, own_b))
     copies = own_rows(volume)
-    t1a, y0a, above, below, own_c, copies = tied((t1a, y0a, above, below, own_c, copies))
+    t1a, y0a, copies = tied((t1a, y0a, copies))
     t2a, y1a, y0b = along_z(t1a), along_y(t1a), along_x(y0a)
     r0 = both(t1a, y0a)
     copies = edge_rows(above, below, copies)

time: 96.6 us -> 87.7 us (0.908)
  waiting for transfers between devices: 35.6 us -> 18.1 us
  starting transfers between devices: 25.4 us -> 33.3 us
    ppermute x4, waiting for transfers between devices: 7.96 us -> 0.01 us  [exchanged(): along_x = lambda v: lax.ppermute(v, 'frames', [(0, 1), (1, 0)])]
    ppermute x5, starting transfers between devices: 3.21 us -> 10.6 us  [exchanged(): along_z = lambda v: lax.ppermute(v, 'lenslet', up)]
    ppermute x5, waiting for transfers between devices: 6.8 us -> 0.3 us  [exchanged(): along_y = lambda v: lax.ppermute(v, 'lenslet', beside)]
    ppermute x15, starting transfers between devices: 5.54 us -> 3.59 us  [exchanged(): to_core = lambda v: lax.ppermute(v, 'lenslet', twin)]
    ppermute x5, waiting for transfers between devices: 17.2 us -> 15.6 us  [exchanged(): along_z = lambda v: lax.ppermute(v, 'lenslet', up)]
    ppermute x5, starting transfers between devices: 8.29 us -> 9.86 us  [exchanged(): along_y = lambda v: lax.ppermute(v, 'lenslet', beside)]
    ppermute x15, waiting for transfers between devices: 3.68 us -> 2.15 us  [exchanged(): to_core = lambda v: lax.ppermute(v, 'lenslet', twin)]
    ppermute x4, starting transfers between devices: 4.02 us -> 5.55 us  [exchanged(): along_x = lambda v: lax.ppermute(v, 'frames', [(0, 1), (1, 0)])]
  transfers between devices with their start and end apart: 31 -> 31, of which waited for: 18 -> 7; matrix products, arithmetic and copies ran while one was open for 4% -> 3% of each run, Pallas kernels for 25% -> 28%
where the time goes in v4:
time: 87.7 us; the launch traced here: 87.5 us
  starting transfers between devices  33.3 us (38%)
  Pallas kernels  30.8 us (35%)
  waiting for transfers between devices  18.1 us (21%)
  local copies, waits for them, and re-layouts  3.5 us (4%)
  between operations  1.03 us (1%)
    pallas_call x6, Pallas kernels, add_pieces(): pl.pallas_call(functools.partial(add_kernel, plan=plan, pieces=pieces, fi...  25.4 us
    ppermute x5, waiting for transfers between devices, exchanged(): along_z = lambda v: lax.ppermute(v, 'lenslet', up)  15.6 us
    ppermute x5, starting transfers between devices, exchanged(): along_z = lambda v: lax.ppermute(v, 'lenslet', up)  10.6 us
    ppermute x5, starting transfers between devices, exchanged(): along_y = lambda v: lax.ppermute(v, 'lenslet', beside)  9.86 us
    ppermute x4, starting transfers between devices, exchanged(): along_x = lambda v: lax.ppermute(v, 'frames', [(0, 1), (1, 0)])  5.55 us
    pallas_call x1, Pallas kernels, own_rows(): pl.pallas_call(own_rows_kernel, in_specs=[pl.BlockSpec(memory_space=pltpu...  4.58 us
    ppermute x2, starting transfers between devices, passed_along(): return lax.ppermute(block, axis, route)  3.74 us
    ppermute x15, starting transfers between devices, exchanged(): to_core = lambda v: lax.ppermute(v, 'lenslet', twin)  3.59 us
  transfers between devices with their start and end apart: 31, of which 7 were waited for; matrix products, arithmetic and copies ran while one was open for 3% of the time, Pallas kernels for 28%

profile of v4, /device:TPU:0, one launch (start us, length us, event | category | flops | bytes accessed | tf_op | source)
XLA Modules:
  0.0 87.5 jit_solution(10526585339113860483)
XLA Ops:
  0.6 2.0 %constant_dynamic-slice_fusion = (bf16[1,200,800]{2,1,0:T(8,128)(2,1)}, bf16[1,200,800]{2,1,0:T(8,128)(2,1)}) fusion(bf16[2,200,800]{2,1,0:T(8,128)(2,1)} %bitcast.6, s32[]{:T(128)S(6)} %select_n.8, s32[]{:T(128)S(6)} %select_n.7), kind=kLoop, calls=%fused_computation.1 | loop fusion | bytes 1280008 | tf_op jit(solution)/shard_map/jit(dynamic_index_in_dim)/dynamic_slice | solution.py:341
  2.7 3.0 %collective-permute-start.2 = (bf16[1,200,800]{2,1,0:T(8,128)(2,1)}, bf16[1,200,800]{2,1,0:T(8,128)(2,1)S(1)}, u32[]{:S(2)}, u32[]{:S(2)}) collective-permute-start(bf16[1,200,800]{2,1,0:T(8,128)(2,1)} %get-tuple-element.30), channel_id=1, source_target_pairs={{0,4},{1,5},{2,6},{3,7},{4,8},{5,9},{6,10},{7,11},{8,12},{9,13},{1... | collective-permute-start | bytes 960008 | tf_op jit(solution)/shard_map/ppermute | solution.py:334
  5.7 1.5 %collective-permute-start.3 = (bf16[1,200,800]{2,1,0:T(8,128)(2,1)}, bf16[1,200,800]{2,1,0:T(8,128)(2,1)S(1)}, u32[]{:S(2)}, u32[]{:S(2)}) collective-permute-start(bf16[1,200,800]{2,1,0:T(8,128)(2,1)} %get-tuple-element.30), channel_id=1, source_target_pairs={{0,2},{1,3},{2,0},{3,1},{4,6},{5,7},{6,4},{7,5},{8,10},{9,11},{10,... | collective-permute-start | bytes 960008 | tf_op jit(solution)/shard_map/ppermute | solution.py:335
  7.2 1.3 %fusion = (bf16[4,2,64,400]{3,2,1,0:T(8,128)(2,1)S(1)}, bf16[4,2,64,400]{3,2,1,0:T(8,128)(2,1)S(1)}) fusion(bf16[4,16,64,400]{3,2,1,0:T(8,128)(2,1)} %volume_ref), kind=kLoop, calls=%fused_computation.3 | loop fusion | bytes 1638400 | tf_op jit(solution)/shard_map/slice | solution.py:349
  8.5 2.4 %collective-permute-start = (bf16[4,2,64,400]{3,2,1,0:T(8,128)(2,1)S(1)}, bf16[4,2,64,400]{3,2,1,0:T(8,128)(2,1)S(1)}, u32[]{:S(2)}, u32[]{:S(2)}) collective-permute-start(bf16[4,2,64,400]{3,2,1,0:T(8,128)(2,1)S(1)} %get-tuple-element.53), channel_id=1, source_target_pairs={{0,1},{1,2},{2,3},{3,4},{4,5},{5,6},{6,7},{7,8},{8,9},{9,10},{10,1... | collective-permute-start | bytes 1228808 | tf_op jit(solution)/shard_map/ppermute | solution.py:20
  10.9 1.3 %collective-permute-start.1 = (bf16[4,2,64,400]{3,2,1,0:T(8,128)(2,1)S(1)}, bf16[4,2,64,400]{3,2,1,0:T(8,128)(2,1)S(1)}, u32[]{:S(2)}, u32[]{:S(2)}) collective-permute-start(bf16[4,2,64,400]{3,2,1,0:T(8,128)(2,1)S(1)} %get-tuple-element.52), channel_id=1, source_target_pairs={{1,0},{2,1},{3,2},{4,3},{5,4},{6,5},{7,6},{8,7},{9,8},{10,9},{11,1... | collective-permute-start | bytes 1228808 | tf_op jit(solution)/shard_map/ppermute | solution.py:20
  12.4 0.7 pad_add_fusion.scalars
  13.2 4.6 %own_rows.1.old_ref = bf16[20,20,64,400]{3,2,1,0:T(8,128)(2,1)S(1)} custom-call(bf16[4,16,64,400]{3,2,1,0:T(8,128)(2,1)} %volume_ref), custom_call_target="tpu_custom_call" | custom-call | tf_op jit(solution)/shard_map/own_rows/pallas_call | solution.py:188
  17.8 1.2 %collective-permute-start.8 = (bf16[1,200,800]{2,1,0:T(8,128)(2,1)S(1)}, bf16[1,200,800]{2,1,0:T(8,128)(2,1)S(1)}, u32[]{:S(2)}, u32[]{:S(2)}) collective-permute-start(bf16[1,200,800]{2,1,0:T(8,128)(2,1)S(1)} %collective-permute-done.2.refs_0_), channel_id=1, source_target_pairs={{0,1},{1,0},{2,3},{3,2},{4,5},{5,4},{6,7},{7,6},{8,9},{9,8},{10,11... | collective-permute-start | bytes 960008 | tf_op jit(solution)/shard_map/ppermute | solution.py:336
  19.1 4.4 %collective-permute-start.5 = (bf16[1,200,800]{2,1,0:T(8,128)(2,1)S(1)}, bf16[1,200,800]{2,1,0:T(8,128)(2,1)S(1)}, u32[]{:S(2)}, u32[]{:S(2)}) collective-permute-start(bf16[1,200,800]{2,1,0:T(8,128)(2,1)S(1)} %collective-permute-done.2.refs_0_), channel_id=1, source_target_pairs={{0,4},{1,5},{2,6},{3,7},{4,8},{5,9},{6,10},{7,11},{8,12},{9,13},{1... | collective-permute-start | bytes 960008 | tf_op jit(solution)/shard_map/ppermute | solution.py:334
  23.4 6.6 %collective-permute-start.6 = (bf16[1,200,800]{2,1,0:T(8,128)(2,1)S(1)}, bf16[1,200,800]{2,1,0:T(8,128)(2,1)S(1)}, u32[]{:S(2)}, u32[]{:S(2)}) collective-permute-start(bf16[1,200,800]{2,1,0:T(8,128)(2,1)S(1)} %collective-permute-done.2.refs_0_), channel_id=1, source_target_pairs={{0,2},{1,3},{2,0},{3,1},{4,6},{5,7},{6,4},{7,5},{8,10},{9,11},{10,... | collective-permute-start | bytes 960008 | tf_op jit(solution)/shard_map/ppermute | solution.py:335
  30.1 1.5 %collective-permute-start.7 = (bf16[1,200,800]{2,1,0:T(8,128)(2,1)S(1)}, bf16[1,200,800]{2,1,0:T(8,128)(2,1)S(1)}, u32[]{:S(2)}, u32[]{:S(2)}) collective-permute-start(bf16[1,200,800]{2,1,0:T(8,128)(2,1)S(1)} %collective-permute-done.3.refs_2_), channel_id=1, source_target_pairs={{0,16},{16,0},{1,17},{17,1},{2,18},{18,2},{3,19},{19,3},{4,20},{20... | collective-permute-start | bytes 960008 | tf_op jit(solution)/shard_map/ppermute | solution.py:337
  31.5 0.9 %edge_rows.1.copies = bf16[20,20,64,400]{3,2,1,0:T(8,128)(2,1)S(1)} custom-call(bf16[4,2,64,400]{3,2,1,0:T(8,128)(2,1)S(1)} %collective-permute-done.above_ref, bf16[4,2,64,400]{3,2,1,0:T(8,128)(2,1)S(1)} %collective-permute-done.1.below_ref, bf16[20,20,64,400]{3,2,1,0:T(8,128)(2,1)S(1)} %own_rows.1.old_ref), custom_call_target="tpu_custom_call", output_to_operand_aliasing={{}: (2, {})} | custom-call | tf_op jit(solution)/shard_map/edge_rows/pallas_call | solution.py:200
  32.5 3.0 %add_pieces.6.refs_4_ = f32[2,1024,200]{2,1,0:T(8,128)S(1)} custom-call(s32[70]{0:T(128)S(1)} %pad_add_fusion.scalars, bf16[20,20,64,400]{3,2,1,0:T(8,128)(2,1)S(1)} %edge_rows.1.copies, bf16[2,200,800]{2,1,0:T(8,128)(2,1)S(1)} %bitcast.8, bf16[2,200,800]{2,1,0:T(8,128)(2,1)S(1)} %collective-permute-done.10.refs_1_.refs_3_, ...), custom_call_target="tpu_custom_call" | custom-call | flops 1310720000 | bytes 2097152 | tf_op jit(solution)/shard_map/add_pieces/pallas_call | solution.py:301
  35.5 3.1 %add_pieces.7.refs_6_ = f32[2,1024,200]{2,1,0:T(8,128)S(1)} custom-call(s32[70]{0:T(128)S(1)} %pad_add_fusion.scalars, bf16[20,20,64,400]{3,2,1,0:T(8,128)(2,1)S(1)} %edge_rows.1.copies, bf16[1,200,800]{2,1,0:T(8,128)(2,1)S(1)} %collective-permute-done.2.refs_0_, ...), custom_call_target="tpu_custom_call", output_to_operand_aliasing={{}: (6, {})} | custom-call | flops 1310720000 | bytes 2097152 | tf_op jit(solution)/shard_map/add_pieces/pallas_call | solution.py:301
  39.3 1.6 %collective-permute-start.11 = (bf16[1,200,800]{2,1,0:T(8,128)(2,1)S(1)}, bf16[1,200,800]{2,1,0:T(8,128)(2,1)S(1)}, u32[]{:S(2)}, u32[]{:S(2)}) collective-permute-start(bf16[1,200,800]{2,1,0:T(8,128)(2,1)S(1)} %collective-permute-done.5.refs_0_), channel_id=1, source_target_pairs={{0,4},{1,5},{2,6},{3,7},{4,8},{5,9},{6,10},{7,11},{8,12},{9,13},{1... | collective-permute-start | bytes 960008 | tf_op jit(solution)/shard_map/ppermute | solution.py:334
  40.9 0.6 collective-permute-start.12
  41.5 1.5 %collective-permute-start.13 = (bf16[1,200,800]{2,1,0:T(8,128)(2,1)S(1)}, bf16[1,200,800]{2,1,0:T(8,128)(2,1)S(1)}, u32[]{:S(2)}, u32[]{:S(2)}) collective-permute-start(bf16[1,200,800]{2,1,0:T(8,128)(2,1)S(1)} %collective-permute-done.6.refs_2_), channel_id=1, source_target_pairs={{0,16},{16,0},{1,17},{17,1},{2,18},{18,2},{3,19},{19,3},{4,20},{20... | collective-permute-start | bytes 960008 | tf_op jit(solution)/shard_map/ppermute | solution.py:337
  43.0 4.3 %add_pieces.8.refs_6_ = f32[2,1024,200]{2,1,0:T(8,128)S(1)} custom-call(s32[70]{0:T(128)S(1)} %pad_add_fusion.scalars, bf16[20,20,64,400]{3,2,1,0:T(8,128)(2,1)S(1)} %edge_rows.1.copies, bf16[1,200,800]{2,1,0:T(8,128)(2,1)S(1)} %collective-permute-done.5.refs_0_, ...), custom_call_target="tpu_custom_call", output_to_operand_aliasing={{}: (8, {})} | custom-call | flops 1966080000 | bytes 3145728 | tf_op jit(solution)/shard_map/add_pieces/pallas_call | solution.py:301
  47.3 4.5 %collective-permute-done.11.refs_0_ = bf16[1,200,800]{2,1,0:T(8,128)(2,1)S(1)} collective-permute-done((bf16[1,200,800]{2,1,0:T(8,128)(2,1)S(1)}, bf16[1,200,800]{2,1,0:T(8,128)(2,1)S(1)}, u32[]{:S(2)}, u32[]{:S(2)}) %collective-permute-start.11) | collective-permute-done | bytes 320032 | tf_op jit(solution)/shard_map/ppermute | solution.py:334
  52.4 1.1 %collective-permute-start.4 = (bf16[1,200,800]{2,1,0:T(8,128)(2,1)S(1)}, bf16[1,200,800]{2,1,0:T(8,128)(2,1)S(1)}, u32[]{:S(2)}, u32[]{:S(2)}) collective-permute-start(bf16[1,200,800]{2,1,0:T(8,128)(2,1)S(1)} %copy-done.3), channel_id=1, source_target_pairs={{0,4},{1,5},{2,6},{3,7},{4,8},{5,9},{6,10},{7,11},{8,12},{9,13},{1... | collective-permute-start | bytes 960008 | tf_op jit(solution)/shard_map/ppermute | solution.py:334
  53.5 1.5 %collective-permute-start.18 = (bf16[1,200,800]{2,1,0:T(8,128)(2,1)S(1)}, bf16[1,200,800]{2,1,0:T(8,128)(2,1)S(1)}, u32[]{:S(2)}, u32[]{:S(2)}) collective-permute-start(bf16[1,200,800]{2,1,0:T(8,128)(2,1)S(1)} %collective-permute-done.5.refs_0_), channel_id=1, source_target_pairs={{0,16},{16,0},{1,17},{17,1},{2,18},{18,2},{3,19},{19,3},{4,20},{20... | collective-permute-start | bytes 960008 | tf_op jit(solution)/shard_map/ppermute | solution.py:337
  55.3 4.3 %add_pieces.9.refs_6_ = f32[2,1024,200]{2,1,0:T(8,128)S(1)} custom-call(s32[70]{0:T(128)S(1)} %pad_add_fusion.scalars, bf16[20,20,64,400]{3,2,1,0:T(8,128)(2,1)S(1)} %edge_rows.1.copies, bf16[1,200,800]{2,1,0:T(8,128)(2,1)S(1)} %collective-permute-done.11.refs_0_, ...), custom_call_target="tpu_custom_call", output_to_operand_aliasing={{}: (8, {})} | custom-call | flops 1966080000 | bytes 3145728 | tf_op jit(solution)/shard_map/add_pieces/pallas_call | solution.py:301
  59.6 5.3 %collective-permute-done.4.refs_0_ = bf16[1,200,800]{2,1,0:T(8,128)(2,1)S(1)} collective-permute-done((bf16[1,200,800]{2,1,0:T(8,128)(2,1)S(1)}, bf16[1,200,800]{2,1,0:T(8,128)(2,1)S(1)}, u32[]{:S(2)}, u32[]{:S(2)}) %collective-permute-start.4) | collective-permute-done | bytes 320032 | tf_op jit(solution)/shard_map/ppermute | solution.py:334
  65.7 0.6 collective-permute-start.22
  66.3 0.8 collective-permute-start.23
  67.1 1.1 %collective-permute-start.24 = (bf16[1,200,800]{2,1,0:T(8,128)(2,1)S(1)}, bf16[1,200,800]{2,1,0:T(8,128)(2,1)S(1)}, u32[]{:S(2)}, u32[]{:S(2)}) collective-permute-start(bf16[1,200,800]{2,1,0:T(8,128)(2,1)S(1)} %collective-permute-done.17.refs_2_), channel_id=1, source_target_pairs={{0,16},{16,0},{1,17},{17,1},{2,18},{18,2},{3,19},{19,3},{4,20},{20... | collective-permute-start | bytes 960008 | tf_op jit(solution)/shard_map/ppermute | solution.py:337
  68.2 4.3 %add_pieces.10.refs_8_ = f32[2,1024,200]{2,1,0:T(8,128)S(1)} custom-call(s32[70]{0:T(128)S(1)} %pad_add_fusion.scalars, bf16[20,20,64,400]{3,2,1,0:T(8,128)(2,1)S(1)} %edge_rows.1.copies, bf16[1,200,800]{2,1,0:T(8,128)(2,1)S(1)} %collective-permute-done.4.refs_0_, ...), custom_call_target="tpu_custom_call", output_to_operand_aliasing={{}: (8, {})} | custom-call | flops 1966080000 | bytes 3145728 | tf_op jit(solution)/shard_map/add_pieces/pallas_call | solution.py:301
  72.5 5.9 %collective-permute-done.22.refs_0_ = bf16[1,200,800]{2,1,0:T(8,128)(2,1)S(1)} collective-permute-done((bf16[1,200,800]{2,1,0:T(8,128)(2,1)S(1)}, bf16[1,200,800]{2,1,0:T(8,128)(2,1)S(1)}, u32[]{:S(2)}, u32[]{:S(2)}) %collective-permute-start.22) | collective-permute-done | bytes 320032 | tf_op jit(solution)/shard_map/ppermute | solution.py:334
  78.9 1.1 %collective-permute-done.28.refs_1_ = bf16[1,200,800]{2,1,0:T(8,128)(2,1)S(1)} collective-permute-done((bf16[1,200,800]{2,1,0:T(8,128)(2,1)S(1)}, bf16[1,200,800]{2,1,0:T(8,128)(2,1)S(1)}, u32[]{:S(2)}, u32[]{:S(2)}) %collective-permute-start.28) | collective-permute-done | bytes 320032 | tf_op jit(solution)/shard_map/ppermute | solution.py:336
  80.0 0.5 collective-permute-done.29.refs_3_
  81.0 6.3 %add_pieces.11 = (f32[16,64,400]{2,1,0:T(8,128)}, f32[16,64,400]{2,1,0:T(8,128)}) custom-call(s32[70]{0:T(128)S(1)} %pad_add_fusion.scalars, bf16[20,20,64,400]{3,2,1,0:T(8,128)(2,1)S(1)} %edge_rows.1.copies, bf16[1,200,800]{2,1,0:T(8,128)(2,1)S(1)} %collective-permute-done.22.refs_0_, bf16[1,200,800]{2,1,0:T(8,128)(2,1)S(1)} %collective-permute-done.28.refs_1_, ...), custom_call_target="tpu_custom_call" | custom-call | flops 1966080000 | bytes 3145728 | tf_op jit(solution)/shard_map/add_pieces/pallas_call | solution.py:301
  (53 shorter events, 3.8 us)
Async XLA Ops:
  2.7 15.1 %collective-permute-start.2 = (bf16[1,200,800]{2,1,0:T(8,128)(2,1)}, bf16[1,200,800]{2,1,0:T(8,128)(2,1)S(1)}, u32[]{:S(2)}, u32[]{:S(2)}) collective-permute-start(bf16[1,200,800]{2,1,0:T(8,128)(2,1)} %get-tuple-element.30), channel_id=1, source_target_pairs={{0,4},{1,5},{2,6},{3,7},{4,8},{5,9},{6,10},{7,11},{8,12},{9,13},{1... | collective-permute-start | bytes 960008 | tf_op jit(solution)/shard_map/ppermute | solution.py:334
  5.7 12.1 %collective-permute-start.3 = (bf16[1,200,800]{2,1,0:T(8,128)(2,1)}, bf16[1,200,800]{2,1,0:T(8,128)(2,1)S(1)}, u32[]{:S(2)}, u32[]{:S(2)}) collective-permute-start(bf16[1,200,800]{2,1,0:T(8,128)(2,1)} %get-tuple-element.30), channel_id=1, source_target_pairs={{0,2},{1,3},{2,0},{3,1},{4,6},{5,7},{6,4},{7,5},{8,10},{9,11},{10,... | collective-permute-start | bytes 960008 | tf_op jit(solution)/shard_map/ppermute | solution.py:335
  7.2 22.9 %collective-permute-start.10 = (bf16[2,200,800]{2,1,0:T(8,128)(2,1)}, bf16[2,200,800]{2,1,0:T(8,128)(2,1)S(1)}, u32[]{:S(2)}, u32[]{:S(2)}) collective-permute-start(bf16[2,200,800]{2,1,0:T(8,128)(2,1)} %bitcast.7), channel_id=1, source_target_pairs={{0,1},{1,0},{2,3},{3,2},{4,5},{5,4},{6,7},{7,6},{8,9},{9,8},{10,11... | collective-permute-start | bytes 1920008 | tf_op jit(solution)/shard_map/ppermute | solution.py:336
  8.5 10.6 %collective-permute-start = (bf16[4,2,64,400]{3,2,1,0:T(8,128)(2,1)S(1)}, bf16[4,2,64,400]{3,2,1,0:T(8,128)(2,1)S(1)}, u32[]{:S(2)}, u32[]{:S(2)}) collective-permute-start(bf16[4,2,64,400]{3,2,1,0:T(8,128)(2,1)S(1)} %get-tuple-element.53), channel_id=1, source_target_pairs={{0,1},{1,2},{2,3},{3,4},{4,5},{5,6},{6,7},{7,8},{8,9},{9,10},{10,1... | collective-permute-start | bytes 1228808 | tf_op jit(solution)/shard_map/ppermute | solution.py:20
  10.9 12.5 %collective-permute-start.1 = (bf16[4,2,64,400]{3,2,1,0:T(8,128)(2,1)S(1)}, bf16[4,2,64,400]{3,2,1,0:T(8,128)(2,1)S(1)}, u32[]{:S(2)}, u32[]{:S(2)}) collective-permute-start(bf16[4,2,64,400]{3,2,1,0:T(8,128)(2,1)S(1)} %get-tuple-element.52), channel_id=1, source_target_pairs={{1,0},{2,1},{3,2},{4,3},{5,4},{6,5},{7,6},{8,7},{9,8},{10,9},{11,1... | collective-permute-start | bytes 1228808 | tf_op jit(solution)/shard_map/ppermute | solution.py:20
  17.8 17.7 %collective-permute-start.8 = (bf16[1,200,800]{2,1,0:T(8,128)(2,1)S(1)}, bf16[1,200,800]{2,1,0:T(8,128)(2,1)S(1)}, u32[]{:S(2)}, u32[]{:S(2)}) collective-permute-start(bf16[1,200,800]{2,1,0:T(8,128)(2,1)S(1)} %collective-permute-done.2.refs_0_), channel_id=1, source_target_pairs={{0,1},{1,0},{2,3},{3,2},{4,5},{5,4},{6,7},{7,6},{8,9},{9,8},{10,11... | collective-permute-start | bytes 960008 | tf_op jit(solution)/shard_map/ppermute | solution.py:336
  19.0 16.5 %collective-permute-start.9 = (bf16[1,200,800]{2,1,0:T(8,128)(2,1)S(1)}, bf16[1,200,800]{2,1,0:T(8,128)(2,1)S(1)}, u32[]{:S(2)}, u32[]{:S(2)}) collective-permute-start(bf16[1,200,800]{2,1,0:T(8,128)(2,1)S(1)} %collective-permute-done.3.refs_2_), channel_id=1, source_target_pairs={{0,1},{1,0},{2,3},{3,2},{4,5},{5,4},{6,7},{7,6},{8,9},{9,8},{10,11... | collective-permute-start | bytes 960008 | tf_op jit(solution)/shard_map/ppermute | solution.py:336
  19.1 19.6 %collective-permute-start.5 = (bf16[1,200,800]{2,1,0:T(8,128)(2,1)S(1)}, bf16[1,200,800]{2,1,0:T(8,128)(2,1)S(1)}, u32[]{:S(2)}, u32[]{:S(2)}) collective-permute-start(bf16[1,200,800]{2,1,0:T(8,128)(2,1)S(1)} %collective-permute-done.2.refs_0_), channel_id=1, source_target_pairs={{0,4},{1,5},{2,6},{3,7},{4,8},{5,9},{6,10},{7,11},{8,12},{9,13},{1... | collective-permute-start | bytes 960008 | tf_op jit(solution)/shard_map/ppermute | solution.py:334
  23.4 15.2 %collective-permute-start.6 = (bf16[1,200,800]{2,1,0:T(8,128)(2,1)S(1)}, bf16[1,200,800]{2,1,0:T(8,128)(2,1)S(1)}, u32[]{:S(2)}, u32[]{:S(2)}) collective-permute-start(bf16[1,200,800]{2,1,0:T(8,128)(2,1)S(1)} %collective-permute-done.2.refs_0_), channel_id=1, source_target_pairs={{0,2},{1,3},{2,0},{3,1},{4,6},{5,7},{6,4},{7,5},{8,10},{9,11},{10,... | collective-permute-start | bytes 960008 | tf_op jit(solution)/shard_map/ppermute | solution.py:335
  30.1 8.6 %collective-permute-start.7 = (bf16[1,200,800]{2,1,0:T(8,128)(2,1)S(1)}, bf16[1,200,800]{2,1,0:T(8,128)(2,1)S(1)}, u32[]{:S(2)}, u32[]{:S(2)}) collective-permute-start(bf16[1,200,800]{2,1,0:T(8,128)(2,1)S(1)} %collective-permute-done.3.refs_2_), channel_id=1, source_target_pairs={{0,16},{16,0},{1,17},{17,1},{2,18},{18,2},{3,19},{19,3},{4,20},{20... | collective-permute-start | bytes 960008 | tf_op jit(solution)/shard_map/ppermute | solution.py:337
  38.6 2.9 %collective-permute-start.14 = (bf16[1,200,800]{2,1,0:T(8,128)(2,1)S(1)}, bf16[1,200,800]{2,1,0:T(8,128)(2,1)S(1)}, u32[]{:S(2)}, u32[]{:S(2)}) collective-permute-start(bf16[1,200,800]{2,1,0:T(8,128)(2,1)S(1)} %collective-permute-done.5.refs_0_), channel_id=1, source_target_pairs={{0,1},{1,0},{2,3},{3,2},{4,5},{5,4},{6,7},{7,6},{8,9},{9,8},{10,11... | collective-permute-start | bytes 960008 | tf_op jit(solution)/shard_map/ppermute | solution.py:336
  38.7 4.3 %collective-permute-start.15 = (bf16[1,200,800]{2,1,0:T(8,128)(2,1)S(1)}, bf16[1,200,800]{2,1,0:T(8,128)(2,1)S(1)}, u32[]{:S(2)}, u32[]{:S(2)}) collective-permute-start(bf16[1,200,800]{2,1,0:T(8,128)(2,1)S(1)} %collective-permute-done.6.refs_2_), channel_id=1, source_target_pairs={{0,1},{1,0},{2,3},{3,2},{4,5},{5,4},{6,7},{7,6},{8,9},{9,8},{10,11... | collective-permute-start | bytes 960008 | tf_op jit(solution)/shard_map/ppermute | solution.py:336
  39.2 3.8 %collective-permute-start.16 = (bf16[1,200,800]{2,1,0:T(8,128)(2,1)S(1)}, bf16[1,200,800]{2,1,0:T(8,128)(2,1)S(1)}, u32[]{:S(2)}, u32[]{:S(2)}) collective-permute-start(bf16[1,200,800]{2,1,0:T(8,128)(2,1)S(1)} %collective-permute-done.7.refs_4_), channel_id=1, source_target_pairs={{0,1},{1,0},{2,3},{3,2},{4,5},{5,4},{6,7},{7,6},{8,9},{9,8},{10,11... | collective-permute-start | bytes 960008 | tf_op jit(solution)/shard_map/ppermute | solution.py:336
  39.3 12.5 %collective-permute-start.11 = (bf16[1,200,800]{2,1,0:T(8,128)(2,1)S(1)}, bf16[1,200,800]{2,1,0:T(8,128)(2,1)S(1)}, u32[]{:S(2)}, u32[]{:S(2)}) collective-permute-start(bf16[1,200,800]{2,1,0:T(8,128)(2,1)S(1)} %collective-permute-done.5.refs_0_), channel_id=1, source_target_pairs={{0,4},{1,5},{2,6},{3,7},{4,8},{5,9},{6,10},{7,11},{8,12},{9,13},{1... | collective-permute-start | bytes 960008 | tf_op jit(solution)/shard_map/ppermute | solution.py:334
  40.9 10.9 %collective-permute-start.12 = (bf16[1,200,800]{2,1,0:T(8,128)(2,1)S(1)}, bf16[1,200,800]{2,1,0:T(8,128)(2,1)S(1)}, u32[]{:S(2)}, u32[]{:S(2)}) collective-permute-start(bf16[1,200,800]{2,1,0:T(8,128)(2,1)S(1)} %collective-permute-done.5.refs_0_), channel_id=1, source_target_pairs={{0,2},{1,3},{2,0},{3,1},{4,6},{5,7},{6,4},{7,5},{8,10},{9,11},{10,... | collective-permute-start | bytes 960008 | tf_op jit(solution)/shard_map/ppermute | solution.py:335
  41.5 10.3 %collective-permute-start.13 = (bf16[1,200,800]{2,1,0:T(8,128)(2,1)S(1)}, bf16[1,200,800]{2,1,0:T(8,128)(2,1)S(1)}, u32[]{:S(2)}, u32[]{:S(2)}) collective-permute-start(bf16[1,200,800]{2,1,0:T(8,128)(2,1)S(1)} %collective-permute-done.6.refs_2_), channel_id=1, source_target_pairs={{0,16},{16,0},{1,17},{17,1},{2,18},{18,2},{3,19},{19,3},{4,20},{20... | collective-permute-start | bytes 960008 | tf_op jit(solution)/shard_map/ppermute | solution.py:337
  51.8 3.2 %collective-permute-start.19 = (bf16[1,200,800]{2,1,0:T(8,128)(2,1)S(1)}, bf16[1,200,800]{2,1,0:T(8,128)(2,1)S(1)}, u32[]{:S(2)}, u32[]{:S(2)}) collective-permute-start(bf16[1,200,800]{2,1,0:T(8,128)(2,1)S(1)} %collective-permute-done.11.refs_0_), channel_id=1, source_target_pairs={{0,1},{1,0},{2,3},{3,2},{4,5},{5,4},{6,7},{7,6},{8,9},{9,8},{10,11... | collective-permute-start | bytes 960008 | tf_op jit(solution)/shard_map/ppermute | solution.py:336
  51.8 3.5 %collective-permute-start.20 = (bf16[1,200,800]{2,1,0:T(8,128)(2,1)S(1)}, bf16[1,200,800]{2,1,0:T(8,128)(2,1)S(1)}, u32[]{:S(2)}, u32[]{:S(2)}) collective-permute-start(bf16[1,200,800]{2,1,0:T(8,128)(2,1)S(1)} %collective-permute-done.12.refs_2_), channel_id=1, source_target_pairs={{0,1},{1,0},{2,3},{3,2},{4,5},{5,4},{6,7},{7,6},{8,9},{9,8},{10,11... | collective-permute-start | bytes 960008 | tf_op jit(solution)/shard_map/ppermute | solution.py:336
  52.3 3.0 %collective-permute-start.21 = (bf16[1,200,800]{2,1,0:T(8,128)(2,1)S(1)}, bf16[1,200,800]{2,1,0:T(8,128)(2,1)S(1)}, u32[]{:S(2)}, u32[]{:S(2)}) collective-permute-start(bf16[1,200,800]{2,1,0:T(8,128)(2,1)S(1)} %collective-permute-done.13.refs_4_), channel_id=1, source_target_pairs={{0,1},{1,0},{2,3},{3,2},{4,5},{5,4},{6,7},{7,6},{8,9},{9,8},{10,11... | collective-permute-start | bytes 960008 | tf_op jit(solution)/shard_map/ppermute | solution.py:336
  52.4 12.5 %collective-permute-start.4 = (bf16[1,200,800]{2,1,0:T(8,128)(2,1)S(1)}, bf16[1,200,800]{2,1,0:T(8,128)(2,1)S(1)}, u32[]{:S(2)}, u32[]{:S(2)}) collective-permute-start(bf16[1,200,800]{2,1,0:T(8,128)(2,1)S(1)} %copy-done.3), channel_id=1, source_target_pairs={{0,4},{1,5},{2,6},{3,7},{4,8},{5,9},{6,10},{7,11},{8,12},{9,13},{1... | collective-permute-start | bytes 960008 | tf_op jit(solution)/shard_map/ppermute | solution.py:334
  53.5 11.4 %collective-permute-start.18 = (bf16[1,200,800]{2,1,0:T(8,128)(2,1)S(1)}, bf16[1,200,800]{2,1,0:T(8,128)(2,1)S(1)}, u32[]{:S(2)}, u32[]{:S(2)}) collective-permute-start(bf16[1,200,800]{2,1,0:T(8,128)(2,1)S(1)} %collective-permute-done.5.refs_0_), channel_id=1, source_target_pairs={{0,16},{16,0},{1,17},{17,1},{2,18},{18,2},{3,19},{19,3},{4,20},{20... | collective-permute-start | bytes 960008 | tf_op jit(solution)/shard_map/ppermute | solution.py:337
  55.0 10.2 %collective-permute-start.17 = (bf16[1,200,800]{2,1,0:T(8,128)(2,1)S(1)}, bf16[1,200,800]{2,1,0:T(8,128)(2,1)S(1)}, u32[]{:S(2)}, u32[]{:S(2)}) collective-permute-start(bf16[1,200,800]{2,1,0:T(8,128)(2,1)S(1)} %collective-permute-done.11.refs_0_), channel_id=1, source_target_pairs={{0,2},{1,3},{2,0},{3,1},{4,6},{5,7},{6,4},{7,5},{8,10},{9,11},{10,... | collective-permute-start | bytes 960008 | tf_op jit(solution)/shard_map/ppermute | solution.py:335
  59.6 21.4 %copy-start.1 = (f32[16,64,400]{2,1,0:T(8,128)S(1)}, f32[16,64,400]{2,1,0:T(8,128)}, u32[]{:S(2)}) copy-start(f32[16,64,400]{2,1,0:T(8,128)} %refs_6_.1) | copy-start | bytes 4915204
  65.2 1.9 %collective-permute-start.25 = (bf16[1,200,800]{2,1,0:T(8,128)(2,1)S(1)}, bf16[1,200,800]{2,1,0:T(8,128)(2,1)S(1)}, u32[]{:S(2)}, u32[]{:S(2)}) collective-permute-start(bf16[1,200,800]{2,1,0:T(8,128)(2,1)S(1)} %collective-permute-done.4.refs_0_), channel_id=1, source_target_pairs={{0,1},{1,0},{2,3},{3,2},{4,5},{5,4},{6,7},{7,6},{8,9},{9,8},{10,11... | collective-permute-start | bytes 960008 | tf_op jit(solution)/shard_map/ppermute | solution.py:336
  65.2 2.9 %collective-permute-start.26 = (bf16[1,200,800]{2,1,0:T(8,128)(2,1)S(1)}, bf16[1,200,800]{2,1,0:T(8,128)(2,1)S(1)}, u32[]{:S(2)}, u32[]{:S(2)}) collective-permute-start(bf16[1,200,800]{2,1,0:T(8,128)(2,1)S(1)} %collective-permute-done.17.refs_2_), channel_id=1, source_target_pairs={{0,1},{1,0},{2,3},{3,2},{4,5},{5,4},{6,7},{7,6},{8,9},{9,8},{10,11... | collective-permute-start | bytes 960008 | tf_op jit(solution)/shard_map/ppermute | solution.py:336
  65.7 2.4 %collective-permute-start.27 = (bf16[1,200,800]{2,1,0:T(8,128)(2,1)S(1)}, bf16[1,200,800]{2,1,0:T(8,128)(2,1)S(1)}, u32[]{:S(2)}, u32[]{:S(2)}) collective-permute-start(bf16[1,200,800]{2,1,0:T(8,128)(2,1)S(1)} %collective-permute-done.18.refs_4_), channel_id=1, source_target_pairs={{0,1},{1,0},{2,3},{3,2},{4,5},{5,4},{6,7},{7,6},{8,9},{9,8},{10,11... | collective-permute-start | bytes 960008 | tf_op jit(solution)/shard_map/ppermute | solution.py:336
  65.7 12.6 %collective-permute-start.22 = (bf16[1,200,800]{2,1,0:T(8,128)(2,1)S(1)}, bf16[1,200,800]{2,1,0:T(8,128)(2,1)S(1)}, u32[]{:S(2)}, u32[]{:S(2)}) collective-permute-start(bf16[1,200,800]{2,1,0:T(8,128)(2,1)S(1)} %collective-permute-done.18.refs_4_), channel_id=1, source_target_pairs={{0,4},{1,5},{2,6},{3,7},{4,8},{5,9},{6,10},{7,11},{8,12},{9,13},{1... | collective-permute-start | bytes 960008 | tf_op jit(solution)/shard_map/ppermute | solution.py:334
  66.3 12.0 %collective-permute-start.23 = (bf16[1,200,800]{2,1,0:T(8,128)(2,1)S(1)}, bf16[1,200,800]{2,1,0:T(8,128)(2,1)S(1)}, u32[]{:S(2)}, u32[]{:S(2)}) collective-permute-start(bf16[1,200,800]{2,1,0:T(8,128)(2,1)S(1)} %collective-permute-done.18.refs_4_), channel_id=1, source_target_pairs={{0,2},{1,3},{2,0},{3,1},{4,6},{5,7},{6,4},{7,5},{8,10},{9,11},{10,... | collective-permute-start | bytes 960008 | tf_op jit(solution)/shard_map/ppermute | solution.py:335
  67.1 11.2 %collective-permute-start.24 = (bf16[1,200,800]{2,1,0:T(8,128)(2,1)S(1)}, bf16[1,200,800]{2,1,0:T(8,128)(2,1)S(1)}, u32[]{:S(2)}, u32[]{:S(2)}) collective-permute-start(bf16[1,200,800]{2,1,0:T(8,128)(2,1)S(1)} %collective-permute-done.17.refs_2_), channel_id=1, source_target_pairs={{0,16},{16,0},{1,17},{17,1},{2,18},{18,2},{3,19},{19,3},{4,20},{20... | collective-permute-start | bytes 960008 | tf_op jit(solution)/shard_map/ppermute | solution.py:337
  78.3 1.7 %collective-permute-start.28 = (bf16[1,200,800]{2,1,0:T(8,128)(2,1)S(1)}, bf16[1,200,800]{2,1,0:T(8,128)(2,1)S(1)}, u32[]{:S(2)}, u32[]{:S(2)}) collective-permute-start(bf16[1,200,800]{2,1,0:T(8,128)(2,1)S(1)} %collective-permute-done.22.refs_0_), channel_id=1, source_target_pairs={{0,1},{1,0},{2,3},{3,2},{4,5},{5,4},{6,7},{7,6},{8,9},{9,8},{10,11... | collective-permute-start | bytes 960008 | tf_op jit(solution)/shard_map/ppermute | solution.py:336
  78.3 2.2 %collective-permute-start.29 = (bf16[1,200,800]{2,1,0:T(8,128)(2,1)S(1)}, bf16[1,200,800]{2,1,0:T(8,128)(2,1)S(1)}, u32[]{:S(2)}, u32[]{:S(2)}) collective-permute-start(bf16[1,200,800]{2,1,0:T(8,128)(2,1)S(1)} %collective-permute-done.23.refs_2_), channel_id=1, source_target_pairs={{0,1},{1,0},{2,3},{3,2},{4,5},{5,4},{6,7},{7,6},{8,9},{9,8},{10,11... | collective-permute-start | bytes 960008 | tf_op jit(solution)/shard_map/ppermute | solution.py:336
  78.8 2.2 %collective-permute-start.30 = (bf16[1,200,800]{2,1,0:T(8,128)(2,1)S(1)}, bf16[1,200,800]{2,1,0:T(8,128)(2,1)S(1)}, u32[]{:S(2)}, u32[]{:S(2)}) collective-permute-start(bf16[1,200,800]{2,1,0:T(8,128)(2,1)S(1)} %collective-permute-done.24.refs_4_), channel_id=1, source_target_pairs={{0,1},{1,0},{2,3},{3,2},{4,5},{5,4},{6,7},{7,6},{8,9},{9,8},{10,11... | collective-permute-start | bytes 960008 | tf_op jit(solution)/shard_map/ppermute | solution.py:336
  (4 other events, 61.5 us)

commit v5 on v4

--- a/solution.py
+++ b/solution.py
@@ -12,6 +12,10 @@
 VMEM = 60 * 1024 * 1024
 SMALL = 12 * 1024 * 1024
 TILE = 8
+LANES = 128
+GROUP = 16
+EDGE = 32
+MINE, THEIRS, BOTH = (0,), (1,), (0, 1)
 
 
 def passed_along(block, axis, distance):
@@ -170,16 +174,16 @@
 
 
 def edge_rows_kernel(above_ref, below_ref, old_ref, out_ref):
-    depths, reach, _, _ = above_ref.shape
-    rows = out_ref.shape[1] - 2 * reach
-
-    def step(n, carry):
-        d, r = n // reach, n % reach
-        put_shifted(out_ref, d, r, above_ref[d, r])
-        put_shifted(out_ref, d, r + rows + reach, below_ref[d, r])
-        return carry
-
-    lax.fori_loop(0, depths * reach, step, 0)
+    depths = out_ref.shape[0] // SHIFTS
+    rows, columns, pixels = out_ref.shape[1] - 2 * REACH, out_ref.shape[2], out_ref.shape[3]
+    tail = pixels - above_ref.shape[1]
+    pieces = columns // EDGE
+    for k in range(depths * REACH):
+        for packed, begin in ((above_ref, 0), (below_ref, rows + REACH)):
+            left = [packed[:EDGE, tail * (k * pieces + j) : tail * (k * pieces + j + 1)] for j in range(pieces)]
+            plane = packed[EDGE + k * columns : EDGE + (k + 1) * columns]
+            plane = jnp.concatenate([plane, jnp.concatenate(left, axis=0)], axis=1)
+            put_shifted(out_ref, k // REACH, begin + k % REACH, plane)
 
 
 def own_rows(volume):
@@ -208,6 +212,86 @@
     )(above, below, copies)
 
 
+def pack_pieces_kernel(scalars, own_ref, a_ref, b_ref):
+    _, part, pair = own_ref.shape
+    pixels = pair // 2
+    wide = pixels // LANES * LANES
+    side = scalars[scalars.shape[0] - 1]
+    for out_ref, half in ((a_ref, side), (b_ref, 1 - side)):
+        w = own_ref[half]
+        out_ref[GROUP:, :wide] = w[:, :wide]
+        out_ref[GROUP:, wide:] = w[:, pixels : pixels + wide]
+        left = jnp.concatenate([w[:, wide:pixels], w[:, pixels + wide :]], axis=1)
+        tail = left.shape[1]
+        groups = -(-part // GROUP)
+        left = jnp.concatenate([left, jnp.zeros((groups * GROUP - part, tail), left.dtype)], axis=0)
+        cut = [left[GROUP * n : GROUP * (n + 1)] for n in range(groups)]
+        cut.append(jnp.zeros((GROUP, 2 * wide - groups * tail), left.dtype))
+        out_ref[:GROUP] = jnp.concatenate(cut, axis=1)
+
+
+def pack_pieces(scalars, own):
+    _, part, pair = own.shape
+    packed = jax.ShapeDtypeStruct((GROUP + part, pair // 2 // LANES * LANES * 2), own.dtype)
+    return pl.pallas_call(
+        pack_pieces_kernel,
+        in_specs=[IN_SMEM, IN_VMEM],
+        out_specs=[IN_VMEM] * 2,
+        out_shape=[pltpu.VMEM(packed.shape, packed.dtype)] * 2,
+        compiler_params=pltpu.CompilerParams(vmem_limit_bytes=SMALL),
+        name="pack_pieces",
+    )(scalars, own)
+
+
+def unpacked(w_ref, n, which, part, pixels):
+    if len(w_ref.shape) == 3:
+        return w_ref[n, :, pixels * which : pixels * (which + 1)]
+    wide = w_ref.shape[1] // 2
+    tail = pixels - wide
+    groups = -(-part // GROUP)
+    first = [w_ref[:GROUP, 2 * tail * k + tail * which : 2 * tail * k + tail * (which + 1)] for k in range(groups)]
+    left = jnp.concatenate(first, axis=0)[:part]
+    return jnp.concatenate([w_ref[GROUP:, wide * which : wide * (which + 1)], left], axis=1)
+
+
+def pack_rows_kernel(volume_ref, last_ref, first_ref, held, sems):
+    depths, rows, columns, pixels = volume_ref.shape
+    wide = pixels // LANES * LANES
+    begins = (rows - REACH, 0)
+    fetch = [
+        pltpu.make_async_copy(volume_ref.at[:, pl.ds(begin, REACH)], held.at[n], sems.at[n])
+        for n, begin in enumerate(begins)
+    ]
+    for copy in fetch:
+        copy.start()
+    for n, out_ref in enumerate((last_ref, first_ref)):
+        fetch[n].wait()
+        cut = []
+        for k in range(depths * REACH):
+            plane = held[n, k // REACH, k % REACH]
+            out_ref[EDGE + k * columns : EDGE + (k + 1) * columns] = plane[:, :wide]
+            cut += [plane[EDGE * j : EDGE * (j + 1), wide:] for j in range(columns // EDGE)]
+        cut.append(jnp.zeros((EDGE, wide - len(cut) * (pixels - wide)), volume_ref.dtype))
+        out_ref[:EDGE] = jnp.concatenate(cut, axis=1)
+
+
+def pack_rows(volume):
+    depths, _, columns, pixels = volume.shape
+    shape = (EDGE + depths * REACH * columns, pixels // LANES * LANES)
+    return pl.pallas_call(
+        pack_rows_kernel,
+        in_specs=[pl.BlockSpec(memory_space=pltpu.HBM)],
+        out_specs=[IN_VMEM] * 2,
+        out_shape=[pltpu.VMEM(shape, volume.dtype)] * 2,
+        scratch_shapes=[
+            pltpu.VMEM((2, depths, REACH, columns, pixels), volume.dtype),
+            pltpu.SemaphoreType.DMA((2,)),
+        ],
+        compiler_params=pltpu.CompilerParams(vmem_limit_bytes=SMALL),
+        name="pack_rows",
+    )(pltpu.with_memory_space_constraint(volume, pltpu.HBM))
+
+
 def operator_spot(scalars, op, depths):
     end, depth = jnp.int32(0), jnp.int32(0)
     for d in range(depths):
@@ -218,8 +302,8 @@
 
 
 def add_kernel(scalars, copies, *refs, plan, pieces, first, last):
-    weights = refs[: 2 * pieces]
-    refs = refs[2 * pieces :]
+    weights = refs[:pieces]
+    refs = refs[pieces:]
     if last:
         meas, dark, old, pred_out, ratio_out, acc, pred, ratio, sems = refs
     elif first:
@@ -232,24 +316,24 @@
     rows = lines // columns
     here, side = scalars[scalars.shape[0] - 2], scalars[scalars.shape[0] - 1]
     dims = (((1,), (1,)), ((), ()))
-    jobs = []
-    for n, (hops, other, kind) in enumerate(plan):
+    jobs, at = [], 0
+    for n, (hops, other, kind, cores) in enumerate(plan):
         shard = ((here + (16 - 4 * hops)) % 16) ^ (2 * other)
         half = n if kind is None else side ^ kind
-        spots = []
-        for core in range(2):
+        products = []
+        for core in cores:
             for which in range(2):
-                spots.append(operator_spot(scalars, 2 * (shard ^ core) + which, depths))
-        jobs.append((n, half, spots))
+                copy, row = operator_spot(scalars, 2 * (shard ^ core) + which, depths)
+                products.append((at, which, copy, row))
+            at += 1
+        jobs.append((n, half, products))
 
     for t in range(rows // TILE):
         m = slice(t * TILE * columns, (t + 1) * TILE * columns)
-        for n, half, spots in jobs:
+        for n, half, products in jobs:
             total = None
-            for j, (copy, row) in enumerate(spots):
-                w_ref = weights[2 * n + j // 2]
-                w = w_ref[0] if w_ref.shape[0] == 1 else w_ref[n]
-                w = w[:, pixels * (j % 2) : pixels * (j % 2 + 1)]
+            for at, which, copy, row in products:
+                w = unpacked(weights[at], n, which, acc.shape[2], pixels)
                 slab = copies[copy, pl.ds(row + t * TILE, TILE)].reshape(TILE * columns, pixels)
                 part = lax.dot_general(slab, w, dims, preferred_element_type=jnp.float32)
                 total = part if total is None else total + part
@@ -280,7 +364,7 @@
     columns, pixels = copies.shape[2:]
     rows = copies.shape[1] - 2 * REACH
     lines, part = rows * columns, pixels // 2
-    pieces = len(plan)
+    pieces = len(weights)
     operands = [scalars, copies, *weights]
     shape = (2, lines, part)
     scratch, params = [], {}
@@ -337,41 +421,43 @@
     along_x = lambda v: lax.ppermute(v, "frames", [(0, 1), (1, 0)])
 
     own = operator_rows.T.reshape(2, part, 2 * pixels)
-    own_a = lax.dynamic_index_in_dim(own, side, 0)
-    own_b = lax.dynamic_index_in_dim(own, 1 - side, 0)
     both = lambda *pieces: [w for piece in pieces for w in (piece, to_core(piece))]
 
     tied = lax.optimization_barrier
     a, b = 0, 1
-    own_a, own_b, volume = tied((own_a, own_b, volume))
+    scalars, own = tied((scalars, own))
+    own_a, own_b = pack_pieces(scalars, own)
     t1a, y0a = along_z(own_a), along_y(own_a)
-    above = passed_along(volume[:, rows - REACH :], "lenslet", 1)
-    below = passed_along(volume[:, :REACH], "lenslet", -1)
     own_c = to_core(own)
-    volume, scalars, own_b = tied((volume, scalars, own_b))
+    last_rows, first_rows = pack_rows(volume)
+    above, below = passed_along(last_rows, "lenslet", 1), passed_along(first_rows, "lenslet", -1)
     copies = own_rows(volume)
     t1a, y0a, copies = tied((t1a, y0a, copies))
     t2a, y1a, y0b = along_z(t1a), along_y(t1a), along_x(y0a)
     r0 = both(t1a, y0a)
     copies = edge_rows(above, below, copies)
-    acc = add_pieces(scalars, copies, [own, own_c, own, own_c], [(0, 0, None), (0, 0, None)], None)
-    acc = add_pieces(scalars, copies, r0, [(1, 0, a), (0, 1, a)], acc)
+    acc = add_pieces(scalars, copies, [own, own_c, own, own_c], [(0, 0, None, BOTH), (0, 0, None, BOTH)], None)
+    acc = add_pieces(scalars, copies, r0, [(1, 0, a, BOTH), (0, 1, a, BOTH)], acc)
     t2a, y1a, y0b, acc = tied((t2a, y1a, y0b, acc))
     t3a, y2a, y1b = along_z(t2a), along_y(t2a), along_x(y1a)
     r1 = both(t2a, y1a, y0b)
-    acc = add_pieces(scalars, copies, r1, [(2, 0, a), (1, 1, a), (0, 1, b)], acc)
+    acc = add_pieces(scalars, copies, r1, [(2, 0, a, BOTH), (1, 1, a, BOTH), (0, 1, b, BOTH)], acc)
     t3a, y2a, y1b, acc = tied((t3a, y2a, y1b, acc))
     t1b, y3a, t2b = along_z(own_b), along_y(t3a), along_x(t2a)
     r2 = both(t3a, y2a, y1b)
-    acc = add_pieces(scalars, copies, r2, [(3, 0, a), (2, 1, a), (1, 1, b)], acc)
-    t1b, y3a, t2b, acc = tied((t1b, y3a, t2b, acc))
+    acc = add_pieces(scalars, copies, r2, [(3, 0, a, BOTH), (2, 1, a, BOTH), (1, 1, b, BOTH)], acc)
+    t2b, y3a, t1b, acc = tied((t2b, y3a, t1b, acc))
     t3b, y2b, y3b = along_z(t2b), along_y(t2b), along_x(y3a)
     r3 = both(t1b, y3a, t2b)
-    acc = add_pieces(scalars, copies, r3, [(1, 0, b), (3, 1, a), (2, 0, b)], acc)
-    t3b, y2b, y3b, acc = tied((t3b, y2b, y3b, acc))
+    acc = add_pieces(scalars, copies, r3, [(1, 0, b, BOTH), (3, 1, a, BOTH), (2, 0, b, BOTH)], acc)
+    t3b, acc = tied((t3b, acc))
+    y2b, acc = tied((y2b, acc))
+    y3b, acc = tied((y3b, acc))
     r4 = both(t3b, y2b, y3b)
+    acc = add_pieces(scalars, copies, r4[0::2], [(3, 0, b, MINE), (2, 1, b, MINE), (3, 1, b, MINE)], acc)
     final = (measured, dark_level.reshape(1, pixels))
-    return tuple(add_pieces(scalars, copies, r4, [(3, 0, b), (2, 1, b), (3, 1, b)], acc, final))
+    plan = [(3, 0, b, THEIRS), (2, 1, b, THEIRS), (3, 1, b, THEIRS)]
+    return tuple(add_pieces(scalars, copies, r4[1::2], plan, acc, final))
 
 
 def gathered(volume, measured, operator_rows, offset_counts, offset_table, dark_level):

time: 87.7 us -> 84.5 us (0.964)
  waiting for transfers between devices: 18.1 us -> 14.6 us
  Pallas kernels: 30.8 us -> 33.6 us
  local copies, waits for them, and re-layouts: 3.5 us -> 1.99 us
  starting transfers between devices: 33.3 us -> 32.3 us
    pallas_call x0 -> x2, Pallas kernels: none -> 2.12 us  [the longest x1 1.33 us: pack_rows(): pl.pallas_call(pack_rows_kernel, in_specs=[pl.BlockSpec(memory_space=pltp...]
    ppermute x15, waiting for transfers between devices: 2.15 us -> 0.04 us  [exchanged(): to_core = lambda v: lax.ppermute(v, 'lenslet', twin)]
    dynamic_slice x1 -> x0, local copies, waits for them, and re-layouts: 2.01 us -> none  [exchanged(): own_b = lax.dynamic_index_in_dim(own, 1 - side, 0)]
    ppermute x5, waiting for transfers between devices: 15.6 us -> 13.8 us  [exchanged(): along_z = lambda v: lax.ppermute(v, 'lenslet', up)]
    unnamed x11 -> x9, local copies, waits for them, and re-layouts: 0.12 us -> 1.89 us
    slice x1 -> x0, local copies, waits for them, and re-layouts: 1.27 us -> none  [exchanged(): below = passed_along(volume[:, :REACH], 'lenslet', -1)]
    ppermute x5, starting transfers between devices: 9.86 us -> 8.88 us  [exchanged(): along_y = lambda v: lax.ppermute(v, 'lenslet', beside)]
    pallas_call x6 -> x7, Pallas kernels: 25.4 us -> 26 us  [add_pieces(): pl.pallas_call(functools.partial(add_kernel, plan=plan, pieces=pieces, fi...]
  transfers between devices with their start and end apart: 31 -> 31, of which waited for: 7 -> 5; matrix products, arithmetic and copies ran while one was open for 3% -> 0% of each run, Pallas kernels for 28% -> 34%
where the time goes in v5:
time: 84.5 us; the launch traced here: 84.2 us
  Pallas kernels  33.6 us (40%)
  starting transfers between devices  32.3 us (38%)
  waiting for transfers between devices  14.6 us (17%)
  local copies, waits for them, and re-layouts  1.99 us (2%)
  between operations  1.05 us (1%)
    pallas_call x7, Pallas kernels, add_pieces(): pl.pallas_call(functools.partial(add_kernel, plan=plan, pieces=pieces, fi...  26 us
    ppermute x5, waiting for transfers between devices, exchanged(): along_z = lambda v: lax.ppermute(v, 'lenslet', up)  13.8 us
    ppermute x5, starting transfers between devices, exchanged(): along_z = lambda v: lax.ppermute(v, 'lenslet', up)  10.6 us
    ppermute x5, starting transfers between devices, exchanged(): along_y = lambda v: lax.ppermute(v, 'lenslet', beside)  8.88 us
    ppermute x4, starting transfers between devices, exchanged(): along_x = lambda v: lax.ppermute(v, 'frames', [(0, 1), (1, 0)])  5.48 us
    pallas_call x1, Pallas kernels, own_rows(): pl.pallas_call(own_rows_kernel, in_specs=[pl.BlockSpec(memory_space=pltpu...  4.58 us
    ppermute x15, starting transfers between devices, exchanged(): to_core = lambda v: lax.ppermute(v, 'lenslet', twin)  4.14 us
    ppermute x2, starting transfers between devices, passed_along(): return lax.ppermute(block, axis, route)  3.16 us
  transfers between devices with their start and end apart: 31, of which 5 were waited for; matrix products, arithmetic and copies ran while one was open for 0% of the time, Pallas kernels for 34%

profile of v5, /device:TPU:0, one launch (start us, length us, event | category | flops | bytes accessed | tf_op | source)
XLA Modules:
  0.0 84.2 jit_solution(14769393217315254955)
XLA Ops:
  0.6 0.8 copy.15
  1.5 0.7 pad_add_fusion.scalars
  2.7 1.1 %copy-done = bf16[800,400]{0,1:T(8,128)(2,1)S(1)} copy-done((bf16[800,400]{0,1:T(8,128)(2,1)S(1)}, bf16[800,400]{0,1:T(8,128)(2,1)}, u32[]{:S(2)}) %copy-start) | copy-done | bytes 640024
  3.8 0.8 pack_pieces.1
  4.6 2.6 %collective-permute-start.2 = (bf16[216,768]{1,0:T(8,128)(2,1)S(1)}, bf16[216,768]{1,0:T(8,128)(2,1)S(1)}, u32[]{:S(2)}, u32[]{:S(2)}) collective-permute-start(bf16[216,768]{1,0:T(8,128)(2,1)S(1)} %get-tuple-element.33), channel_id=1, source_target_pairs={{0,4},{1,5},{2,6},{3,7},{4,8},{5,9},{6,10},{7,11},{8,12},{9,13},{1... | collective-permute-start | bytes 995336 | tf_op jit(solution)/shard_map/ppermute | solution.py:418
  7.2 1.5 %collective-permute-start.3 = (bf16[216,768]{1,0:T(8,128)(2,1)S(1)}, bf16[216,768]{1,0:T(8,128)(2,1)S(1)}, u32[]{:S(2)}, u32[]{:S(2)}) collective-permute-start(bf16[216,768]{1,0:T(8,128)(2,1)S(1)} %get-tuple-element.33), channel_id=1, source_target_pairs={{0,2},{1,3},{2,0},{3,1},{4,6},{5,7},{6,4},{7,5},{8,10},{9,11},{10,... | collective-permute-start | bytes 995336 | tf_op jit(solution)/shard_map/ppermute | solution.py:419
  8.8 1.3 %pack_rows.1 = (bf16[544,384]{1,0:T(8,128)(2,1)S(1)}, bf16[544,384]{1,0:T(8,128)(2,1)S(1)}) custom-call(bf16[4,16,64,400]{3,2,1,0:T(8,128)(2,1)} %volume_ref.3), custom_call_target="tpu_custom_call" | custom-call | tf_op jit(solution)/shard_map/pack_rows/pallas_call | solution.py:281
  10.1 1.9 %collective-permute-start = (bf16[544,384]{1,0:T(8,128)(2,1)S(1)}, bf16[544,384]{1,0:T(8,128)(2,1)S(1)}, u32[]{:S(2)}, u32[]{:S(2)}) collective-permute-start(bf16[544,384]{1,0:T(8,128)(2,1)S(1)} %get-tuple-element.30), channel_id=1, source_target_pairs={{0,1},{1,2},{2,3},{3,4},{4,5},{5,6},{6,7},{7,8},{8,9},{9,10},{10,1... | collective-permute-start | bytes 1253384 | tf_op jit(solution)/shard_map/ppermute | solution.py:24
  12.0 1.3 %collective-permute-start.1 = (bf16[544,384]{1,0:T(8,128)(2,1)S(1)}, bf16[544,384]{1,0:T(8,128)(2,1)S(1)}, u32[]{:S(2)}, u32[]{:S(2)}) collective-permute-start(bf16[544,384]{1,0:T(8,128)(2,1)S(1)} %get-tuple-element.31), channel_id=1, source_target_pairs={{1,0},{2,1},{3,2},{4,3},{5,4},{6,5},{7,6},{8,7},{9,8},{10,9},{11,1... | collective-permute-start | bytes 1253384 | tf_op jit(solution)/shard_map/ppermute | solution.py:24
  13.3 4.6 %own_rows.1.old_ref = bf16[20,20,64,400]{3,2,1,0:T(8,128)(2,1)S(1)} custom-call(bf16[4,16,64,400]{3,2,1,0:T(8,128)(2,1)} %volume_ref.3), custom_call_target="tpu_custom_call" | custom-call | tf_op jit(solution)/shard_map/own_rows/pallas_call | solution.py:192
  17.9 1.4 %collective-permute-start.7 = (bf16[216,768]{1,0:T(8,128)(2,1)S(1)}, bf16[216,768]{1,0:T(8,128)(2,1)S(1)}, u32[]{:S(2)}, u32[]{:S(2)}) collective-permute-start(bf16[216,768]{1,0:T(8,128)(2,1)S(1)} %collective-permute-done.2.refs_0_), channel_id=1, source_target_pairs={{0,1},{1,0},{2,3},{3,2},{4,5},{5,4},{6,7},{7,6},{8,9},{9,8},{10,11... | collective-permute-start | bytes 995336 | tf_op jit(solution)/shard_map/ppermute | solution.py:420
  19.3 4.4 %collective-permute-start.4 = (bf16[216,768]{1,0:T(8,128)(2,1)S(1)}, bf16[216,768]{1,0:T(8,128)(2,1)S(1)}, u32[]{:S(2)}, u32[]{:S(2)}) collective-permute-start(bf16[216,768]{1,0:T(8,128)(2,1)S(1)} %collective-permute-done.2.refs_0_), channel_id=1, source_target_pairs={{0,4},{1,5},{2,6},{3,7},{4,8},{5,9},{6,10},{7,11},{8,12},{9,13},{1... | collective-permute-start | bytes 995336 | tf_op jit(solution)/shard_map/ppermute | solution.py:418
  23.7 5.5 %collective-permute-start.5 = (bf16[216,768]{1,0:T(8,128)(2,1)S(1)}, bf16[216,768]{1,0:T(8,128)(2,1)S(1)}, u32[]{:S(2)}, u32[]{:S(2)}) collective-permute-start(bf16[216,768]{1,0:T(8,128)(2,1)S(1)} %collective-permute-done.2.refs_0_), channel_id=1, source_target_pairs={{0,2},{1,3},{2,0},{3,1},{4,6},{5,7},{6,4},{7,5},{8,10},{9,11},{10,... | collective-permute-start | bytes 995336 | tf_op jit(solution)/shard_map/ppermute | solution.py:419
  29.2 0.9 %edge_rows.1.copies = bf16[20,20,64,400]{3,2,1,0:T(8,128)(2,1)S(1)} custom-call(bf16[544,384]{1,0:T(8,128)(2,1)S(1)} %collective-permute-done.above_ref, bf16[544,384]{1,0:T(8,128)(2,1)S(1)} %collective-permute-done.1.below_ref, bf16[20,20,64,400]{3,2,1,0:T(8,128)(2,1)S(1)} %own_rows.1.old_ref), custom_call_target="tpu_custom_call", output_to_operand_aliasing={{}: (2, {})} | custom-call | tf_op jit(solution)/shard_map/edge_rows/pallas_call | solution.py:204
  30.1 1.6 %collective-permute-start.6 = (bf16[216,768]{1,0:T(8,128)(2,1)S(1)}, bf16[216,768]{1,0:T(8,128)(2,1)S(1)}, u32[]{:S(2)}, u32[]{:S(2)}) collective-permute-start(bf16[216,768]{1,0:T(8,128)(2,1)S(1)} %collective-permute-done.3.refs_2_), channel_id=1, source_target_pairs={{0,16},{16,0},{1,17},{17,1},{2,18},{18,2},{3,19},{19,3},{4,20},{20... | collective-permute-start | bytes 995336 | tf_op jit(solution)/shard_map/ppermute | solution.py:421
  31.7 3.0 %add_pieces.7.refs_4_ = f32[2,1024,200]{2,1,0:T(8,128)S(1)} custom-call(s32[70]{0:T(128)S(1)} %pad_add_fusion.scalars, bf16[20,20,64,400]{3,2,1,0:T(8,128)(2,1)S(1)} %edge_rows.1.copies, bf16[2,200,800]{2,1,0:T(8,128)(2,1)S(1)} %bitcast.8, bf16[2,200,800]{2,1,0:T(8,128)(2,1)S(1)} %collective-permute-done.9.refs_1_.refs_3_, bf16[2,200,800]{2,1,0:T(8,128)(2,1)S(1)} %bitcast.9, ...), custom_call_target="tpu_custom_call" | custom-call | flops 2621440000 | bytes 4194304 | tf_op jit(solution)/shard_map/add_pieces/pallas_call | solution.py:385
  34.7 3.1 %add_pieces.8.refs_6_ = f32[2,1024,200]{2,1,0:T(8,128)S(1)} custom-call(s32[70]{0:T(128)S(1)} %pad_add_fusion.scalars, bf16[20,20,64,400]{3,2,1,0:T(8,128)(2,1)S(1)} %edge_rows.1.copies, bf16[216,768]{1,0:T(8,128)(2,1)S(1)} %collective-permute-done.2.refs_0_, bf16[216,768]{1,0:T(8,128)(2,1)S(1)} %collective-permute-done.7.refs_1_, ...), custom_call_target="tpu_custom_call", output_to_operand_aliasing={{}: (6, {})} | custom-call | flops 2621440000 | bytes 4194304 | tf_op jit(solution)/shard_map/add_pieces/pallas_call | solution.py:385
  38.4 1.6 %collective-permute-start.11 = (bf16[216,768]{1,0:T(8,128)(2,1)S(1)}, bf16[216,768]{1,0:T(8,128)(2,1)S(1)}, u32[]{:S(2)}, u32[]{:S(2)}) collective-permute-start(bf16[216,768]{1,0:T(8,128)(2,1)S(1)} %collective-permute-done.4.refs_0_), channel_id=1, source_target_pairs={{0,4},{1,5},{2,6},{3,7},{4,8},{5,9},{6,10},{7,11},{8,12},{9,13},{1... | collective-permute-start | bytes 995336 | tf_op jit(solution)/shard_map/ppermute | solution.py:418
  40.0 1.1 %collective-permute-start.12 = (bf16[216,768]{1,0:T(8,128)(2,1)S(1)}, bf16[216,768]{1,0:T(8,128)(2,1)S(1)}, u32[]{:S(2)}, u32[]{:S(2)}) collective-permute-start(bf16[216,768]{1,0:T(8,128)(2,1)S(1)} %collective-permute-done.4.refs_0_), channel_id=1, source_target_pairs={{0,2},{1,3},{2,0},{3,1},{4,6},{5,7},{6,4},{7,5},{8,10},{9,11},{10,... | collective-permute-start | bytes 995336 | tf_op jit(solution)/shard_map/ppermute | solution.py:419
  41.1 1.5 %collective-permute-start.13 = (bf16[216,768]{1,0:T(8,128)(2,1)S(1)}, bf16[216,768]{1,0:T(8,128)(2,1)S(1)}, u32[]{:S(2)}, u32[]{:S(2)}) collective-permute-start(bf16[216,768]{1,0:T(8,128)(2,1)S(1)} %collective-permute-done.5.refs_2_), channel_id=1, source_target_pairs={{0,16},{16,0},{1,17},{17,1},{2,18},{18,2},{3,19},{19,3},{4,20},{20... | collective-permute-start | bytes 995336 | tf_op jit(solution)/shard_map/ppermute | solution.py:421
  42.6 4.2 %add_pieces.9.refs_6_ = f32[2,1024,200]{2,1,0:T(8,128)S(1)} custom-call(s32[70]{0:T(128)S(1)} %pad_add_fusion.scalars, bf16[20,20,64,400]{3,2,1,0:T(8,128)(2,1)S(1)} %edge_rows.1.copies, bf16[216,768]{1,0:T(8,128)(2,1)S(1)} %collective-permute-done.4.refs_0_, bf16[216,768]{1,0:T(8,128)(2,1)S(1)} %collective-permute-done.14.refs_1_, ...), custom_call_target="tpu_custom_call", output_to_operand_aliasing={{}: (8, {})} | custom-call | flops 3932160000 | bytes 6291456 | tf_op jit(solution)/shard_map/add_pieces/pallas_call | solution.py:385
  46.8 3.6 %collective-permute-done.11.refs_0_ = bf16[216,768]{1,0:T(8,128)(2,1)S(1)} collective-permute-done((bf16[216,768]{1,0:T(8,128)(2,1)S(1)}, bf16[216,768]{1,0:T(8,128)(2,1)S(1)}, u32[]{:S(2)}, u32[]{:S(2)}) %collective-permute-start.11) | collective-permute-done | bytes 331808 | tf_op jit(solution)/shard_map/ppermute | solution.py:418
  51.2 1.2 %collective-permute-start.18 = (bf16[216,768]{1,0:T(8,128)(2,1)S(1)}, bf16[216,768]{1,0:T(8,128)(2,1)S(1)}, u32[]{:S(2)}, u32[]{:S(2)}) collective-permute-start(bf16[216,768]{1,0:T(8,128)(2,1)S(1)} %get-tuple-element.42), channel_id=1, source_target_pairs={{0,4},{1,5},{2,6},{3,7},{4,8},{5,9},{6,10},{7,11},{8,12},{9,13},{1... | collective-permute-start | bytes 995336 | tf_op jit(solution)/shard_map/ppermute | solution.py:418
  52.5 1.5 %collective-permute-start.10 = (bf16[216,768]{1,0:T(8,128)(2,1)S(1)}, bf16[216,768]{1,0:T(8,128)(2,1)S(1)}, u32[]{:S(2)}, u32[]{:S(2)}) collective-permute-start(bf16[216,768]{1,0:T(8,128)(2,1)S(1)} %collective-permute-done.4.refs_0_), channel_id=1, source_target_pairs={{0,16},{16,0},{1,17},{17,1},{2,18},{18,2},{3,19},{19,3},{4,20},{20... | collective-permute-start | bytes 995336 | tf_op jit(solution)/shard_map/ppermute | solution.py:421
  54.3 4.2 %add_pieces.10.refs_6_ = f32[2,1024,200]{2,1,0:T(8,128)S(1)} custom-call(s32[70]{0:T(128)S(1)} %pad_add_fusion.scalars, bf16[20,20,64,400]{3,2,1,0:T(8,128)(2,1)S(1)} %edge_rows.1.copies, bf16[216,768]{1,0:T(8,128)(2,1)S(1)} %collective-permute-done.11.refs_0_, bf16[216,768]{1,0:T(8,128)(2,1)S(1)} %collective-permute-done.19.refs_1_, ...), custom_call_target="tpu_custom_call", output_to_operand_aliasing={{}: (8, {})} | custom-call | flops 3932160000 | bytes 6291456 | tf_op jit(solution)/shard_map/add_pieces/pallas_call | solution.py:385
  58.5 4.7 %collective-permute-done.18.refs_0_ = bf16[216,768]{1,0:T(8,128)(2,1)S(1)} collective-permute-done((bf16[216,768]{1,0:T(8,128)(2,1)S(1)}, bf16[216,768]{1,0:T(8,128)(2,1)S(1)}, u32[]{:S(2)}, u32[]{:S(2)}) %collective-permute-start.18) | collective-permute-done | bytes 331808 | tf_op jit(solution)/shard_map/ppermute | solution.py:418
  64.1 0.8 collective-permute-start.22
  65.5 0.9 %collective-permute-start.29 = (bf16[216,768]{1,0:T(8,128)(2,1)S(1)}, bf16[216,768]{1,0:T(8,128)(2,1)S(1)}, u32[]{:S(2)}, u32[]{:S(2)}) collective-permute-start(bf16[216,768]{1,0:T(8,128)(2,1)S(1)} %collective-permute-done.17.refs_2_), channel_id=1, source_target_pairs={{0,16},{16,0},{1,17},{17,1},{2,18},{18,2},{3,19},{19,3},{4,20},{20... | collective-permute-start | bytes 995336 | tf_op jit(solution)/shard_map/ppermute | solution.py:421
  66.4 4.2 %add_pieces.11.refs_3_ = f32[2,1024,200]{2,1,0:T(8,128)S(1)} custom-call(s32[70]{0:T(128)S(1)} %pad_add_fusion.scalars, bf16[20,20,64,400]{3,2,1,0:T(8,128)(2,1)S(1)} %edge_rows.1.copies, bf16[216,768]{1,0:T(8,128)(2,1)S(1)} %collective-permute-done.18.refs_0_, bf16[216,768]{1,0:T(8,128)(2,1)S(1)} %collective-permute-done.23.refs_1_, ...), custom_call_target="tpu_custom_call", output_to_operand_aliasing={{}: (8, {})} | custom-call | flops 3932160000 | bytes 6291456 | tf_op jit(solution)/shard_map/add_pieces/pallas_call | solution.py:385
  70.7 5.5 %collective-permute-done.22.refs_0_ = bf16[216,768]{1,0:T(8,128)(2,1)S(1)} collective-permute-done((bf16[216,768]{1,0:T(8,128)(2,1)S(1)}, bf16[216,768]{1,0:T(8,128)(2,1)S(1)}, u32[]{:S(2)}, u32[]{:S(2)}) %collective-permute-start.22) | collective-permute-done | bytes 331808 | tf_op jit(solution)/shard_map/ppermute | solution.py:418
  76.7 2.6 %add_pieces.12.refs_5_ = f32[2,1024,200]{2,1,0:T(8,128)S(1)} custom-call(s32[70]{0:T(128)S(1)} %pad_add_fusion.scalars, bf16[20,20,64,400]{3,2,1,0:T(8,128)(2,1)S(1)} %edge_rows.1.copies, bf16[216,768]{1,0:T(8,128)(2,1)S(1)} %collective-permute-done.22.refs_0_, bf16[216,768]{1,0:T(8,128)(2,1)S(1)} %collective-permute-done.27.refs_1_, ...), custom_call_target="tpu_custom_call", output_to_operand_aliasing={{}: (5, {})} | custom-call | flops 1966080000 | bytes 3145728 | tf_op jit(solution)/shard_map/add_pieces/pallas_call | solution.py:385
  79.4 4.6 %add_pieces.13 = (f32[16,64,400]{2,1,0:T(8,128)}, f32[16,64,400]{2,1,0:T(8,128)}) custom-call(s32[70]{0:T(128)S(1)} %pad_add_fusion.scalars, bf16[20,20,64,400]{3,2,1,0:T(8,128)(2,1)S(1)} %edge_rows.1.copies, bf16[216,768]{1,0:T(8,128)(2,1)S(1)} %collective-permute-done.26.refs_0_, bf16[216,768]{1,0:T(8,128)(2,1)S(1)} %collective-permute-done.28.refs_1_, ...), custom_call_target="tpu_custom_call" | custom-call | flops 1966080000 | bytes 3145728 | tf_op jit(solution)/shard_map/add_pieces/pallas_call | solution.py:385
  (52 shorter events, 4.5 us)
Async XLA Ops:
  2.2 27.9 %collective-permute-start.9 = (bf16[2,200,800]{2,1,0:T(8,128)(2,1)}, bf16[2,200,800]{2,1,0:T(8,128)(2,1)S(1)}, u32[]{:S(2)}, u32[]{:S(2)}) collective-permute-start(bf16[2,200,800]{2,1,0:T(8,128)(2,1)} %bitcast.6), channel_id=1, source_target_pairs={{0,1},{1,0},{2,3},{3,2},{4,5},{5,4},{6,7},{7,6},{8,9},{9,8},{10,11... | collective-permute-start | bytes 1920008 | tf_op jit(solution)/shard_map/ppermute | solution.py:420
  4.6 13.3 %collective-permute-start.2 = (bf16[216,768]{1,0:T(8,128)(2,1)S(1)}, bf16[216,768]{1,0:T(8,128)(2,1)S(1)}, u32[]{:S(2)}, u32[]{:S(2)}) collective-permute-start(bf16[216,768]{1,0:T(8,128)(2,1)S(1)} %get-tuple-element.33), channel_id=1, source_target_pairs={{0,4},{1,5},{2,6},{3,7},{4,8},{5,9},{6,10},{7,11},{8,12},{9,13},{1... | collective-permute-start | bytes 995336 | tf_op jit(solution)/shard_map/ppermute | solution.py:418
  7.2 10.6 %collective-permute-start.3 = (bf16[216,768]{1,0:T(8,128)(2,1)S(1)}, bf16[216,768]{1,0:T(8,128)(2,1)S(1)}, u32[]{:S(2)}, u32[]{:S(2)}) collective-permute-start(bf16[216,768]{1,0:T(8,128)(2,1)S(1)} %get-tuple-element.33), channel_id=1, source_target_pairs={{0,2},{1,3},{2,0},{3,1},{4,6},{5,7},{6,4},{7,5},{8,10},{9,11},{10,... | collective-permute-start | bytes 995336 | tf_op jit(solution)/shard_map/ppermute | solution.py:419
  10.1 9.2 %collective-permute-start = (bf16[544,384]{1,0:T(8,128)(2,1)S(1)}, bf16[544,384]{1,0:T(8,128)(2,1)S(1)}, u32[]{:S(2)}, u32[]{:S(2)}) collective-permute-start(bf16[544,384]{1,0:T(8,128)(2,1)S(1)} %get-tuple-element.30), channel_id=1, source_target_pairs={{0,1},{1,2},{2,3},{3,4},{4,5},{5,6},{6,7},{7,8},{8,9},{9,10},{10,1... | collective-permute-start | bytes 1253384 | tf_op jit(solution)/shard_map/ppermute | solution.py:24
  12.0 11.8 %collective-permute-start.1 = (bf16[544,384]{1,0:T(8,128)(2,1)S(1)}, bf16[544,384]{1,0:T(8,128)(2,1)S(1)}, u32[]{:S(2)}, u32[]{:S(2)}) collective-permute-start(bf16[544,384]{1,0:T(8,128)(2,1)S(1)} %get-tuple-element.31), channel_id=1, source_target_pairs={{1,0},{2,1},{3,2},{4,3},{5,4},{6,5},{7,6},{8,7},{9,8},{10,9},{11,1... | collective-permute-start | bytes 1253384 | tf_op jit(solution)/shard_map/ppermute | solution.py:24
  17.9 13.8 %copy-start.1 = (bf16[800,400]{0,1:T(8,128)(2,1)S(1)}, bf16[800,400]{0,1:T(8,128)(2,1)}, u32[]{:S(2)}) copy-start(bf16[800,400]{0,1:T(8,128)(2,1)} %param.8) | copy-start | bytes 1920004
  17.9 16.8 %collective-permute-start.7 = (bf16[216,768]{1,0:T(8,128)(2,1)S(1)}, bf16[216,768]{1,0:T(8,128)(2,1)S(1)}, u32[]{:S(2)}, u32[]{:S(2)}) collective-permute-start(bf16[216,768]{1,0:T(8,128)(2,1)S(1)} %collective-permute-done.2.refs_0_), channel_id=1, source_target_pairs={{0,1},{1,0},{2,3},{3,2},{4,5},{5,4},{6,7},{7,6},{8,9},{9,8},{10,11... | collective-permute-start | bytes 995336 | tf_op jit(solution)/shard_map/ppermute | solution.py:420
  19.2 15.4 %collective-permute-start.8 = (bf16[216,768]{1,0:T(8,128)(2,1)S(1)}, bf16[216,768]{1,0:T(8,128)(2,1)S(1)}, u32[]{:S(2)}, u32[]{:S(2)}) collective-permute-start(bf16[216,768]{1,0:T(8,128)(2,1)S(1)} %collective-permute-done.3.refs_2_), channel_id=1, source_target_pairs={{0,1},{1,0},{2,3},{3,2},{4,5},{5,4},{6,7},{7,6},{8,9},{9,8},{10,11... | collective-permute-start | bytes 995336 | tf_op jit(solution)/shard_map/ppermute | solution.py:420
  19.3 18.4 %collective-permute-start.4 = (bf16[216,768]{1,0:T(8,128)(2,1)S(1)}, bf16[216,768]{1,0:T(8,128)(2,1)S(1)}, u32[]{:S(2)}, u32[]{:S(2)}) collective-permute-start(bf16[216,768]{1,0:T(8,128)(2,1)S(1)} %collective-permute-done.2.refs_0_), channel_id=1, source_target_pairs={{0,4},{1,5},{2,6},{3,7},{4,8},{5,9},{6,10},{7,11},{8,12},{9,13},{1... | collective-permute-start | bytes 995336 | tf_op jit(solution)/shard_map/ppermute | solution.py:418
  23.7 14.0 %collective-permute-start.5 = (bf16[216,768]{1,0:T(8,128)(2,1)S(1)}, bf16[216,768]{1,0:T(8,128)(2,1)S(1)}, u32[]{:S(2)}, u32[]{:S(2)}) collective-permute-start(bf16[216,768]{1,0:T(8,128)(2,1)S(1)} %collective-permute-done.2.refs_0_), channel_id=1, source_target_pairs={{0,2},{1,3},{2,0},{3,1},{4,6},{5,7},{6,4},{7,5},{8,10},{9,11},{10,... | collective-permute-start | bytes 995336 | tf_op jit(solution)/shard_map/ppermute | solution.py:419
  30.1 7.7 %collective-permute-start.6 = (bf16[216,768]{1,0:T(8,128)(2,1)S(1)}, bf16[216,768]{1,0:T(8,128)(2,1)S(1)}, u32[]{:S(2)}, u32[]{:S(2)}) collective-permute-start(bf16[216,768]{1,0:T(8,128)(2,1)S(1)} %collective-permute-done.3.refs_2_), channel_id=1, source_target_pairs={{0,16},{16,0},{1,17},{17,1},{2,18},{18,2},{3,19},{19,3},{4,20},{20... | collective-permute-start | bytes 995336 | tf_op jit(solution)/shard_map/ppermute | solution.py:421
  37.8 3.3 %collective-permute-start.14 = (bf16[216,768]{1,0:T(8,128)(2,1)S(1)}, bf16[216,768]{1,0:T(8,128)(2,1)S(1)}, u32[]{:S(2)}, u32[]{:S(2)}) collective-permute-start(bf16[216,768]{1,0:T(8,128)(2,1)S(1)} %collective-permute-done.4.refs_0_), channel_id=1, source_target_pairs={{0,1},{1,0},{2,3},{3,2},{4,5},{5,4},{6,7},{7,6},{8,9},{9,8},{10,11... | collective-permute-start | bytes 995336 | tf_op jit(solution)/shard_map/ppermute | solution.py:420
  37.9 4.7 %collective-permute-start.15 = (bf16[216,768]{1,0:T(8,128)(2,1)S(1)}, bf16[216,768]{1,0:T(8,128)(2,1)S(1)}, u32[]{:S(2)}, u32[]{:S(2)}) collective-permute-start(bf16[216,768]{1,0:T(8,128)(2,1)S(1)} %collective-permute-done.5.refs_2_), channel_id=1, source_target_pairs={{0,1},{1,0},{2,3},{3,2},{4,5},{5,4},{6,7},{7,6},{8,9},{9,8},{10,11... | collective-permute-start | bytes 995336 | tf_op jit(solution)/shard_map/ppermute | solution.py:420
  38.4 4.2 %collective-permute-start.16 = (bf16[216,768]{1,0:T(8,128)(2,1)S(1)}, bf16[216,768]{1,0:T(8,128)(2,1)S(1)}, u32[]{:S(2)}, u32[]{:S(2)}) collective-permute-start(bf16[216,768]{1,0:T(8,128)(2,1)S(1)} %collective-permute-done.6.refs_4_), channel_id=1, source_target_pairs={{0,1},{1,0},{2,3},{3,2},{4,5},{5,4},{6,7},{7,6},{8,9},{9,8},{10,11... | collective-permute-start | bytes 995336 | tf_op jit(solution)/shard_map/ppermute | solution.py:420
  38.4 11.9 %collective-permute-start.11 = (bf16[216,768]{1,0:T(8,128)(2,1)S(1)}, bf16[216,768]{1,0:T(8,128)(2,1)S(1)}, u32[]{:S(2)}, u32[]{:S(2)}) collective-permute-start(bf16[216,768]{1,0:T(8,128)(2,1)S(1)} %collective-permute-done.4.refs_0_), channel_id=1, source_target_pairs={{0,4},{1,5},{2,6},{3,7},{4,8},{5,9},{6,10},{7,11},{8,12},{9,13},{1... | collective-permute-start | bytes 995336 | tf_op jit(solution)/shard_map/ppermute | solution.py:418
  40.0 10.4 %collective-permute-start.12 = (bf16[216,768]{1,0:T(8,128)(2,1)S(1)}, bf16[216,768]{1,0:T(8,128)(2,1)S(1)}, u32[]{:S(2)}, u32[]{:S(2)}) collective-permute-start(bf16[216,768]{1,0:T(8,128)(2,1)S(1)} %collective-permute-done.4.refs_0_), channel_id=1, source_target_pairs={{0,2},{1,3},{2,0},{3,1},{4,6},{5,7},{6,4},{7,5},{8,10},{9,11},{10,... | collective-permute-start | bytes 995336 | tf_op jit(solution)/shard_map/ppermute | solution.py:419
  41.1 9.7 %collective-permute-start.13 = (bf16[216,768]{1,0:T(8,128)(2,1)S(1)}, bf16[216,768]{1,0:T(8,128)(2,1)S(1)}, u32[]{:S(2)}, u32[]{:S(2)}) collective-permute-start(bf16[216,768]{1,0:T(8,128)(2,1)S(1)} %collective-permute-done.5.refs_2_), channel_id=1, source_target_pairs={{0,16},{16,0},{1,17},{17,1},{2,18},{18,2},{3,19},{19,3},{4,20},{20... | collective-permute-start | bytes 995336 | tf_op jit(solution)/shard_map/ppermute | solution.py:421
  50.7 3.2 %collective-permute-start.19 = (bf16[216,768]{1,0:T(8,128)(2,1)S(1)}, bf16[216,768]{1,0:T(8,128)(2,1)S(1)}, u32[]{:S(2)}, u32[]{:S(2)}) collective-permute-start(bf16[216,768]{1,0:T(8,128)(2,1)S(1)} %collective-permute-done.11.refs_0_), channel_id=1, source_target_pairs={{0,1},{1,0},{2,3},{3,2},{4,5},{5,4},{6,7},{7,6},{8,9},{9,8},{10,11... | collective-permute-start | bytes 995336 | tf_op jit(solution)/shard_map/ppermute | solution.py:420
  50.7 3.5 %collective-permute-start.20 = (bf16[216,768]{1,0:T(8,128)(2,1)S(1)}, bf16[216,768]{1,0:T(8,128)(2,1)S(1)}, u32[]{:S(2)}, u32[]{:S(2)}) collective-permute-start(bf16[216,768]{1,0:T(8,128)(2,1)S(1)} %collective-permute-done.12.refs_2_), channel_id=1, source_target_pairs={{0,1},{1,0},{2,3},{3,2},{4,5},{5,4},{6,7},{7,6},{8,9},{9,8},{10,11... | collective-permute-start | bytes 995336 | tf_op jit(solution)/shard_map/ppermute | solution.py:420
  51.2 3.0 %collective-permute-start.21 = (bf16[216,768]{1,0:T(8,128)(2,1)S(1)}, bf16[216,768]{1,0:T(8,128)(2,1)S(1)}, u32[]{:S(2)}, u32[]{:S(2)}) collective-permute-start(bf16[216,768]{1,0:T(8,128)(2,1)S(1)} %collective-permute-done.13.refs_4_), channel_id=1, source_target_pairs={{0,1},{1,0},{2,3},{3,2},{4,5},{5,4},{6,7},{7,6},{8,9},{9,8},{10,11... | collective-permute-start | bytes 995336 | tf_op jit(solution)/shard_map/ppermute | solution.py:420
  51.2 12.0 %collective-permute-start.18 = (bf16[216,768]{1,0:T(8,128)(2,1)S(1)}, bf16[216,768]{1,0:T(8,128)(2,1)S(1)}, u32[]{:S(2)}, u32[]{:S(2)}) collective-permute-start(bf16[216,768]{1,0:T(8,128)(2,1)S(1)} %get-tuple-element.42), channel_id=1, source_target_pairs={{0,4},{1,5},{2,6},{3,7},{4,8},{5,9},{6,10},{7,11},{8,12},{9,13},{1... | collective-permute-start | bytes 995336 | tf_op jit(solution)/shard_map/ppermute | solution.py:418
  52.5 10.8 %collective-permute-start.10 = (bf16[216,768]{1,0:T(8,128)(2,1)S(1)}, bf16[216,768]{1,0:T(8,128)(2,1)S(1)}, u32[]{:S(2)}, u32[]{:S(2)}) collective-permute-start(bf16[216,768]{1,0:T(8,128)(2,1)S(1)} %collective-permute-done.4.refs_0_), channel_id=1, source_target_pairs={{0,16},{16,0},{1,17},{17,1},{2,18},{18,2},{3,19},{19,3},{4,20},{20... | collective-permute-start | bytes 995336 | tf_op jit(solution)/shard_map/ppermute | solution.py:421
  54.0 9.7 %collective-permute-start.17 = (bf16[216,768]{1,0:T(8,128)(2,1)S(1)}, bf16[216,768]{1,0:T(8,128)(2,1)S(1)}, u32[]{:S(2)}, u32[]{:S(2)}) collective-permute-start(bf16[216,768]{1,0:T(8,128)(2,1)S(1)} %collective-permute-done.11.refs_0_), channel_id=1, source_target_pairs={{0,2},{1,3},{2,0},{3,1},{4,6},{5,7},{6,4},{7,5},{8,10},{9,11},{10,... | collective-permute-start | bytes 995336 | tf_op jit(solution)/shard_map/ppermute | solution.py:419
  63.6 1.8 %collective-permute-start.23 = (bf16[216,768]{1,0:T(8,128)(2,1)S(1)}, bf16[216,768]{1,0:T(8,128)(2,1)S(1)}, u32[]{:S(2)}, u32[]{:S(2)}) collective-permute-start(bf16[216,768]{1,0:T(8,128)(2,1)S(1)} %collective-permute-done.18.refs_0_), channel_id=1, source_target_pairs={{0,1},{1,0},{2,3},{3,2},{4,5},{5,4},{6,7},{7,6},{8,9},{9,8},{10,11... | collective-permute-start | bytes 995336 | tf_op jit(solution)/shard_map/ppermute | solution.py:420
  63.6 2.8 %collective-permute-start.24 = (bf16[216,768]{1,0:T(8,128)(2,1)S(1)}, bf16[216,768]{1,0:T(8,128)(2,1)S(1)}, u32[]{:S(2)}, u32[]{:S(2)}) collective-permute-start(bf16[216,768]{1,0:T(8,128)(2,1)S(1)} %collective-permute-done.17.refs_2_), channel_id=1, source_target_pairs={{0,1},{1,0},{2,3},{3,2},{4,5},{5,4},{6,7},{7,6},{8,9},{9,8},{10,11... | collective-permute-start | bytes 995336 | tf_op jit(solution)/shard_map/ppermute | solution.py:420
  64.1 2.3 %collective-permute-start.25 = (bf16[216,768]{1,0:T(8,128)(2,1)S(1)}, bf16[216,768]{1,0:T(8,128)(2,1)S(1)}, u32[]{:S(2)}, u32[]{:S(2)}) collective-permute-start(bf16[216,768]{1,0:T(8,128)(2,1)S(1)} %collective-permute-done.10.refs_4_), channel_id=1, source_target_pairs={{0,1},{1,0},{2,3},{3,2},{4,5},{5,4},{6,7},{7,6},{8,9},{9,8},{10,11... | collective-permute-start | bytes 995336 | tf_op jit(solution)/shard_map/ppermute | solution.py:420
  64.1 12.0 %collective-permute-start.22 = (bf16[216,768]{1,0:T(8,128)(2,1)S(1)}, bf16[216,768]{1,0:T(8,128)(2,1)S(1)}, u32[]{:S(2)}, u32[]{:S(2)}) collective-permute-start(bf16[216,768]{1,0:T(8,128)(2,1)S(1)} %collective-permute-done.10.refs_4_), channel_id=1, source_target_pairs={{0,4},{1,5},{2,6},{3,7},{4,8},{5,9},{6,10},{7,11},{8,12},{9,13},{1... | collective-permute-start | bytes 995336 | tf_op jit(solution)/shard_map/ppermute | solution.py:418
  64.9 11.2 %collective-permute-start.27 = (bf16[216,768]{1,0:T(8,128)(2,1)S(1)}, bf16[216,768]{1,0:T(8,128)(2,1)S(1)}, u32[]{:S(2)}, u32[]{:S(2)}) collective-permute-start(bf16[216,768]{1,0:T(8,128)(2,1)S(1)} %collective-permute-done.10.refs_4_), channel_id=1, source_target_pairs={{0,2},{1,3},{2,0},{3,1},{4,6},{5,7},{6,4},{7,5},{8,10},{9,11},{10,... | collective-permute-start | bytes 995336 | tf_op jit(solution)/shard_map/ppermute | solution.py:419
  65.5 10.7 %collective-permute-start.29 = (bf16[216,768]{1,0:T(8,128)(2,1)S(1)}, bf16[216,768]{1,0:T(8,128)(2,1)S(1)}, u32[]{:S(2)}, u32[]{:S(2)}) collective-permute-start(bf16[216,768]{1,0:T(8,128)(2,1)S(1)} %collective-permute-done.17.refs_2_), channel_id=1, source_target_pairs={{0,16},{16,0},{1,17},{17,1},{2,18},{18,2},{3,19},{19,3},{4,20},{20... | collective-permute-start | bytes 995336 | tf_op jit(solution)/shard_map/ppermute | solution.py:421
  76.2 3.2 %collective-permute-start.30 = (bf16[216,768]{1,0:T(8,128)(2,1)S(1)}, bf16[216,768]{1,0:T(8,128)(2,1)S(1)}, u32[]{:S(2)}, u32[]{:S(2)}) collective-permute-start(bf16[216,768]{1,0:T(8,128)(2,1)S(1)} %collective-permute-done.29.refs_2_), channel_id=1, source_target_pairs={{0,1},{1,0},{2,3},{3,2},{4,5},{5,4},{6,7},{7,6},{8,9},{9,8},{10,11... | collective-permute-start | bytes 995336 | tf_op jit(solution)/shard_map/ppermute | solution.py:420
  76.2 3.2 %collective-permute-start.28 = (bf16[216,768]{1,0:T(8,128)(2,1)S(1)}, bf16[216,768]{1,0:T(8,128)(2,1)S(1)}, u32[]{:S(2)}, u32[]{:S(2)}) collective-permute-start(bf16[216,768]{1,0:T(8,128)(2,1)S(1)} %collective-permute-done.27.refs_1_), channel_id=1, source_target_pairs={{0,1},{1,0},{2,3},{3,2},{4,5},{5,4},{6,7},{7,6},{8,9},{9,8},{10,11... | collective-permute-start | bytes 995336 | tf_op jit(solution)/shard_map/ppermute | solution.py:420
  76.7 2.7 %collective-permute-start.26 = (bf16[216,768]{1,0:T(8,128)(2,1)S(1)}, bf16[216,768]{1,0:T(8,128)(2,1)S(1)}, u32[]{:S(2)}, u32[]{:S(2)}) collective-permute-start(bf16[216,768]{1,0:T(8,128)(2,1)S(1)} %collective-permute-done.22.refs_0_), channel_id=1, source_target_pairs={{0,1},{1,0},{2,3},{3,2},{4,5},{5,4},{6,7},{7,6},{8,9},{9,8},{10,11... | collective-permute-start | bytes 995336 | tf_op jit(solution)/shard_map/ppermute | solution.py:420
  (3 other events, 18.6 us)

commit v6 on v5

--- a/solution.py
+++ b/solution.py
@@ -212,11 +212,11 @@
     )(above, below, copies)
 
 
-def pack_pieces_kernel(scalars, own_ref, a_ref, b_ref):
+def pack_pieces_kernel(side_ref, own_ref, a_ref, b_ref):
     _, part, pair = own_ref.shape
     pixels = pair // 2
     wide = pixels // LANES * LANES
-    side = scalars[scalars.shape[0] - 1]
+    side = side_ref[0]
     for out_ref, half in ((a_ref, side), (b_ref, 1 - side)):
         w = own_ref[half]
         out_ref[GROUP:, :wide] = w[:, :wide]
@@ -230,7 +230,7 @@
         out_ref[:GROUP] = jnp.concatenate(cut, axis=1)
 
 
-def pack_pieces(scalars, own):
+def pack_pieces(side, own):
     _, part, pair = own.shape
     packed = jax.ShapeDtypeStruct((GROUP + part, pair // 2 // LANES * LANES * 2), own.dtype)
     return pl.pallas_call(
@@ -240,7 +240,7 @@
         out_shape=[pltpu.VMEM(packed.shape, packed.dtype)] * 2,
         compiler_params=pltpu.CompilerParams(vmem_limit_bytes=SMALL),
         name="pack_pieces",
-    )(scalars, own)
+    )(side.reshape(1), own)
 
 
 def unpacked(w_ref, n, which, part, pixels):
@@ -328,13 +328,14 @@
             at += 1
         jobs.append((n, half, products))
 
-    for t in range(rows // TILE):
-        m = slice(t * TILE * columns, (t + 1) * TILE * columns)
+    tile = 4 if last else TILE
+    for t in range(rows // tile):
+        m = slice(t * tile * columns, (t + 1) * tile * columns)
         for n, half, products in jobs:
             total = None
             for at, which, copy, row in products:
                 w = unpacked(weights[at], n, which, acc.shape[2], pixels)
-                slab = copies[copy, pl.ds(row + t * TILE, TILE)].reshape(TILE * columns, pixels)
+                slab = copies[copy, pl.ds(row + t * tile, tile)].reshape(tile * columns, pixels)
                 part = lax.dot_general(slab, w, dims, preferred_element_type=jnp.float32)
                 total = part if total is None else total + part
             if first:
@@ -347,15 +348,15 @@
             else:
                 acc[half, m] = acc[half, m] + total if n else old[half, m] + total
         if last:
-            r = slice(t * TILE, (t + 1) * TILE)
-            full = jnp.concatenate([acc[0, m], acc[1, m]], axis=1).reshape(TILE, columns, pixels)
+            r = slice(t * tile, (t + 1) * tile)
+            full = jnp.concatenate([acc[0, m], acc[1, m]], axis=1).reshape(tile, columns, pixels)
             pred[r] = full
             ratio[r] = meas[r] / (full + dark[...].reshape(1, 1, pixels))
             for q, (src, dst) in enumerate(((pred, pred_out), (ratio, ratio_out))):
                 pltpu.make_async_copy(src.at[r], dst.at[r], sems.at[2 * t + q]).start()
     if last:
-        for t in range(rows // TILE):
-            r = slice(t * TILE, (t + 1) * TILE)
+        for t in range(rows // tile):
+            r = slice(t * tile, (t + 1) * tile)
             for q, (src, dst) in enumerate(((pred, pred_out), (ratio, ratio_out))):
                 pltpu.make_async_copy(src.at[r], dst.at[r], sems.at[2 * t + q]).wait()
 
@@ -375,7 +376,7 @@
         out_shape = [jax.ShapeDtypeStruct(full, jnp.float32)] * 2
         out_specs = [IN_HBM] * 2
         scratch = [pltpu.VMEM(shape, jnp.float32), pltpu.VMEM(full, jnp.float32), pltpu.VMEM(full, jnp.float32)]
-        scratch.append(pltpu.SemaphoreType.DMA((2 * (rows // TILE),)))
+        scratch.append(pltpu.SemaphoreType.DMA((2 * (rows // 4),)))
     else:
         out_shape, out_specs = pltpu.VMEM(shape, jnp.float32), IN_VMEM
         if acc is not None:
@@ -425,12 +426,13 @@
 
     tied = lax.optimization_barrier
     a, b = 0, 1
-    scalars, own = tied((scalars, own))
-    own_a, own_b = pack_pieces(scalars, own)
+    own_a, own_b = pack_pieces(side, own)
     t1a, y0a = along_z(own_a), along_y(own_a)
+    t1b = along_z(own_b)
     own_c = to_core(own)
     last_rows, first_rows = pack_rows(volume)
     above, below = passed_along(last_rows, "lenslet", 1), passed_along(first_rows, "lenslet", -1)
+    volume, scalars = tied((volume, scalars))
     copies = own_rows(volume)
     t1a, y0a, copies = tied((t1a, y0a, copies))
     t2a, y1a, y0b = along_z(t1a), along_y(t1a), along_x(y0a)
@@ -438,25 +440,23 @@
     copies = edge_rows(above, below, copies)
     acc = add_pieces(scalars, copies, [own, own_c, own, own_c], [(0, 0, None, BOTH), (0, 0, None, BOTH)], None)
     acc = add_pieces(scalars, copies, r0, [(1, 0, a, BOTH), (0, 1, a, BOTH)], acc)
-    t2a, y1a, y0b, acc = tied((t2a, y1a, y0b, acc))
-    t3a, y2a, y1b = along_z(t2a), along_y(t2a), along_x(y1a)
-    r1 = both(t2a, y1a, y0b)
-    acc = add_pieces(scalars, copies, r1, [(2, 0, a, BOTH), (1, 1, a, BOTH), (0, 1, b, BOTH)], acc)
-    t3a, y2a, y1b, acc = tied((t3a, y2a, y1b, acc))
-    t1b, y3a, t2b = along_z(own_b), along_y(t3a), along_x(t2a)
-    r2 = both(t3a, y2a, y1b)
-    acc = add_pieces(scalars, copies, r2, [(3, 0, a, BOTH), (2, 1, a, BOTH), (1, 1, b, BOTH)], acc)
-    t2b, y3a, t1b, acc = tied((t2b, y3a, t1b, acc))
-    t3b, y2b, y3b = along_z(t2b), along_y(t2b), along_x(y3a)
-    r3 = both(t1b, y3a, t2b)
-    acc = add_pieces(scalars, copies, r3, [(1, 0, b, BOTH), (3, 1, a, BOTH), (2, 0, b, BOTH)], acc)
-    t3b, acc = tied((t3b, acc))
-    y2b, acc = tied((y2b, acc))
-    y3b, acc = tied((y3b, acc))
-    r4 = both(t3b, y2b, y3b)
-    acc = add_pieces(scalars, copies, r4[0::2], [(3, 0, b, MINE), (2, 1, b, MINE), (3, 1, b, MINE)], acc)
+    t2a, y1a, y0b, t1b, acc = tied((t2a, y1a, y0b, t1b, acc))
+    t3a, y2a, t2b = along_z(t2a), along_y(t2a), along_x(t2a)
+    r1 = both(t2a, y1a, y0b, t1b)
+    acc = add_pieces(scalars, copies, r1, [(2, 0, a, BOTH), (1, 1, a, BOTH), (0, 1, b, BOTH), (1, 0, b, BOTH)], acc)
+    t3a, y2a, t2b, acc = tied((t3a, y2a, t2b, acc))
+    t3b, y3a, y1b = along_z(t2b), along_y(t3a), along_x(y1a)
+    r2 = both(t3a, y2a, t2b)
+    acc = add_pieces(scalars, copies, r2, [(3, 0, a, BOTH), (2, 1, a, BOTH), (2, 0, b, BOTH)], acc)
+    t3b, y3a, y1b, acc = tied((t3b, y3a, y1b, acc))
+    y2b, y3b = along_y(t2b), along_x(y3a)
+    r3 = both(t3b, y3a, y1b)
+    acc = add_pieces(scalars, copies, r3, [(3, 0, b, BOTH), (3, 1, a, BOTH), (1, 1, b, BOTH)], acc)
+    y2b, y3b, acc = tied((y2b, y3b, acc))
+    r4 = both(y2b, y3b)
+    acc = add_pieces(scalars, copies, r4[0::2], [(2, 1, b, MINE), (3, 1, b, MINE)], acc)
     final = (measured, dark_level.reshape(1, pixels))
-    plan = [(3, 0, b, THEIRS), (2, 1, b, THEIRS), (3, 1, b, THEIRS)]
+    plan = [(2, 1, b, THEIRS), (3, 1, b, THEIRS)]
     return tuple(add_pieces(scalars, copies, r4[1::2], plan, acc, final))
 
 

time: 84.5 us -> 82.8 us (0.980)
  local copies, waits for them, and re-layouts: 1.99 us -> 0.21 us
  waiting for transfers between devices: 14.6 us -> 13.4 us
  Pallas kernels: 33.6 us -> 34.8 us
    ppermute x5, waiting for transfers between devices: 13.8 us -> 6.02 us  [exchanged(): along_z = lambda v: lax.ppermute(v, 'lenslet', up)]
    ppermute x5, waiting for transfers between devices: 0.38 us -> 3.95 us  [exchanged(): along_y = lambda v: lax.ppermute(v, 'lenslet', beside)]
    ppermute x4, waiting for transfers between devices: 0.34 us -> 3.01 us  [exchanged(): along_x = lambda v: lax.ppermute(v, 'frames', [(0, 1), (1, 0)])]
    unnamed x9, local copies, waits for them, and re-layouts: 1.89 us -> 0.11 us
    ppermute x5, starting transfers between devices: 8.88 us -> 10.5 us  [exchanged(): along_y = lambda v: lax.ppermute(v, 'lenslet', beside)]
    pallas_call x1, Pallas kernels: 0.78 us -> 2.02 us  [pack_pieces(): pl.pallas_call(pack_pieces_kernel, in_specs=[IN_SMEM, IN_VMEM], out_specs...]
  transfers between devices with their start and end apart: 31 -> 31, of which waited for: 5 -> 6; matrix products, arithmetic and copies ran while one was open for 0% -> 0% of each run, Pallas kernels for 34% -> 35%
where the time goes in v6:
time: 82.8 us; the launch traced here: 82.6 us
  Pallas kernels  34.8 us (42%)
  starting transfers between devices  33 us (40%)
  waiting for transfers between devices  13.4 us (16%)
  between operations  1.04 us (1%)
    pallas_call x7, Pallas kernels, add_pieces(): pl.pallas_call(functools.partial(add_kernel, plan=plan, pieces=pieces, fi...  26 us
    ppermute x5, starting transfers between devices, exchanged(): along_y = lambda v: lax.ppermute(v, 'lenslet', beside)  10.5 us
    ppermute x5, starting transfers between devices, exchanged(): along_z = lambda v: lax.ppermute(v, 'lenslet', up)  9.83 us
    ppermute x5, waiting for transfers between devices, exchanged(): along_z = lambda v: lax.ppermute(v, 'lenslet', up)  6.02 us
    ppermute x4, starting transfers between devices, exchanged(): along_x = lambda v: lax.ppermute(v, 'frames', [(0, 1), (1, 0)])  5.01 us
    pallas_call x1, Pallas kernels, own_rows(): pl.pallas_call(own_rows_kernel, in_specs=[pl.BlockSpec(memory_space=pltpu...  4.58 us
    ppermute x15, starting transfers between devices, exchanged(): to_core = lambda v: lax.ppermute(v, 'lenslet', twin)  3.96 us
    ppermute x5, waiting for transfers between devices, exchanged(): along_y = lambda v: lax.ppermute(v, 'lenslet', beside)  3.95 us
  transfers between devices with their start and end apart: 31, of which 6 were waited for; matrix products, arithmetic and copies ran while one was open for 0% of the time, Pallas kernels for 35%

profile of v6, /device:TPU:0, one launch (start us, length us, event | category | flops | bytes accessed | tf_op | source)
XLA Modules:
  0.0 82.6 jit_solution(5106385614973473068)
XLA Ops:
  0.6 2.0 %pack_pieces.1 = (bf16[216,768]{1,0:T(8,128)(2,1)}, bf16[216,768]{1,0:T(8,128)(2,1)S(1)}) custom-call(s32[1]{0:T(128)} %bitcast.1.side_ref, bf16[2,200,800]{2,1,0:T(8,128)(2,1)} %bitcast.3.own_ref.refs_0_.refs_2_), custom_call_target="tpu_custom_call" | custom-call | tf_op jit(solution)/shard_map/pack_pieces/pallas_call | solution.py:236
  2.7 3.0 %collective-permute-start.2 = (bf16[216,768]{1,0:T(8,128)(2,1)}, bf16[216,768]{1,0:T(8,128)(2,1)S(1)}, u32[]{:S(2)}, u32[]{:S(2)}) collective-permute-start(bf16[216,768]{1,0:T(8,128)(2,1)} %get-tuple-element.30), channel_id=1, source_target_pairs={{0,4},{1,5},{2,6},{3,7},{4,8},{5,9},{6,10},{7,11},{8,12},{9,13},{1... | collective-permute-start | bytes 995336 | tf_op jit(solution)/shard_map/ppermute | solution.py:419
  5.7 1.5 %collective-permute-start.3 = (bf16[216,768]{1,0:T(8,128)(2,1)}, bf16[216,768]{1,0:T(8,128)(2,1)S(1)}, u32[]{:S(2)}, u32[]{:S(2)}) collective-permute-start(bf16[216,768]{1,0:T(8,128)(2,1)} %get-tuple-element.30), channel_id=1, source_target_pairs={{0,2},{1,3},{2,0},{3,1},{4,6},{5,7},{6,4},{7,5},{8,10},{9,11},{10,... | collective-permute-start | bytes 995336 | tf_op jit(solution)/shard_map/ppermute | solution.py:420
  7.2 1.3 %pack_rows.1 = (bf16[544,384]{1,0:T(8,128)(2,1)S(1)}, bf16[544,384]{1,0:T(8,128)(2,1)S(1)}) custom-call(bf16[4,16,64,400]{3,2,1,0:T(8,128)(2,1)} %volume_ref.2), custom_call_target="tpu_custom_call" | custom-call | tf_op jit(solution)/shard_map/pack_rows/pallas_call | solution.py:281
  8.5 2.4 %collective-permute-start = (bf16[544,384]{1,0:T(8,128)(2,1)S(1)}, bf16[544,384]{1,0:T(8,128)(2,1)S(1)}, u32[]{:S(2)}, u32[]{:S(2)}) collective-permute-start(bf16[544,384]{1,0:T(8,128)(2,1)S(1)} %get-tuple-element.28), channel_id=1, source_target_pairs={{0,1},{1,2},{2,3},{3,4},{4,5},{5,6},{6,7},{7,8},{8,9},{9,10},{10,1... | collective-permute-start | bytes 1253384 | tf_op jit(solution)/shard_map/ppermute | solution.py:24
  11.0 1.3 %collective-permute-start.1 = (bf16[544,384]{1,0:T(8,128)(2,1)S(1)}, bf16[544,384]{1,0:T(8,128)(2,1)S(1)}, u32[]{:S(2)}, u32[]{:S(2)}) collective-permute-start(bf16[544,384]{1,0:T(8,128)(2,1)S(1)} %get-tuple-element.29), channel_id=1, source_target_pairs={{1,0},{2,1},{3,2},{4,3},{5,4},{6,5},{7,6},{8,7},{9,8},{10,9},{11,1... | collective-permute-start | bytes 1253384 | tf_op jit(solution)/shard_map/ppermute | solution.py:24
  12.6 4.6 %own_rows.1.old_ref = bf16[20,20,64,400]{3,2,1,0:T(8,128)(2,1)S(1)} custom-call(bf16[4,16,64,400]{3,2,1,0:T(8,128)(2,1)} %volume_ref.2), custom_call_target="tpu_custom_call" | custom-call | tf_op jit(solution)/shard_map/own_rows/pallas_call | solution.py:192
  17.2 1.2 %collective-permute-start.8 = (bf16[216,768]{1,0:T(8,128)(2,1)S(1)}, bf16[216,768]{1,0:T(8,128)(2,1)S(1)}, u32[]{:S(2)}, u32[]{:S(2)}) collective-permute-start(bf16[216,768]{1,0:T(8,128)(2,1)S(1)} %collective-permute-done.2.refs_0_), channel_id=1, source_target_pairs={{0,1},{1,0},{2,3},{3,2},{4,5},{5,4},{6,7},{7,6},{8,9},{9,8},{10,11... | collective-permute-start | bytes 995336 | tf_op jit(solution)/shard_map/ppermute | solution.py:421
  18.5 3.6 %collective-permute-start.7 = (bf16[216,768]{1,0:T(8,128)(2,1)S(1)}, bf16[216,768]{1,0:T(8,128)(2,1)S(1)}, u32[]{:S(2)}, u32[]{:S(2)}) collective-permute-start(bf16[216,768]{1,0:T(8,128)(2,1)S(1)} %get-tuple-element.35), channel_id=1, source_target_pairs={{0,4},{1,5},{2,6},{3,7},{4,8},{5,9},{6,10},{7,11},{8,12},{9,13},{1... | collective-permute-start | bytes 995336 | tf_op jit(solution)/shard_map/ppermute | solution.py:419
  22.1 1.6 %collective-permute-start.4 = (bf16[216,768]{1,0:T(8,128)(2,1)S(1)}, bf16[216,768]{1,0:T(8,128)(2,1)S(1)}, u32[]{:S(2)}, u32[]{:S(2)}) collective-permute-start(bf16[216,768]{1,0:T(8,128)(2,1)S(1)} %collective-permute-done.2.refs_0_), channel_id=1, source_target_pairs={{0,4},{1,5},{2,6},{3,7},{4,8},{5,9},{6,10},{7,11},{8,12},{9,13},{1... | collective-permute-start | bytes 995336 | tf_op jit(solution)/shard_map/ppermute | solution.py:419
  23.7 0.9 %edge_rows.1.copies = bf16[20,20,64,400]{3,2,1,0:T(8,128)(2,1)S(1)} custom-call(bf16[544,384]{1,0:T(8,128)(2,1)S(1)} %collective-permute-done.above_ref, bf16[544,384]{1,0:T(8,128)(2,1)S(1)} %collective-permute-done.1.below_ref, bf16[20,20,64,400]{3,2,1,0:T(8,128)(2,1)S(1)} %own_rows.1.old_ref), custom_call_target="tpu_custom_call", output_to_operand_aliasing={{}: (2, {})} | custom-call | tf_op jit(solution)/shard_map/edge_rows/pallas_call | solution.py:204
  24.6 5.2 %collective-permute-start.5 = (bf16[216,768]{1,0:T(8,128)(2,1)S(1)}, bf16[216,768]{1,0:T(8,128)(2,1)S(1)}, u32[]{:S(2)}, u32[]{:S(2)}) collective-permute-start(bf16[216,768]{1,0:T(8,128)(2,1)S(1)} %collective-permute-done.2.refs_0_), channel_id=1, source_target_pairs={{0,2},{1,3},{2,0},{3,1},{4,6},{5,7},{6,4},{7,5},{8,10},{9,11},{10,... | collective-permute-start | bytes 995336 | tf_op jit(solution)/shard_map/ppermute | solution.py:420
  29.8 1.5 %collective-permute-start.6 = (bf16[216,768]{1,0:T(8,128)(2,1)S(1)}, bf16[216,768]{1,0:T(8,128)(2,1)S(1)}, u32[]{:S(2)}, u32[]{:S(2)}) collective-permute-start(bf16[216,768]{1,0:T(8,128)(2,1)S(1)} %collective-permute-done.3.refs_2_), channel_id=1, source_target_pairs={{0,16},{16,0},{1,17},{17,1},{2,18},{18,2},{3,19},{19,3},{4,20},{20... | collective-permute-start | bytes 995336 | tf_op jit(solution)/shard_map/ppermute | solution.py:422
  31.3 3.8 %add_pieces.7.refs_4_ = f32[2,1024,200]{2,1,0:T(8,128)S(1)} custom-call(s32[70]{0:T(128)S(1)} %pad_add_fusion.scalars, bf16[20,20,64,400]{3,2,1,0:T(8,128)(2,1)S(1)} %edge_rows.1.copies, bf16[2,200,800]{2,1,0:T(8,128)(2,1)} %bitcast.3.own_ref.refs_0_.refs_2_, bf16[2,200,800]{2,1,0:T(8,128)(2,1)S(1)} %collective-permute-done.10.refs_1_.refs_3_, ...), custom_call_target="tpu_custom_call" | custom-call | flops 2621440000 | bytes 4194304 | tf_op jit(solution)/shard_map/add_pieces/pallas_call | solution.py:386
  35.1 3.0 %add_pieces.8.refs_8_ = f32[2,1024,200]{2,1,0:T(8,128)S(1)} custom-call(s32[70]{0:T(128)S(1)} %pad_add_fusion.scalars, bf16[20,20,64,400]{3,2,1,0:T(8,128)(2,1)S(1)} %edge_rows.1.copies, bf16[216,768]{1,0:T(8,128)(2,1)S(1)} %collective-permute-done.2.refs_0_, bf16[216,768]{1,0:T(8,128)(2,1)S(1)} %collective-permute-done.8.refs_1_, ...), custom_call_target="tpu_custom_call", output_to_operand_aliasing={{}: (6, {})} | custom-call | flops 2621440000 | bytes 4194304 | tf_op jit(solution)/shard_map/add_pieces/pallas_call | solution.py:386
  39.3 1.0 %collective-permute-start.11 = (bf16[216,768]{1,0:T(8,128)(2,1)S(1)}, bf16[216,768]{1,0:T(8,128)(2,1)S(1)}, u32[]{:S(2)}, u32[]{:S(2)}) collective-permute-start(bf16[216,768]{1,0:T(8,128)(2,1)S(1)} %collective-permute-done.4.refs_0_), channel_id=1, source_target_pairs={{0,4},{1,5},{2,6},{3,7},{4,8},{5,9},{6,10},{7,11},{8,12},{9,13},{1... | collective-permute-start | bytes 995336 | tf_op jit(solution)/shard_map/ppermute | solution.py:419
  40.3 1.0 %collective-permute-start.12 = (bf16[216,768]{1,0:T(8,128)(2,1)S(1)}, bf16[216,768]{1,0:T(8,128)(2,1)S(1)}, u32[]{:S(2)}, u32[]{:S(2)}) collective-permute-start(bf16[216,768]{1,0:T(8,128)(2,1)S(1)} %collective-permute-done.4.refs_0_), channel_id=1, source_target_pairs={{0,2},{1,3},{2,0},{3,1},{4,6},{5,7},{6,4},{7,5},{8,10},{9,11},{10,... | collective-permute-start | bytes 995336 | tf_op jit(solution)/shard_map/ppermute | solution.py:420
  41.3 1.5 %collective-permute-start.13 = (bf16[216,768]{1,0:T(8,128)(2,1)S(1)}, bf16[216,768]{1,0:T(8,128)(2,1)S(1)}, u32[]{:S(2)}, u32[]{:S(2)}) collective-permute-start(bf16[216,768]{1,0:T(8,128)(2,1)S(1)} %collective-permute-done.4.refs_0_), channel_id=1, source_target_pairs={{0,16},{16,0},{1,17},{17,1},{2,18},{18,2},{3,19},{19,3},{4,20},{20... | collective-permute-start | bytes 995336 | tf_op jit(solution)/shard_map/ppermute | solution.py:422
  42.8 5.3 %add_pieces.9.refs_6_ = f32[2,1024,200]{2,1,0:T(8,128)S(1)} custom-call(s32[70]{0:T(128)S(1)} %pad_add_fusion.scalars, bf16[20,20,64,400]{3,2,1,0:T(8,128)(2,1)S(1)} %edge_rows.1.copies, bf16[216,768]{1,0:T(8,128)(2,1)S(1)} %collective-permute-done.4.refs_0_, bf16[216,768]{1,0:T(8,128)(2,1)S(1)} %collective-permute-done.14.refs_1_, ...), custom_call_target="tpu_custom_call", output_to_operand_aliasing={{}: (10, {})} | custom-call | flops 5242880000 | bytes 8388608 | tf_op jit(solution)/shard_map/add_pieces/pallas_call | solution.py:386
  48.1 3.0 %collective-permute-done.11.refs_0_ = bf16[216,768]{1,0:T(8,128)(2,1)S(1)} collective-permute-done((bf16[216,768]{1,0:T(8,128)(2,1)S(1)}, bf16[216,768]{1,0:T(8,128)(2,1)S(1)}, u32[]{:S(2)}, u32[]{:S(2)}) %collective-permute-start.11) | collective-permute-done | bytes 331808 | tf_op jit(solution)/shard_map/ppermute | solution.py:419
  51.7 1.5 %collective-permute-start.21 = (bf16[216,768]{1,0:T(8,128)(2,1)S(1)}, bf16[216,768]{1,0:T(8,128)(2,1)S(1)}, u32[]{:S(2)}, u32[]{:S(2)}) collective-permute-start(bf16[216,768]{1,0:T(8,128)(2,1)S(1)} %collective-permute-done.5.refs_2_), channel_id=1, source_target_pairs={{0,16},{16,0},{1,17},{17,1},{2,18},{18,2},{3,19},{19,3},{4,20},{20... | collective-permute-start | bytes 995336 | tf_op jit(solution)/shard_map/ppermute | solution.py:422
  53.2 0.6 collective-permute-start.19
  53.8 1.7 %collective-permute-start.20 = (bf16[216,768]{1,0:T(8,128)(2,1)S(1)}, bf16[216,768]{1,0:T(8,128)(2,1)S(1)}, u32[]{:S(2)}, u32[]{:S(2)}) collective-permute-start(bf16[216,768]{1,0:T(8,128)(2,1)S(1)} %collective-permute-done.11.refs_0_), channel_id=1, source_target_pairs={{0,2},{1,3},{2,0},{3,1},{4,6},{5,7},{6,4},{7,5},{8,10},{9,11},{10,... | collective-permute-start | bytes 995336 | tf_op jit(solution)/shard_map/ppermute | solution.py:420
  55.5 4.2 %add_pieces.10.refs_6_ = f32[2,1024,200]{2,1,0:T(8,128)S(1)} custom-call(s32[70]{0:T(128)S(1)} %pad_add_fusion.scalars, bf16[20,20,64,400]{3,2,1,0:T(8,128)(2,1)S(1)} %edge_rows.1.copies, bf16[216,768]{1,0:T(8,128)(2,1)S(1)} %collective-permute-done.11.refs_0_, bf16[216,768]{1,0:T(8,128)(2,1)S(1)} %collective-permute-done.22.refs_1_, ...), custom_call_target="tpu_custom_call", output_to_operand_aliasing={{}: (8, {})} | custom-call | flops 3932160000 | bytes 6291456 | tf_op jit(solution)/shard_map/add_pieces/pallas_call | solution.py:386
  59.7 2.1 %collective-permute-done.21.refs_4_ = bf16[216,768]{1,0:T(8,128)(2,1)S(1)} collective-permute-done((bf16[216,768]{1,0:T(8,128)(2,1)S(1)}, bf16[216,768]{1,0:T(8,128)(2,1)S(1)}, u32[]{:S(2)}, u32[]{:S(2)}) %collective-permute-start.21) | collective-permute-done | bytes 331808 | tf_op jit(solution)/shard_map/ppermute | solution.py:422
  61.8 3.0 %collective-permute-done.19.refs_0_ = bf16[216,768]{1,0:T(8,128)(2,1)S(1)} collective-permute-done((bf16[216,768]{1,0:T(8,128)(2,1)S(1)}, bf16[216,768]{1,0:T(8,128)(2,1)S(1)}, u32[]{:S(2)}, u32[]{:S(2)}) %collective-permute-start.19) | collective-permute-done | bytes 331808 | tf_op jit(solution)/shard_map/ppermute | solution.py:419
  65.4 1.1 %collective-permute-start.18 = (bf16[216,768]{1,0:T(8,128)(2,1)S(1)}, bf16[216,768]{1,0:T(8,128)(2,1)S(1)}, u32[]{:S(2)}, u32[]{:S(2)}) collective-permute-start(bf16[216,768]{1,0:T(8,128)(2,1)S(1)} %collective-permute-done.13.refs_4_), channel_id=1, source_target_pairs={{0,2},{1,3},{2,0},{3,1},{4,6},{5,7},{6,4},{7,5},{8,10},{9,11},{10,... | collective-permute-start | bytes 995336 | tf_op jit(solution)/shard_map/ppermute | solution.py:420
  67.4 4.2 %add_pieces.11.refs_2_ = f32[2,1024,200]{2,1,0:T(8,128)S(1)} custom-call(s32[70]{0:T(128)S(1)} %pad_add_fusion.scalars, bf16[20,20,64,400]{3,2,1,0:T(8,128)(2,1)S(1)} %edge_rows.1.copies, bf16[216,768]{1,0:T(8,128)(2,1)S(1)} %collective-permute-done.19.refs_0_, bf16[216,768]{1,0:T(8,128)(2,1)S(1)} %collective-permute-done.26.refs_1_, ...), custom_call_target="tpu_custom_call", output_to_operand_aliasing={{}: (8, {})} | custom-call | flops 3932160000 | bytes 6291456 | tf_op jit(solution)/shard_map/add_pieces/pallas_call | solution.py:386
  71.6 3.9 %collective-permute-done.18.refs_0_ = bf16[216,768]{1,0:T(8,128)(2,1)S(1)} collective-permute-done((bf16[216,768]{1,0:T(8,128)(2,1)S(1)}, bf16[216,768]{1,0:T(8,128)(2,1)S(1)}, u32[]{:S(2)}, u32[]{:S(2)}) %collective-permute-start.18) | collective-permute-done | bytes 331808 | tf_op jit(solution)/shard_map/ppermute | solution.py:420
  75.6 0.9 %collective-permute-done.25.refs_1_ = bf16[216,768]{1,0:T(8,128)(2,1)S(1)} collective-permute-done((bf16[216,768]{1,0:T(8,128)(2,1)S(1)}, bf16[216,768]{1,0:T(8,128)(2,1)S(1)}, u32[]{:S(2)}, u32[]{:S(2)}) %collective-permute-start.25) | collective-permute-done | bytes 331808 | tf_op jit(solution)/shard_map/ppermute | solution.py:422
  76.9 2.0 %add_pieces.12.refs_4_ = f32[2,1024,200]{2,1,0:T(8,128)S(1)} custom-call(s32[70]{0:T(128)S(1)} %pad_add_fusion.scalars, bf16[20,20,64,400]{3,2,1,0:T(8,128)(2,1)S(1)} %edge_rows.1.copies, bf16[216,768]{1,0:T(8,128)(2,1)S(1)} %collective-permute-done.18.refs_0_, bf16[216,768]{1,0:T(8,128)(2,1)S(1)} %collective-permute-done.25.refs_1_, ...), custom_call_target="tpu_custom_call", output_to_operand_aliasing={{}: (4, {})} | custom-call | flops 1310720000 | bytes 2097152 | tf_op jit(solution)/shard_map/add_pieces/pallas_call | solution.py:386
  79.0 3.5 %add_pieces.13 = (f32[16,64,400]{2,1,0:T(8,128)}, f32[16,64,400]{2,1,0:T(8,128)}) custom-call(s32[70]{0:T(128)S(1)} %pad_add_fusion.scalars, bf16[20,20,64,400]{3,2,1,0:T(8,128)(2,1)S(1)} %edge_rows.1.copies, bf16[216,768]{1,0:T(8,128)(2,1)S(1)} %collective-permute-done.29.refs_0_, bf16[216,768]{1,0:T(8,128)(2,1)S(1)} %collective-permute-done.30.refs_1_, ...), custom_call_target="tpu_custom_call" | custom-call | flops 1310720000 | bytes 2097152 | tf_op jit(solution)/shard_map/add_pieces/pallas_call | solution.py:386
  (52 shorter events, 4.1 us)
Async XLA Ops:
  2.7 9.8 %copy-start.3 = (s32[4]{0:T(128)S(1)}, s32[4]{0:T(128)}, u32[]{:S(2)}) copy-start(s32[4]{0:T(128)} %param.9) | copy-start | bytes 52
  2.7 14.5 %collective-permute-start.2 = (bf16[216,768]{1,0:T(8,128)(2,1)}, bf16[216,768]{1,0:T(8,128)(2,1)S(1)}, u32[]{:S(2)}, u32[]{:S(2)}) collective-permute-start(bf16[216,768]{1,0:T(8,128)(2,1)} %get-tuple-element.30), channel_id=1, source_target_pairs={{0,4},{1,5},{2,6},{3,7},{4,8},{5,9},{6,10},{7,11},{8,12},{9,13},{1... | collective-permute-start | bytes 995336 | tf_op jit(solution)/shard_map/ppermute | solution.py:419
  5.7 11.5 %collective-permute-start.3 = (bf16[216,768]{1,0:T(8,128)(2,1)}, bf16[216,768]{1,0:T(8,128)(2,1)S(1)}, u32[]{:S(2)}, u32[]{:S(2)}) collective-permute-start(bf16[216,768]{1,0:T(8,128)(2,1)} %get-tuple-element.30), channel_id=1, source_target_pairs={{0,2},{1,3},{2,0},{3,1},{4,6},{5,7},{6,4},{7,5},{8,10},{9,11},{10,... | collective-permute-start | bytes 995336 | tf_op jit(solution)/shard_map/ppermute | solution.py:420
  7.2 17.4 %collective-permute-start.10 = (bf16[2,200,800]{2,1,0:T(8,128)(2,1)}, bf16[2,200,800]{2,1,0:T(8,128)(2,1)S(1)}, u32[]{:S(2)}, u32[]{:S(2)}) collective-permute-start(bf16[2,200,800]{2,1,0:T(8,128)(2,1)} %bitcast.3.own_ref.refs_0_.refs_2_), channel_id=1, source_target_pairs={{0,1},{1,0},{2,3},{3,2},{4,5},{5,4},{6,7},{7,6},{8,9},{9,8},{10,11... | collective-permute-start | bytes 1920008 | tf_op jit(solution)/shard_map/ppermute | solution.py:421
  8.5 9.9 %collective-permute-start = (bf16[544,384]{1,0:T(8,128)(2,1)S(1)}, bf16[544,384]{1,0:T(8,128)(2,1)S(1)}, u32[]{:S(2)}, u32[]{:S(2)}) collective-permute-start(bf16[544,384]{1,0:T(8,128)(2,1)S(1)} %get-tuple-element.28), channel_id=1, source_target_pairs={{0,1},{1,2},{2,3},{3,4},{4,5},{5,6},{6,7},{7,8},{8,9},{9,10},{10,1... | collective-permute-start | bytes 1253384 | tf_op jit(solution)/shard_map/ppermute | solution.py:24
  11.0 11.1 %collective-permute-start.1 = (bf16[544,384]{1,0:T(8,128)(2,1)S(1)}, bf16[544,384]{1,0:T(8,128)(2,1)S(1)}, u32[]{:S(2)}, u32[]{:S(2)}) collective-permute-start(bf16[544,384]{1,0:T(8,128)(2,1)S(1)} %get-tuple-element.29), channel_id=1, source_target_pairs={{1,0},{2,1},{3,2},{4,3},{5,4},{6,5},{7,6},{8,7},{9,8},{10,9},{11,1... | collective-permute-start | bytes 1253384 | tf_op jit(solution)/shard_map/ppermute | solution.py:24
  17.2 12.6 %collective-permute-start.8 = (bf16[216,768]{1,0:T(8,128)(2,1)S(1)}, bf16[216,768]{1,0:T(8,128)(2,1)S(1)}, u32[]{:S(2)}, u32[]{:S(2)}) collective-permute-start(bf16[216,768]{1,0:T(8,128)(2,1)S(1)} %collective-permute-done.2.refs_0_), channel_id=1, source_target_pairs={{0,1},{1,0},{2,3},{3,2},{4,5},{5,4},{6,7},{7,6},{8,9},{9,8},{10,11... | collective-permute-start | bytes 995336 | tf_op jit(solution)/shard_map/ppermute | solution.py:421
  18.4 16.7 %collective-permute-start.9 = (bf16[216,768]{1,0:T(8,128)(2,1)S(1)}, bf16[216,768]{1,0:T(8,128)(2,1)S(1)}, u32[]{:S(2)}, u32[]{:S(2)}) collective-permute-start(bf16[216,768]{1,0:T(8,128)(2,1)S(1)} %collective-permute-done.3.refs_2_), channel_id=1, source_target_pairs={{0,1},{1,0},{2,3},{3,2},{4,5},{5,4},{6,7},{7,6},{8,9},{9,8},{10,11... | collective-permute-start | bytes 995336 | tf_op jit(solution)/shard_map/ppermute | solution.py:421
  18.5 19.7 %collective-permute-start.7 = (bf16[216,768]{1,0:T(8,128)(2,1)S(1)}, bf16[216,768]{1,0:T(8,128)(2,1)S(1)}, u32[]{:S(2)}, u32[]{:S(2)}) collective-permute-start(bf16[216,768]{1,0:T(8,128)(2,1)S(1)} %get-tuple-element.35), channel_id=1, source_target_pairs={{0,4},{1,5},{2,6},{3,7},{4,8},{5,9},{6,10},{7,11},{8,12},{9,13},{1... | collective-permute-start | bytes 995336 | tf_op jit(solution)/shard_map/ppermute | solution.py:419
  22.1 16.1 %collective-permute-start.4 = (bf16[216,768]{1,0:T(8,128)(2,1)S(1)}, bf16[216,768]{1,0:T(8,128)(2,1)S(1)}, u32[]{:S(2)}, u32[]{:S(2)}) collective-permute-start(bf16[216,768]{1,0:T(8,128)(2,1)S(1)} %collective-permute-done.2.refs_0_), channel_id=1, source_target_pairs={{0,4},{1,5},{2,6},{3,7},{4,8},{5,9},{6,10},{7,11},{8,12},{9,13},{1... | collective-permute-start | bytes 995336 | tf_op jit(solution)/shard_map/ppermute | solution.py:419
  24.6 13.6 %collective-permute-start.5 = (bf16[216,768]{1,0:T(8,128)(2,1)S(1)}, bf16[216,768]{1,0:T(8,128)(2,1)S(1)}, u32[]{:S(2)}, u32[]{:S(2)}) collective-permute-start(bf16[216,768]{1,0:T(8,128)(2,1)S(1)} %collective-permute-done.2.refs_0_), channel_id=1, source_target_pairs={{0,2},{1,3},{2,0},{3,1},{4,6},{5,7},{6,4},{7,5},{8,10},{9,11},{10,... | collective-permute-start | bytes 995336 | tf_op jit(solution)/shard_map/ppermute | solution.py:420
  29.8 8.4 %collective-permute-start.6 = (bf16[216,768]{1,0:T(8,128)(2,1)S(1)}, bf16[216,768]{1,0:T(8,128)(2,1)S(1)}, u32[]{:S(2)}, u32[]{:S(2)}) collective-permute-start(bf16[216,768]{1,0:T(8,128)(2,1)S(1)} %collective-permute-done.3.refs_2_), channel_id=1, source_target_pairs={{0,16},{16,0},{1,17},{17,1},{2,18},{18,2},{3,19},{19,3},{4,20},{20... | collective-permute-start | bytes 995336 | tf_op jit(solution)/shard_map/ppermute | solution.py:422
  38.2 2.1 %collective-permute-start.14 = (bf16[216,768]{1,0:T(8,128)(2,1)S(1)}, bf16[216,768]{1,0:T(8,128)(2,1)S(1)}, u32[]{:S(2)}, u32[]{:S(2)}) collective-permute-start(bf16[216,768]{1,0:T(8,128)(2,1)S(1)} %collective-permute-done.4.refs_0_), channel_id=1, source_target_pairs={{0,1},{1,0},{2,3},{3,2},{4,5},{5,4},{6,7},{7,6},{8,9},{9,8},{10,11... | collective-permute-start | bytes 995336 | tf_op jit(solution)/shard_map/ppermute | solution.py:421
  38.6 2.7 %collective-permute-start.15 = (bf16[216,768]{1,0:T(8,128)(2,1)S(1)}, bf16[216,768]{1,0:T(8,128)(2,1)S(1)}, u32[]{:S(2)}, u32[]{:S(2)}) collective-permute-start(bf16[216,768]{1,0:T(8,128)(2,1)S(1)} %collective-permute-done.5.refs_2_), channel_id=1, source_target_pairs={{0,1},{1,0},{2,3},{3,2},{4,5},{5,4},{6,7},{7,6},{8,9},{9,8},{10,11... | collective-permute-start | bytes 995336 | tf_op jit(solution)/shard_map/ppermute | solution.py:421
  38.8 4.0 %collective-permute-start.16 = (bf16[216,768]{1,0:T(8,128)(2,1)S(1)}, bf16[216,768]{1,0:T(8,128)(2,1)S(1)}, u32[]{:S(2)}, u32[]{:S(2)}) collective-permute-start(bf16[216,768]{1,0:T(8,128)(2,1)S(1)} %collective-permute-done.6.refs_4_), channel_id=1, source_target_pairs={{0,1},{1,0},{2,3},{3,2},{4,5},{5,4},{6,7},{7,6},{8,9},{9,8},{10,11... | collective-permute-start | bytes 995336 | tf_op jit(solution)/shard_map/ppermute | solution.py:421
  39.1 3.7 %collective-permute-start.17 = (bf16[216,768]{1,0:T(8,128)(2,1)S(1)}, bf16[216,768]{1,0:T(8,128)(2,1)S(1)}, u32[]{:S(2)}, u32[]{:S(2)}) collective-permute-start(bf16[216,768]{1,0:T(8,128)(2,1)S(1)} %collective-permute-done.7.refs_6_), channel_id=1, source_target_pairs={{0,1},{1,0},{2,3},{3,2},{4,5},{5,4},{6,7},{7,6},{8,9},{9,8},{10,11... | collective-permute-start | bytes 995336 | tf_op jit(solution)/shard_map/ppermute | solution.py:421
  39.3 11.8 %collective-permute-start.11 = (bf16[216,768]{1,0:T(8,128)(2,1)S(1)}, bf16[216,768]{1,0:T(8,128)(2,1)S(1)}, u32[]{:S(2)}, u32[]{:S(2)}) collective-permute-start(bf16[216,768]{1,0:T(8,128)(2,1)S(1)} %collective-permute-done.4.refs_0_), channel_id=1, source_target_pairs={{0,4},{1,5},{2,6},{3,7},{4,8},{5,9},{6,10},{7,11},{8,12},{9,13},{1... | collective-permute-start | bytes 995336 | tf_op jit(solution)/shard_map/ppermute | solution.py:419
  40.3 10.8 %collective-permute-start.12 = (bf16[216,768]{1,0:T(8,128)(2,1)S(1)}, bf16[216,768]{1,0:T(8,128)(2,1)S(1)}, u32[]{:S(2)}, u32[]{:S(2)}) collective-permute-start(bf16[216,768]{1,0:T(8,128)(2,1)S(1)} %collective-permute-done.4.refs_0_), channel_id=1, source_target_pairs={{0,2},{1,3},{2,0},{3,1},{4,6},{5,7},{6,4},{7,5},{8,10},{9,11},{10,... | collective-permute-start | bytes 995336 | tf_op jit(solution)/shard_map/ppermute | solution.py:420
  41.3 9.8 %collective-permute-start.13 = (bf16[216,768]{1,0:T(8,128)(2,1)S(1)}, bf16[216,768]{1,0:T(8,128)(2,1)S(1)}, u32[]{:S(2)}, u32[]{:S(2)}) collective-permute-start(bf16[216,768]{1,0:T(8,128)(2,1)S(1)} %collective-permute-done.4.refs_0_), channel_id=1, source_target_pairs={{0,16},{16,0},{1,17},{17,1},{2,18},{18,2},{3,19},{19,3},{4,20},{20... | collective-permute-start | bytes 995336 | tf_op jit(solution)/shard_map/ppermute | solution.py:422
  51.1 2.7 %collective-permute-start.22 = (bf16[216,768]{1,0:T(8,128)(2,1)S(1)}, bf16[216,768]{1,0:T(8,128)(2,1)S(1)}, u32[]{:S(2)}, u32[]{:S(2)}) collective-permute-start(bf16[216,768]{1,0:T(8,128)(2,1)S(1)} %collective-permute-done.11.refs_0_), channel_id=1, source_target_pairs={{0,1},{1,0},{2,3},{3,2},{4,5},{5,4},{6,7},{7,6},{8,9},{9,8},{10,11... | collective-permute-start | bytes 995336 | tf_op jit(solution)/shard_map/ppermute | solution.py:421
  51.1 4.4 %collective-permute-start.23 = (bf16[216,768]{1,0:T(8,128)(2,1)S(1)}, bf16[216,768]{1,0:T(8,128)(2,1)S(1)}, u32[]{:S(2)}, u32[]{:S(2)}) collective-permute-start(bf16[216,768]{1,0:T(8,128)(2,1)S(1)} %collective-permute-done.12.refs_2_), channel_id=1, source_target_pairs={{0,1},{1,0},{2,3},{3,2},{4,5},{5,4},{6,7},{7,6},{8,9},{9,8},{10,11... | collective-permute-start | bytes 995336 | tf_op jit(solution)/shard_map/ppermute | solution.py:421
  51.6 3.9 %collective-permute-start.24 = (bf16[216,768]{1,0:T(8,128)(2,1)S(1)}, bf16[216,768]{1,0:T(8,128)(2,1)S(1)}, u32[]{:S(2)}, u32[]{:S(2)}) collective-permute-start(bf16[216,768]{1,0:T(8,128)(2,1)S(1)} %collective-permute-done.13.refs_4_), channel_id=1, source_target_pairs={{0,1},{1,0},{2,3},{3,2},{4,5},{5,4},{6,7},{7,6},{8,9},{9,8},{10,11... | collective-permute-start | bytes 995336 | tf_op jit(solution)/shard_map/ppermute | solution.py:421
  51.7 10.1 %collective-permute-start.21 = (bf16[216,768]{1,0:T(8,128)(2,1)S(1)}, bf16[216,768]{1,0:T(8,128)(2,1)S(1)}, u32[]{:S(2)}, u32[]{:S(2)}) collective-permute-start(bf16[216,768]{1,0:T(8,128)(2,1)S(1)} %collective-permute-done.5.refs_2_), channel_id=1, source_target_pairs={{0,16},{16,0},{1,17},{17,1},{2,18},{18,2},{3,19},{19,3},{4,20},{20... | collective-permute-start | bytes 995336 | tf_op jit(solution)/shard_map/ppermute | solution.py:422
  53.2 11.7 %collective-permute-start.19 = (bf16[216,768]{1,0:T(8,128)(2,1)S(1)}, bf16[216,768]{1,0:T(8,128)(2,1)S(1)}, u32[]{:S(2)}, u32[]{:S(2)}) collective-permute-start(bf16[216,768]{1,0:T(8,128)(2,1)S(1)} %collective-permute-done.13.refs_4_), channel_id=1, source_target_pairs={{0,4},{1,5},{2,6},{3,7},{4,8},{5,9},{6,10},{7,11},{8,12},{9,13},{1... | collective-permute-start | bytes 995336 | tf_op jit(solution)/shard_map/ppermute | solution.py:419
  53.8 11.1 %collective-permute-start.20 = (bf16[216,768]{1,0:T(8,128)(2,1)S(1)}, bf16[216,768]{1,0:T(8,128)(2,1)S(1)}, u32[]{:S(2)}, u32[]{:S(2)}) collective-permute-start(bf16[216,768]{1,0:T(8,128)(2,1)S(1)} %collective-permute-done.11.refs_0_), channel_id=1, source_target_pairs={{0,2},{1,3},{2,0},{3,1},{4,6},{5,7},{6,4},{7,5},{8,10},{9,11},{10,... | collective-permute-start | bytes 995336 | tf_op jit(solution)/shard_map/ppermute | solution.py:420
  64.9 2.2 %collective-permute-start.26 = (bf16[216,768]{1,0:T(8,128)(2,1)S(1)}, bf16[216,768]{1,0:T(8,128)(2,1)S(1)}, u32[]{:S(2)}, u32[]{:S(2)}) collective-permute-start(bf16[216,768]{1,0:T(8,128)(2,1)S(1)} %collective-permute-done.19.refs_0_), channel_id=1, source_target_pairs={{0,1},{1,0},{2,3},{3,2},{4,5},{5,4},{6,7},{7,6},{8,9},{9,8},{10,11... | collective-permute-start | bytes 995336 | tf_op jit(solution)/shard_map/ppermute | solution.py:421
  64.9 2.2 %collective-permute-start.27 = (bf16[216,768]{1,0:T(8,128)(2,1)S(1)}, bf16[216,768]{1,0:T(8,128)(2,1)S(1)}, u32[]{:S(2)}, u32[]{:S(2)}) collective-permute-start(bf16[216,768]{1,0:T(8,128)(2,1)S(1)} %collective-permute-done.20.refs_2_), channel_id=1, source_target_pairs={{0,1},{1,0},{2,3},{3,2},{4,5},{5,4},{6,7},{7,6},{8,9},{9,8},{10,11... | collective-permute-start | bytes 995336 | tf_op jit(solution)/shard_map/ppermute | solution.py:421
  65.4 2.1 %collective-permute-start.28 = (bf16[216,768]{1,0:T(8,128)(2,1)S(1)}, bf16[216,768]{1,0:T(8,128)(2,1)S(1)}, u32[]{:S(2)}, u32[]{:S(2)}) collective-permute-start(bf16[216,768]{1,0:T(8,128)(2,1)S(1)} %collective-permute-done.21.refs_4_), channel_id=1, source_target_pairs={{0,1},{1,0},{2,3},{3,2},{4,5},{5,4},{6,7},{7,6},{8,9},{9,8},{10,11... | collective-permute-start | bytes 995336 | tf_op jit(solution)/shard_map/ppermute | solution.py:421
  65.4 10.2 %collective-permute-start.18 = (bf16[216,768]{1,0:T(8,128)(2,1)S(1)}, bf16[216,768]{1,0:T(8,128)(2,1)S(1)}, u32[]{:S(2)}, u32[]{:S(2)}) collective-permute-start(bf16[216,768]{1,0:T(8,128)(2,1)S(1)} %collective-permute-done.13.refs_4_), channel_id=1, source_target_pairs={{0,2},{1,3},{2,0},{3,1},{4,6},{5,7},{6,4},{7,5},{8,10},{9,11},{10,... | collective-permute-start | bytes 995336 | tf_op jit(solution)/shard_map/ppermute | solution.py:420
  66.5 9.9 %collective-permute-start.25 = (bf16[216,768]{1,0:T(8,128)(2,1)S(1)}, bf16[216,768]{1,0:T(8,128)(2,1)S(1)}, u32[]{:S(2)}, u32[]{:S(2)}) collective-permute-start(bf16[216,768]{1,0:T(8,128)(2,1)S(1)} %collective-permute-done.20.refs_2_), channel_id=1, source_target_pairs={{0,16},{16,0},{1,17},{17,1},{2,18},{18,2},{3,19},{19,3},{4,20},{20... | collective-permute-start | bytes 995336 | tf_op jit(solution)/shard_map/ppermute | solution.py:422
  76.4 2.5 %collective-permute-start.29 = (bf16[216,768]{1,0:T(8,128)(2,1)S(1)}, bf16[216,768]{1,0:T(8,128)(2,1)S(1)}, u32[]{:S(2)}, u32[]{:S(2)}) collective-permute-start(bf16[216,768]{1,0:T(8,128)(2,1)S(1)} %collective-permute-done.18.refs_0_), channel_id=1, source_target_pairs={{0,1},{1,0},{2,3},{3,2},{4,5},{5,4},{6,7},{7,6},{8,9},{9,8},{10,11... | collective-permute-start | bytes 995336 | tf_op jit(solution)/shard_map/ppermute | solution.py:421
  76.4 2.5 %collective-permute-start.30 = (bf16[216,768]{1,0:T(8,128)(2,1)S(1)}, bf16[216,768]{1,0:T(8,128)(2,1)S(1)}, u32[]{:S(2)}, u32[]{:S(2)}) collective-permute-start(bf16[216,768]{1,0:T(8,128)(2,1)S(1)} %collective-permute-done.25.refs_1_), channel_id=1, source_target_pairs={{0,1},{1,0},{2,3},{3,2},{4,5},{5,4},{6,7},{7,6},{8,9},{9,8},{10,11... | collective-permute-start | bytes 995336 | tf_op jit(solution)/shard_map/ppermute | solution.py:421
  (3 other events, 24.3 us)

commit v7 on v6

--- a/solution.py
+++ b/solution.py
@@ -11,7 +11,7 @@
 SHIFTS = 2 * REACH + 1
 VMEM = 60 * 1024 * 1024
 SMALL = 12 * 1024 * 1024
-TILE = 8
+TILE = 16
 LANES = 128
 GROUP = 16
 EDGE = 32

time: 82.8 us -> 82.8 us (level)
  no operation moved by 1% of the time
where the time goes in v7:
time: 82.8 us; the launch traced here: 82.6 us
  Pallas kernels  34.6 us (42%)
  starting transfers between devices  33.1 us (40%)
  waiting for transfers between devices  13.6 us (16%)
  between operations  1.03 us (1%)
    pallas_call x7, Pallas kernels, add_pieces(): pl.pallas_call(functools.partial(add_kernel, plan=plan, pieces=pieces, fi...  25.8 us
    ppermute x5, starting transfers between devices, exchanged(): along_y = lambda v: lax.ppermute(v, 'lenslet', beside)  10.5 us
    ppermute x5, starting transfers between devices, exchanged(): along_z = lambda v: lax.ppermute(v, 'lenslet', up)  9.84 us
    ppermute x5, waiting for transfers between devices, exchanged(): along_z = lambda v: lax.ppermute(v, 'lenslet', up)  6.05 us
    ppermute x4, starting transfers between devices, exchanged(): along_x = lambda v: lax.ppermute(v, 'frames', [(0, 1), (1, 0)])  5.01 us
    pallas_call x1, Pallas kernels, own_rows(): pl.pallas_call(own_rows_kernel, in_specs=[pl.BlockSpec(memory_space=pltpu...  4.58 us
    ppermute x5, waiting for transfers between devices, exchanged(): along_y = lambda v: lax.ppermute(v, 'lenslet', beside)  3.98 us
    ppermute x15, starting transfers between devices, exchanged(): to_core = lambda v: lax.ppermute(v, 'lenslet', twin)  3.96 us
  transfers between devices with their start and end apart: 31, of which 6 were waited for; matrix products, arithmetic and copies ran while one was open for 0% of the time, Pallas kernels for 35%

profile of v7, /device:TPU:0, one launch (start us, length us, event | category | flops | bytes accessed | tf_op | source)
XLA Modules:
  0.0 82.6 jit_solution(2849031823659310048)
XLA Ops:
  0.6 2.0 %pack_pieces.1 = (bf16[216,768]{1,0:T(8,128)(2,1)}, bf16[216,768]{1,0:T(8,128)(2,1)S(1)}) custom-call(s32[1]{0:T(128)} %bitcast.1.side_ref, bf16[2,200,800]{2,1,0:T(8,128)(2,1)} %bitcast.3.own_ref.refs_0_.refs_2_), custom_call_target="tpu_custom_call" | custom-call | tf_op jit(solution)/shard_map/pack_pieces/pallas_call | solution.py:236
  2.7 3.0 %collective-permute-start.2 = (bf16[216,768]{1,0:T(8,128)(2,1)}, bf16[216,768]{1,0:T(8,128)(2,1)S(1)}, u32[]{:S(2)}, u32[]{:S(2)}) collective-permute-start(bf16[216,768]{1,0:T(8,128)(2,1)} %get-tuple-element.30), channel_id=1, source_target_pairs={{0,4},{1,5},{2,6},{3,7},{4,8},{5,9},{6,10},{7,11},{8,12},{9,13},{1... | collective-permute-start | bytes 995336 | tf_op jit(solution)/shard_map/ppermute | solution.py:419
  5.7 1.5 %collective-permute-start.3 = (bf16[216,768]{1,0:T(8,128)(2,1)}, bf16[216,768]{1,0:T(8,128)(2,1)S(1)}, u32[]{:S(2)}, u32[]{:S(2)}) collective-permute-start(bf16[216,768]{1,0:T(8,128)(2,1)} %get-tuple-element.30), channel_id=1, source_target_pairs={{0,2},{1,3},{2,0},{3,1},{4,6},{5,7},{6,4},{7,5},{8,10},{9,11},{10,... | collective-permute-start | bytes 995336 | tf_op jit(solution)/shard_map/ppermute | solution.py:420
  7.2 1.3 %pack_rows.1 = (bf16[544,384]{1,0:T(8,128)(2,1)S(1)}, bf16[544,384]{1,0:T(8,128)(2,1)S(1)}) custom-call(bf16[4,16,64,400]{3,2,1,0:T(8,128)(2,1)} %volume_ref.2), custom_call_target="tpu_custom_call" | custom-call | tf_op jit(solution)/shard_map/pack_rows/pallas_call | solution.py:281
  8.5 2.4 %collective-permute-start = (bf16[544,384]{1,0:T(8,128)(2,1)S(1)}, bf16[544,384]{1,0:T(8,128)(2,1)S(1)}, u32[]{:S(2)}, u32[]{:S(2)}) collective-permute-start(bf16[544,384]{1,0:T(8,128)(2,1)S(1)} %get-tuple-element.28), channel_id=1, source_target_pairs={{0,1},{1,2},{2,3},{3,4},{4,5},{5,6},{6,7},{7,8},{8,9},{9,10},{10,1... | collective-permute-start | bytes 1253384 | tf_op jit(solution)/shard_map/ppermute | solution.py:24
  11.0 1.3 %collective-permute-start.1 = (bf16[544,384]{1,0:T(8,128)(2,1)S(1)}, bf16[544,384]{1,0:T(8,128)(2,1)S(1)}, u32[]{:S(2)}, u32[]{:S(2)}) collective-permute-start(bf16[544,384]{1,0:T(8,128)(2,1)S(1)} %get-tuple-element.29), channel_id=1, source_target_pairs={{1,0},{2,1},{3,2},{4,3},{5,4},{6,5},{7,6},{8,7},{9,8},{10,9},{11,1... | collective-permute-start | bytes 1253384 | tf_op jit(solution)/shard_map/ppermute | solution.py:24
  12.6 4.6 %own_rows.1.old_ref = bf16[20,20,64,400]{3,2,1,0:T(8,128)(2,1)S(1)} custom-call(bf16[4,16,64,400]{3,2,1,0:T(8,128)(2,1)} %volume_ref.2), custom_call_target="tpu_custom_call" | custom-call | tf_op jit(solution)/shard_map/own_rows/pallas_call | solution.py:192
  17.2 1.2 %collective-permute-start.8 = (bf16[216,768]{1,0:T(8,128)(2,1)S(1)}, bf16[216,768]{1,0:T(8,128)(2,1)S(1)}, u32[]{:S(2)}, u32[]{:S(2)}) collective-permute-start(bf16[216,768]{1,0:T(8,128)(2,1)S(1)} %collective-permute-done.2.refs_0_), channel_id=1, source_target_pairs={{0,1},{1,0},{2,3},{3,2},{4,5},{5,4},{6,7},{7,6},{8,9},{9,8},{10,11... | collective-permute-start | bytes 995336 | tf_op jit(solution)/shard_map/ppermute | solution.py:421
  18.5 3.6 %collective-permute-start.7 = (bf16[216,768]{1,0:T(8,128)(2,1)S(1)}, bf16[216,768]{1,0:T(8,128)(2,1)S(1)}, u32[]{:S(2)}, u32[]{:S(2)}) collective-permute-start(bf16[216,768]{1,0:T(8,128)(2,1)S(1)} %get-tuple-element.35), channel_id=1, source_target_pairs={{0,4},{1,5},{2,6},{3,7},{4,8},{5,9},{6,10},{7,11},{8,12},{9,13},{1... | collective-permute-start | bytes 995336 | tf_op jit(solution)/shard_map/ppermute | solution.py:419
  22.1 1.6 %collective-permute-start.4 = (bf16[216,768]{1,0:T(8,128)(2,1)S(1)}, bf16[216,768]{1,0:T(8,128)(2,1)S(1)}, u32[]{:S(2)}, u32[]{:S(2)}) collective-permute-start(bf16[216,768]{1,0:T(8,128)(2,1)S(1)} %collective-permute-done.2.refs_0_), channel_id=1, source_target_pairs={{0,4},{1,5},{2,6},{3,7},{4,8},{5,9},{6,10},{7,11},{8,12},{9,13},{1... | collective-permute-start | bytes 995336 | tf_op jit(solution)/shard_map/ppermute | solution.py:419
  23.7 0.9 %edge_rows.1.copies = bf16[20,20,64,400]{3,2,1,0:T(8,128)(2,1)S(1)} custom-call(bf16[544,384]{1,0:T(8,128)(2,1)S(1)} %collective-permute-done.above_ref, bf16[544,384]{1,0:T(8,128)(2,1)S(1)} %collective-permute-done.1.below_ref, bf16[20,20,64,400]{3,2,1,0:T(8,128)(2,1)S(1)} %own_rows.1.old_ref), custom_call_target="tpu_custom_call", output_to_operand_aliasing={{}: (2, {})} | custom-call | tf_op jit(solution)/shard_map/edge_rows/pallas_call | solution.py:204
  24.6 5.2 %collective-permute-start.5 = (bf16[216,768]{1,0:T(8,128)(2,1)S(1)}, bf16[216,768]{1,0:T(8,128)(2,1)S(1)}, u32[]{:S(2)}, u32[]{:S(2)}) collective-permute-start(bf16[216,768]{1,0:T(8,128)(2,1)S(1)} %collective-permute-done.2.refs_0_), channel_id=1, source_target_pairs={{0,2},{1,3},{2,0},{3,1},{4,6},{5,7},{6,4},{7,5},{8,10},{9,11},{10,... | collective-permute-start | bytes 995336 | tf_op jit(solution)/shard_map/ppermute | solution.py:420
  29.8 1.5 %collective-permute-start.6 = (bf16[216,768]{1,0:T(8,128)(2,1)S(1)}, bf16[216,768]{1,0:T(8,128)(2,1)S(1)}, u32[]{:S(2)}, u32[]{:S(2)}) collective-permute-start(bf16[216,768]{1,0:T(8,128)(2,1)S(1)} %collective-permute-done.3.refs_2_), channel_id=1, source_target_pairs={{0,16},{16,0},{1,17},{17,1},{2,18},{18,2},{3,19},{19,3},{4,20},{20... | collective-permute-start | bytes 995336 | tf_op jit(solution)/shard_map/ppermute | solution.py:422
  31.3 3.8 %add_pieces.7.refs_4_ = f32[2,1024,200]{2,1,0:T(8,128)S(1)} custom-call(s32[70]{0:T(128)S(1)} %pad_add_fusion.scalars, bf16[20,20,64,400]{3,2,1,0:T(8,128)(2,1)S(1)} %edge_rows.1.copies, bf16[2,200,800]{2,1,0:T(8,128)(2,1)} %bitcast.3.own_ref.refs_0_.refs_2_, bf16[2,200,800]{2,1,0:T(8,128)(2,1)S(1)} %collective-permute-done.10.refs_1_.refs_3_, ...), custom_call_target="tpu_custom_call" | custom-call | flops 2621440000 | bytes 4194304 | tf_op jit(solution)/shard_map/add_pieces/pallas_call | solution.py:386
  35.1 3.0 %add_pieces.8.refs_8_ = f32[2,1024,200]{2,1,0:T(8,128)S(1)} custom-call(s32[70]{0:T(128)S(1)} %pad_add_fusion.scalars, bf16[20,20,64,400]{3,2,1,0:T(8,128)(2,1)S(1)} %edge_rows.1.copies, bf16[216,768]{1,0:T(8,128)(2,1)S(1)} %collective-permute-done.2.refs_0_, bf16[216,768]{1,0:T(8,128)(2,1)S(1)} %collective-permute-done.8.refs_1_, ...), custom_call_target="tpu_custom_call", output_to_operand_aliasing={{}: (6, {})} | custom-call | flops 2621440000 | bytes 4194304 | tf_op jit(solution)/shard_map/add_pieces/pallas_call | solution.py:386
  39.3 1.0 %collective-permute-start.11 = (bf16[216,768]{1,0:T(8,128)(2,1)S(1)}, bf16[216,768]{1,0:T(8,128)(2,1)S(1)}, u32[]{:S(2)}, u32[]{:S(2)}) collective-permute-start(bf16[216,768]{1,0:T(8,128)(2,1)S(1)} %collective-permute-done.4.refs_0_), channel_id=1, source_target_pairs={{0,4},{1,5},{2,6},{3,7},{4,8},{5,9},{6,10},{7,11},{8,12},{9,13},{1... | collective-permute-start | bytes 995336 | tf_op jit(solution)/shard_map/ppermute | solution.py:419
  40.3 1.0 %collective-permute-start.12 = (bf16[216,768]{1,0:T(8,128)(2,1)S(1)}, bf16[216,768]{1,0:T(8,128)(2,1)S(1)}, u32[]{:S(2)}, u32[]{:S(2)}) collective-permute-start(bf16[216,768]{1,0:T(8,128)(2,1)S(1)} %collective-permute-done.4.refs_0_), channel_id=1, source_target_pairs={{0,2},{1,3},{2,0},{3,1},{4,6},{5,7},{6,4},{7,5},{8,10},{9,11},{10,... | collective-permute-start | bytes 995336 | tf_op jit(solution)/shard_map/ppermute | solution.py:420
  41.3 1.5 %collective-permute-start.13 = (bf16[216,768]{1,0:T(8,128)(2,1)S(1)}, bf16[216,768]{1,0:T(8,128)(2,1)S(1)}, u32[]{:S(2)}, u32[]{:S(2)}) collective-permute-start(bf16[216,768]{1,0:T(8,128)(2,1)S(1)} %collective-permute-done.4.refs_0_), channel_id=1, source_target_pairs={{0,16},{16,0},{1,17},{17,1},{2,18},{18,2},{3,19},{19,3},{4,20},{20... | collective-permute-start | bytes 995336 | tf_op jit(solution)/shard_map/ppermute | solution.py:422
  42.8 5.3 %add_pieces.9.refs_6_ = f32[2,1024,200]{2,1,0:T(8,128)S(1)} custom-call(s32[70]{0:T(128)S(1)} %pad_add_fusion.scalars, bf16[20,20,64,400]{3,2,1,0:T(8,128)(2,1)S(1)} %edge_rows.1.copies, bf16[216,768]{1,0:T(8,128)(2,1)S(1)} %collective-permute-done.4.refs_0_, bf16[216,768]{1,0:T(8,128)(2,1)S(1)} %collective-permute-done.14.refs_1_, ...), custom_call_target="tpu_custom_call", output_to_operand_aliasing={{}: (10, {})} | custom-call | flops 5242880000 | bytes 8388608 | tf_op jit(solution)/shard_map/add_pieces/pallas_call | solution.py:386
  48.1 3.0 %collective-permute-done.11.refs_0_ = bf16[216,768]{1,0:T(8,128)(2,1)S(1)} collective-permute-done((bf16[216,768]{1,0:T(8,128)(2,1)S(1)}, bf16[216,768]{1,0:T(8,128)(2,1)S(1)}, u32[]{:S(2)}, u32[]{:S(2)}) %collective-permute-start.11) | collective-permute-done | bytes 331808 | tf_op jit(solution)/shard_map/ppermute | solution.py:419
  51.7 1.5 %collective-permute-start.21 = (bf16[216,768]{1,0:T(8,128)(2,1)S(1)}, bf16[216,768]{1,0:T(8,128)(2,1)S(1)}, u32[]{:S(2)}, u32[]{:S(2)}) collective-permute-start(bf16[216,768]{1,0:T(8,128)(2,1)S(1)} %collective-permute-done.5.refs_2_), channel_id=1, source_target_pairs={{0,16},{16,0},{1,17},{17,1},{2,18},{18,2},{3,19},{19,3},{4,20},{20... | collective-permute-start | bytes 995336 | tf_op jit(solution)/shard_map/ppermute | solution.py:422
  53.2 0.6 collective-permute-start.19
  53.8 1.7 %collective-permute-start.20 = (bf16[216,768]{1,0:T(8,128)(2,1)S(1)}, bf16[216,768]{1,0:T(8,128)(2,1)S(1)}, u32[]{:S(2)}, u32[]{:S(2)}) collective-permute-start(bf16[216,768]{1,0:T(8,128)(2,1)S(1)} %collective-permute-done.11.refs_0_), channel_id=1, source_target_pairs={{0,2},{1,3},{2,0},{3,1},{4,6},{5,7},{6,4},{7,5},{8,10},{9,11},{10,... | collective-permute-start | bytes 995336 | tf_op jit(solution)/shard_map/ppermute | solution.py:420
  55.5 4.1 %add_pieces.10.refs_6_ = f32[2,1024,200]{2,1,0:T(8,128)S(1)} custom-call(s32[70]{0:T(128)S(1)} %pad_add_fusion.scalars, bf16[20,20,64,400]{3,2,1,0:T(8,128)(2,1)S(1)} %edge_rows.1.copies, bf16[216,768]{1,0:T(8,128)(2,1)S(1)} %collective-permute-done.11.refs_0_, bf16[216,768]{1,0:T(8,128)(2,1)S(1)} %collective-permute-done.22.refs_1_, ...), custom_call_target="tpu_custom_call", output_to_operand_aliasing={{}: (8, {})} | custom-call | flops 3932160000 | bytes 6291456 | tf_op jit(solution)/shard_map/add_pieces/pallas_call | solution.py:386
  59.6 2.3 %collective-permute-done.21.refs_4_ = bf16[216,768]{1,0:T(8,128)(2,1)S(1)} collective-permute-done((bf16[216,768]{1,0:T(8,128)(2,1)S(1)}, bf16[216,768]{1,0:T(8,128)(2,1)S(1)}, u32[]{:S(2)}, u32[]{:S(2)}) %collective-permute-start.21) | collective-permute-done | bytes 331808 | tf_op jit(solution)/shard_map/ppermute | solution.py:422
  61.8 3.0 %collective-permute-done.19.refs_0_ = bf16[216,768]{1,0:T(8,128)(2,1)S(1)} collective-permute-done((bf16[216,768]{1,0:T(8,128)(2,1)S(1)}, bf16[216,768]{1,0:T(8,128)(2,1)S(1)}, u32[]{:S(2)}, u32[]{:S(2)}) %collective-permute-start.19) | collective-permute-done | bytes 331808 | tf_op jit(solution)/shard_map/ppermute | solution.py:419
  65.4 1.1 %collective-permute-start.18 = (bf16[216,768]{1,0:T(8,128)(2,1)S(1)}, bf16[216,768]{1,0:T(8,128)(2,1)S(1)}, u32[]{:S(2)}, u32[]{:S(2)}) collective-permute-start(bf16[216,768]{1,0:T(8,128)(2,1)S(1)} %collective-permute-done.13.refs_4_), channel_id=1, source_target_pairs={{0,2},{1,3},{2,0},{3,1},{4,6},{5,7},{6,4},{7,5},{8,10},{9,11},{10,... | collective-permute-start | bytes 995336 | tf_op jit(solution)/shard_map/ppermute | solution.py:420
  67.4 4.1 %add_pieces.11.refs_2_ = f32[2,1024,200]{2,1,0:T(8,128)S(1)} custom-call(s32[70]{0:T(128)S(1)} %pad_add_fusion.scalars, bf16[20,20,64,400]{3,2,1,0:T(8,128)(2,1)S(1)} %edge_rows.1.copies, bf16[216,768]{1,0:T(8,128)(2,1)S(1)} %collective-permute-done.19.refs_0_, bf16[216,768]{1,0:T(8,128)(2,1)S(1)} %collective-permute-done.26.refs_1_, ...), custom_call_target="tpu_custom_call", output_to_operand_aliasing={{}: (8, {})} | custom-call | flops 3932160000 | bytes 6291456 | tf_op jit(solution)/shard_map/add_pieces/pallas_call | solution.py:386
  71.6 4.0 %collective-permute-done.18.refs_0_ = bf16[216,768]{1,0:T(8,128)(2,1)S(1)} collective-permute-done((bf16[216,768]{1,0:T(8,128)(2,1)S(1)}, bf16[216,768]{1,0:T(8,128)(2,1)S(1)}, u32[]{:S(2)}, u32[]{:S(2)}) %collective-permute-start.18) | collective-permute-done | bytes 331808 | tf_op jit(solution)/shard_map/ppermute | solution.py:420
  75.6 0.9 %collective-permute-done.25.refs_1_ = bf16[216,768]{1,0:T(8,128)(2,1)S(1)} collective-permute-done((bf16[216,768]{1,0:T(8,128)(2,1)S(1)}, bf16[216,768]{1,0:T(8,128)(2,1)S(1)}, u32[]{:S(2)}, u32[]{:S(2)}) %collective-permute-start.25) | collective-permute-done | bytes 331808 | tf_op jit(solution)/shard_map/ppermute | solution.py:422
  76.9 2.0 %add_pieces.12.refs_4_ = f32[2,1024,200]{2,1,0:T(8,128)S(1)} custom-call(s32[70]{0:T(128)S(1)} %pad_add_fusion.scalars, bf16[20,20,64,400]{3,2,1,0:T(8,128)(2,1)S(1)} %edge_rows.1.copies, bf16[216,768]{1,0:T(8,128)(2,1)S(1)} %collective-permute-done.18.refs_0_, bf16[216,768]{1,0:T(8,128)(2,1)S(1)} %collective-permute-done.25.refs_1_, ...), custom_call_target="tpu_custom_call", output_to_operand_aliasing={{}: (4, {})} | custom-call | flops 1310720000 | bytes 2097152 | tf_op jit(solution)/shard_map/add_pieces/pallas_call | solution.py:386
  79.0 3.5 %add_pieces.13 = (f32[16,64,400]{2,1,0:T(8,128)}, f32[16,64,400]{2,1,0:T(8,128)}) custom-call(s32[70]{0:T(128)S(1)} %pad_add_fusion.scalars, bf16[20,20,64,400]{3,2,1,0:T(8,128)(2,1)S(1)} %edge_rows.1.copies, bf16[216,768]{1,0:T(8,128)(2,1)S(1)} %collective-permute-done.29.refs_0_, bf16[216,768]{1,0:T(8,128)(2,1)S(1)} %collective-permute-done.30.refs_1_, ...), custom_call_target="tpu_custom_call" | custom-call | flops 1310720000 | bytes 2097152 | tf_op jit(solution)/shard_map/add_pieces/pallas_call | solution.py:386
  (52 shorter events, 4.1 us)
Async XLA Ops:
  2.7 9.8 %copy-start.3 = (s32[4]{0:T(128)S(1)}, s32[4]{0:T(128)}, u32[]{:S(2)}) copy-start(s32[4]{0:T(128)} %param.9) | copy-start | bytes 52
  2.7 14.5 %collective-permute-start.2 = (bf16[216,768]{1,0:T(8,128)(2,1)}, bf16[216,768]{1,0:T(8,128)(2,1)S(1)}, u32[]{:S(2)}, u32[]{:S(2)}) collective-permute-start(bf16[216,768]{1,0:T(8,128)(2,1)} %get-tuple-element.30), channel_id=1, source_target_pairs={{0,4},{1,5},{2,6},{3,7},{4,8},{5,9},{6,10},{7,11},{8,12},{9,13},{1... | collective-permute-start | bytes 995336 | tf_op jit(solution)/shard_map/ppermute | solution.py:419
  5.7 11.5 %collective-permute-start.3 = (bf16[216,768]{1,0:T(8,128)(2,1)}, bf16[216,768]{1,0:T(8,128)(2,1)S(1)}, u32[]{:S(2)}, u32[]{:S(2)}) collective-permute-start(bf16[216,768]{1,0:T(8,128)(2,1)} %get-tuple-element.30), channel_id=1, source_target_pairs={{0,2},{1,3},{2,0},{3,1},{4,6},{5,7},{6,4},{7,5},{8,10},{9,11},{10,... | collective-permute-start | bytes 995336 | tf_op jit(solution)/shard_map/ppermute | solution.py:420
  7.2 17.4 %collective-permute-start.10 = (bf16[2,200,800]{2,1,0:T(8,128)(2,1)}, bf16[2,200,800]{2,1,0:T(8,128)(2,1)S(1)}, u32[]{:S(2)}, u32[]{:S(2)}) collective-permute-start(bf16[2,200,800]{2,1,0:T(8,128)(2,1)} %bitcast.3.own_ref.refs_0_.refs_2_), channel_id=1, source_target_pairs={{0,1},{1,0},{2,3},{3,2},{4,5},{5,4},{6,7},{7,6},{8,9},{9,8},{10,11... | collective-permute-start | bytes 1920008 | tf_op jit(solution)/shard_map/ppermute | solution.py:421
  8.5 9.9 %collective-permute-start = (bf16[544,384]{1,0:T(8,128)(2,1)S(1)}, bf16[544,384]{1,0:T(8,128)(2,1)S(1)}, u32[]{:S(2)}, u32[]{:S(2)}) collective-permute-start(bf16[544,384]{1,0:T(8,128)(2,1)S(1)} %get-tuple-element.28), channel_id=1, source_target_pairs={{0,1},{1,2},{2,3},{3,4},{4,5},{5,6},{6,7},{7,8},{8,9},{9,10},{10,1... | collective-permute-start | bytes 1253384 | tf_op jit(solution)/shard_map/ppermute | solution.py:24
  11.0 11.1 %collective-permute-start.1 = (bf16[544,384]{1,0:T(8,128)(2,1)S(1)}, bf16[544,384]{1,0:T(8,128)(2,1)S(1)}, u32[]{:S(2)}, u32[]{:S(2)}) collective-permute-start(bf16[544,384]{1,0:T(8,128)(2,1)S(1)} %get-tuple-element.29), channel_id=1, source_target_pairs={{1,0},{2,1},{3,2},{4,3},{5,4},{6,5},{7,6},{8,7},{9,8},{10,9},{11,1... | collective-permute-start | bytes 1253384 | tf_op jit(solution)/shard_map/ppermute | solution.py:24
  17.2 12.6 %collective-permute-start.8 = (bf16[216,768]{1,0:T(8,128)(2,1)S(1)}, bf16[216,768]{1,0:T(8,128)(2,1)S(1)}, u32[]{:S(2)}, u32[]{:S(2)}) collective-permute-start(bf16[216,768]{1,0:T(8,128)(2,1)S(1)} %collective-permute-done.2.refs_0_), channel_id=1, source_target_pairs={{0,1},{1,0},{2,3},{3,2},{4,5},{5,4},{6,7},{7,6},{8,9},{9,8},{10,11... | collective-permute-start | bytes 995336 | tf_op jit(solution)/shard_map/ppermute | solution.py:421
  18.4 16.7 %collective-permute-start.9 = (bf16[216,768]{1,0:T(8,128)(2,1)S(1)}, bf16[216,768]{1,0:T(8,128)(2,1)S(1)}, u32[]{:S(2)}, u32[]{:S(2)}) collective-permute-start(bf16[216,768]{1,0:T(8,128)(2,1)S(1)} %collective-permute-done.3.refs_2_), channel_id=1, source_target_pairs={{0,1},{1,0},{2,3},{3,2},{4,5},{5,4},{6,7},{7,6},{8,9},{9,8},{10,11... | collective-permute-start | bytes 995336 | tf_op jit(solution)/shard_map/ppermute | solution.py:421
  18.5 19.7 %collective-permute-start.7 = (bf16[216,768]{1,0:T(8,128)(2,1)S(1)}, bf16[216,768]{1,0:T(8,128)(2,1)S(1)}, u32[]{:S(2)}, u32[]{:S(2)}) collective-permute-start(bf16[216,768]{1,0:T(8,128)(2,1)S(1)} %get-tuple-element.35), channel_id=1, source_target_pairs={{0,4},{1,5},{2,6},{3,7},{4,8},{5,9},{6,10},{7,11},{8,12},{9,13},{1... | collective-permute-start | bytes 995336 | tf_op jit(solution)/shard_map/ppermute | solution.py:419
  22.1 16.1 %collective-permute-start.4 = (bf16[216,768]{1,0:T(8,128)(2,1)S(1)}, bf16[216,768]{1,0:T(8,128)(2,1)S(1)}, u32[]{:S(2)}, u32[]{:S(2)}) collective-permute-start(bf16[216,768]{1,0:T(8,128)(2,1)S(1)} %collective-permute-done.2.refs_0_), channel_id=1, source_target_pairs={{0,4},{1,5},{2,6},{3,7},{4,8},{5,9},{6,10},{7,11},{8,12},{9,13},{1... | collective-permute-start | bytes 995336 | tf_op jit(solution)/shard_map/ppermute | solution.py:419
  24.6 13.6 %collective-permute-start.5 = (bf16[216,768]{1,0:T(8,128)(2,1)S(1)}, bf16[216,768]{1,0:T(8,128)(2,1)S(1)}, u32[]{:S(2)}, u32[]{:S(2)}) collective-permute-start(bf16[216,768]{1,0:T(8,128)(2,1)S(1)} %collective-permute-done.2.refs_0_), channel_id=1, source_target_pairs={{0,2},{1,3},{2,0},{3,1},{4,6},{5,7},{6,4},{7,5},{8,10},{9,11},{10,... | collective-permute-start | bytes 995336 | tf_op jit(solution)/shard_map/ppermute | solution.py:420
  29.8 8.4 %collective-permute-start.6 = (bf16[216,768]{1,0:T(8,128)(2,1)S(1)}, bf16[216,768]{1,0:T(8,128)(2,1)S(1)}, u32[]{:S(2)}, u32[]{:S(2)}) collective-permute-start(bf16[216,768]{1,0:T(8,128)(2,1)S(1)} %collective-permute-done.3.refs_2_), channel_id=1, source_target_pairs={{0,16},{16,0},{1,17},{17,1},{2,18},{18,2},{3,19},{19,3},{4,20},{20... | collective-permute-start | bytes 995336 | tf_op jit(solution)/shard_map/ppermute | solution.py:422
  38.2 2.1 %collective-permute-start.14 = (bf16[216,768]{1,0:T(8,128)(2,1)S(1)}, bf16[216,768]{1,0:T(8,128)(2,1)S(1)}, u32[]{:S(2)}, u32[]{:S(2)}) collective-permute-start(bf16[216,768]{1,0:T(8,128)(2,1)S(1)} %collective-permute-done.4.refs_0_), channel_id=1, source_target_pairs={{0,1},{1,0},{2,3},{3,2},{4,5},{5,4},{6,7},{7,6},{8,9},{9,8},{10,11... | collective-permute-start | bytes 995336 | tf_op jit(solution)/shard_map/ppermute | solution.py:421
  38.6 2.7 %collective-permute-start.15 = (bf16[216,768]{1,0:T(8,128)(2,1)S(1)}, bf16[216,768]{1,0:T(8,128)(2,1)S(1)}, u32[]{:S(2)}, u32[]{:S(2)}) collective-permute-start(bf16[216,768]{1,0:T(8,128)(2,1)S(1)} %collective-permute-done.5.refs_2_), channel_id=1, source_target_pairs={{0,1},{1,0},{2,3},{3,2},{4,5},{5,4},{6,7},{7,6},{8,9},{9,8},{10,11... | collective-permute-start | bytes 995336 | tf_op jit(solution)/shard_map/ppermute | solution.py:421
  38.8 4.0 %collective-permute-start.16 = (bf16[216,768]{1,0:T(8,128)(2,1)S(1)}, bf16[216,768]{1,0:T(8,128)(2,1)S(1)}, u32[]{:S(2)}, u32[]{:S(2)}) collective-permute-start(bf16[216,768]{1,0:T(8,128)(2,1)S(1)} %collective-permute-done.6.refs_4_), channel_id=1, source_target_pairs={{0,1},{1,0},{2,3},{3,2},{4,5},{5,4},{6,7},{7,6},{8,9},{9,8},{10,11... | collective-permute-start | bytes 995336 | tf_op jit(solution)/shard_map/ppermute | solution.py:421
  39.1 3.7 %collective-permute-start.17 = (bf16[216,768]{1,0:T(8,128)(2,1)S(1)}, bf16[216,768]{1,0:T(8,128)(2,1)S(1)}, u32[]{:S(2)}, u32[]{:S(2)}) collective-permute-start(bf16[216,768]{1,0:T(8,128)(2,1)S(1)} %collective-permute-done.7.refs_6_), channel_id=1, source_target_pairs={{0,1},{1,0},{2,3},{3,2},{4,5},{5,4},{6,7},{7,6},{8,9},{9,8},{10,11... | collective-permute-start | bytes 995336 | tf_op jit(solution)/shard_map/ppermute | solution.py:421
  39.3 11.8 %collective-permute-start.11 = (bf16[216,768]{1,0:T(8,128)(2,1)S(1)}, bf16[216,768]{1,0:T(8,128)(2,1)S(1)}, u32[]{:S(2)}, u32[]{:S(2)}) collective-permute-start(bf16[216,768]{1,0:T(8,128)(2,1)S(1)} %collective-permute-done.4.refs_0_), channel_id=1, source_target_pairs={{0,4},{1,5},{2,6},{3,7},{4,8},{5,9},{6,10},{7,11},{8,12},{9,13},{1... | collective-permute-start | bytes 995336 | tf_op jit(solution)/shard_map/ppermute | solution.py:419
  40.3 10.8 %collective-permute-start.12 = (bf16[216,768]{1,0:T(8,128)(2,1)S(1)}, bf16[216,768]{1,0:T(8,128)(2,1)S(1)}, u32[]{:S(2)}, u32[]{:S(2)}) collective-permute-start(bf16[216,768]{1,0:T(8,128)(2,1)S(1)} %collective-permute-done.4.refs_0_), channel_id=1, source_target_pairs={{0,2},{1,3},{2,0},{3,1},{4,6},{5,7},{6,4},{7,5},{8,10},{9,11},{10,... | collective-permute-start | bytes 995336 | tf_op jit(solution)/shard_map/ppermute | solution.py:420
  41.3 9.8 %collective-permute-start.13 = (bf16[216,768]{1,0:T(8,128)(2,1)S(1)}, bf16[216,768]{1,0:T(8,128)(2,1)S(1)}, u32[]{:S(2)}, u32[]{:S(2)}) collective-permute-start(bf16[216,768]{1,0:T(8,128)(2,1)S(1)} %collective-permute-done.4.refs_0_), channel_id=1, source_target_pairs={{0,16},{16,0},{1,17},{17,1},{2,18},{18,2},{3,19},{19,3},{4,20},{20... | collective-permute-start | bytes 995336 | tf_op jit(solution)/shard_map/ppermute | solution.py:422
  51.1 2.7 %collective-permute-start.22 = (bf16[216,768]{1,0:T(8,128)(2,1)S(1)}, bf16[216,768]{1,0:T(8,128)(2,1)S(1)}, u32[]{:S(2)}, u32[]{:S(2)}) collective-permute-start(bf16[216,768]{1,0:T(8,128)(2,1)S(1)} %collective-permute-done.11.refs_0_), channel_id=1, source_target_pairs={{0,1},{1,0},{2,3},{3,2},{4,5},{5,4},{6,7},{7,6},{8,9},{9,8},{10,11... | collective-permute-start | bytes 995336 | tf_op jit(solution)/shard_map/ppermute | solution.py:421
  51.1 4.4 %collective-permute-start.23 = (bf16[216,768]{1,0:T(8,128)(2,1)S(1)}, bf16[216,768]{1,0:T(8,128)(2,1)S(1)}, u32[]{:S(2)}, u32[]{:S(2)}) collective-permute-start(bf16[216,768]{1,0:T(8,128)(2,1)S(1)} %collective-permute-done.12.refs_2_), channel_id=1, source_target_pairs={{0,1},{1,0},{2,3},{3,2},{4,5},{5,4},{6,7},{7,6},{8,9},{9,8},{10,11... | collective-permute-start | bytes 995336 | tf_op jit(solution)/shard_map/ppermute | solution.py:421
  51.6 3.9 %collective-permute-start.24 = (bf16[216,768]{1,0:T(8,128)(2,1)S(1)}, bf16[216,768]{1,0:T(8,128)(2,1)S(1)}, u32[]{:S(2)}, u32[]{:S(2)}) collective-permute-start(bf16[216,768]{1,0:T(8,128)(2,1)S(1)} %collective-permute-done.13.refs_4_), channel_id=1, source_target_pairs={{0,1},{1,0},{2,3},{3,2},{4,5},{5,4},{6,7},{7,6},{8,9},{9,8},{10,11... | collective-permute-start | bytes 995336 | tf_op jit(solution)/shard_map/ppermute | solution.py:421
  51.7 10.1 %collective-permute-start.21 = (bf16[216,768]{1,0:T(8,128)(2,1)S(1)}, bf16[216,768]{1,0:T(8,128)(2,1)S(1)}, u32[]{:S(2)}, u32[]{:S(2)}) collective-permute-start(bf16[216,768]{1,0:T(8,128)(2,1)S(1)} %collective-permute-done.5.refs_2_), channel_id=1, source_target_pairs={{0,16},{16,0},{1,17},{17,1},{2,18},{18,2},{3,19},{19,3},{4,20},{20... | collective-permute-start | bytes 995336 | tf_op jit(solution)/shard_map/ppermute | solution.py:422
  53.2 11.7 %collective-permute-start.19 = (bf16[216,768]{1,0:T(8,128)(2,1)S(1)}, bf16[216,768]{1,0:T(8,128)(2,1)S(1)}, u32[]{:S(2)}, u32[]{:S(2)}) collective-permute-start(bf16[216,768]{1,0:T(8,128)(2,1)S(1)} %collective-permute-done.13.refs_4_), channel_id=1, source_target_pairs={{0,4},{1,5},{2,6},{3,7},{4,8},{5,9},{6,10},{7,11},{8,12},{9,13},{1... | collective-permute-start | bytes 995336 | tf_op jit(solution)/shard_map/ppermute | solution.py:419
  53.8 11.1 %collective-permute-start.20 = (bf16[216,768]{1,0:T(8,128)(2,1)S(1)}, bf16[216,768]{1,0:T(8,128)(2,1)S(1)}, u32[]{:S(2)}, u32[]{:S(2)}) collective-permute-start(bf16[216,768]{1,0:T(8,128)(2,1)S(1)} %collective-permute-done.11.refs_0_), channel_id=1, source_target_pairs={{0,2},{1,3},{2,0},{3,1},{4,6},{5,7},{6,4},{7,5},{8,10},{9,11},{10,... | collective-permute-start | bytes 995336 | tf_op jit(solution)/shard_map/ppermute | solution.py:420
  64.9 2.2 %collective-permute-start.26 = (bf16[216,768]{1,0:T(8,128)(2,1)S(1)}, bf16[216,768]{1,0:T(8,128)(2,1)S(1)}, u32[]{:S(2)}, u32[]{:S(2)}) collective-permute-start(bf16[216,768]{1,0:T(8,128)(2,1)S(1)} %collective-permute-done.19.refs_0_), channel_id=1, source_target_pairs={{0,1},{1,0},{2,3},{3,2},{4,5},{5,4},{6,7},{7,6},{8,9},{9,8},{10,11... | collective-permute-start | bytes 995336 | tf_op jit(solution)/shard_map/ppermute | solution.py:421
  64.9 2.2 %collective-permute-start.27 = (bf16[216,768]{1,0:T(8,128)(2,1)S(1)}, bf16[216,768]{1,0:T(8,128)(2,1)S(1)}, u32[]{:S(2)}, u32[]{:S(2)}) collective-permute-start(bf16[216,768]{1,0:T(8,128)(2,1)S(1)} %collective-permute-done.20.refs_2_), channel_id=1, source_target_pairs={{0,1},{1,0},{2,3},{3,2},{4,5},{5,4},{6,7},{7,6},{8,9},{9,8},{10,11... | collective-permute-start | bytes 995336 | tf_op jit(solution)/shard_map/ppermute | solution.py:421
  65.4 2.1 %collective-permute-start.28 = (bf16[216,768]{1,0:T(8,128)(2,1)S(1)}, bf16[216,768]{1,0:T(8,128)(2,1)S(1)}, u32[]{:S(2)}, u32[]{:S(2)}) collective-permute-start(bf16[216,768]{1,0:T(8,128)(2,1)S(1)} %collective-permute-done.21.refs_4_), channel_id=1, source_target_pairs={{0,1},{1,0},{2,3},{3,2},{4,5},{5,4},{6,7},{7,6},{8,9},{9,8},{10,11... | collective-permute-start | bytes 995336 | tf_op jit(solution)/shard_map/ppermute | solution.py:421
  65.4 10.2 %collective-permute-start.18 = (bf16[216,768]{1,0:T(8,128)(2,1)S(1)}, bf16[216,768]{1,0:T(8,128)(2,1)S(1)}, u32[]{:S(2)}, u32[]{:S(2)}) collective-permute-start(bf16[216,768]{1,0:T(8,128)(2,1)S(1)} %collective-permute-done.13.refs_4_), channel_id=1, source_target_pairs={{0,2},{1,3},{2,0},{3,1},{4,6},{5,7},{6,4},{7,5},{8,10},{9,11},{10,... | collective-permute-start | bytes 995336 | tf_op jit(solution)/shard_map/ppermute | solution.py:420
  66.5 9.9 %collective-permute-start.25 = (bf16[216,768]{1,0:T(8,128)(2,1)S(1)}, bf16[216,768]{1,0:T(8,128)(2,1)S(1)}, u32[]{:S(2)}, u32[]{:S(2)}) collective-permute-start(bf16[216,768]{1,0:T(8,128)(2,1)S(1)} %collective-permute-done.20.refs_2_), channel_id=1, source_target_pairs={{0,16},{16,0},{1,17},{17,1},{2,18},{18,2},{3,19},{19,3},{4,20},{20... | collective-permute-start | bytes 995336 | tf_op jit(solution)/shard_map/ppermute | solution.py:422
  76.4 2.5 %collective-permute-start.29 = (bf16[216,768]{1,0:T(8,128)(2,1)S(1)}, bf16[216,768]{1,0:T(8,128)(2,1)S(1)}, u32[]{:S(2)}, u32[]{:S(2)}) collective-permute-start(bf16[216,768]{1,0:T(8,128)(2,1)S(1)} %collective-permute-done.18.refs_0_), channel_id=1, source_target_pairs={{0,1},{1,0},{2,3},{3,2},{4,5},{5,4},{6,7},{7,6},{8,9},{9,8},{10,11... | collective-permute-start | bytes 995336 | tf_op jit(solution)/shard_map/ppermute | solution.py:421
  76.4 2.5 %collective-permute-start.30 = (bf16[216,768]{1,0:T(8,128)(2,1)S(1)}, bf16[216,768]{1,0:T(8,128)(2,1)S(1)}, u32[]{:S(2)}, u32[]{:S(2)}) collective-permute-start(bf16[216,768]{1,0:T(8,128)(2,1)S(1)} %collective-permute-done.25.refs_1_), channel_id=1, source_target_pairs={{0,1},{1,0},{2,3},{3,2},{4,5},{5,4},{6,7},{7,6},{8,9},{9,8},{10,11... | collective-permute-start | bytes 995336 | tf_op jit(solution)/shard_map/ppermute | solution.py:421
  (3 other events, 24.3 us)
